TPU v7x, 256 devices: a whole 4x4x8 slice. The times are simulated.
256 devices in a mesh: exp: 32 (over y, z_hi, core), hid: 8 (over z_lo, x).
Axes of the slice: x: 4, y: 4, z: 8 (z_hi: 4, z_lo: 2; z = z_hi * 2 + z_lo), core: 2. Of those that a mesh axis runs over, the one named last changes fastest.
Arguments:
- tokens: bfloat16 [1024, 2048], P(('exp', 'hid')), may hold values from -6 to 6
- grad_out: bfloat16 [1024, 2048], P(('exp', 'hid')), may hold values from -3 to 3
- router_logits: float32 [1024, 128], P(('exp', 'hid')), may hold values from -12 to 330
- selected: int32 [1024, 8], P(('exp', 'hid')), may hold values from 0 to 127, as said below
- router_w: bfloat16 [2048, 128], replicated, may hold values from -0.59765625 to 0.59765625
- w_gate: bfloat16 [256, 2048, 384], P(('exp', 'hid')), may hold values from -0.125 to 0.125
- w_up: bfloat16 [256, 2048, 384], P(('exp', 'hid')), may hold values from -0.125 to 0.125
- w_down: bfloat16 [256, 384, 2048], P(('exp', 'hid')), may hold values from -0.21875 to 0.21875
Outputs:
- x_grad: bfloat16 [1024, 2048], P(('exp', 'hid'))
- router_grad: float32 [2048, 128], P(('exp', 'hid'))
Inputs may be any that keep to these rules, and one draw needn't show every extreme that they name: `selected`: each row names 8 different experts; within each aligned block of 32 rows (the tokens of one index of exp) no expert is named by more than 4 rows, and in every block some expert is named by exactly 4 rows.
All inputs are finite; a program needn't handle non-finite values.
Results may differ from a plain program's by a relative error of at most 0.0075.
Values may be sent and summed in bfloat16 or wider, within the bound.
A program may use at most 64 MiB of HBM per device.

v0:
```python
import jax
import jax.numpy as jnp
from jax import lax
from jax.sharding import PartitionSpec as P


def softmax_rows(values):
    top_val = jnp.max(values, axis=-1, keepdims=True)
    raised = jnp.exp(values - top_val)
    return raised / jnp.sum(raised, axis=-1, keepdims=True)


def combine_table(logits, chosen, expert_count):
    picked = jnp.take_along_axis(logits, chosen, axis=1)
    weights = softmax_rows(picked)
    expert_ids = jnp.arange(expert_count, dtype=jnp.int32)
    matched = (chosen[:, :, None] == expert_ids[None, None, :]).astype(jnp.float32)
    return jnp.sum(weights[:, :, None] * matched, axis=1).astype(jnp.bfloat16)


def unit_terms(x_rows, g_rows, c_rows, w_gate, w_up, w_down, unit_pick):
    gate_pre = jnp.einsum("td,udf->utf", x_rows, w_gate, preferred_element_type=jnp.float32)
    up_pre = jnp.einsum("td,udf->utf", x_rows, w_up, preferred_element_type=jnp.float32)
    back_grad = jnp.einsum("td,ufd->utf", g_rows, w_down, preferred_element_type=jnp.float32)
    sig_gate = jax.nn.sigmoid(gate_pre)
    act_gate = gate_pre * sig_gate
    score_part = jnp.sum(act_gate * up_pre * back_grad, axis=2).T
    column_rows = jnp.dot(c_rows, unit_pick, preferred_element_type=jnp.float32)
    weighted = column_rows.T[:, :, None] * back_grad
    grad_gate = (weighted * up_pre * sig_gate * (1.0 + gate_pre * (1.0 - sig_gate))).astype(
        jnp.bfloat16
    )
    grad_up = (weighted * act_gate).astype(jnp.bfloat16)
    input_part = jnp.einsum("utf,udf->td", grad_gate, w_gate, preferred_element_type=jnp.float32)
    input_part = input_part + jnp.einsum(
        "utf,udf->td", grad_up, w_up, preferred_element_type=jnp.float32
    )
    return (score_part, input_part, column_rows)


def on_device(tokens, grad_out, router_logits, selected, router_w, w_gate, w_up, w_down):
    tok_local, model_width = tokens.shape
    unit_count = w_gate.shape[0]
    expert_count = router_logits.shape[1]
    spread_exp = lax.axis_size("exp")
    spread_hid = lax.axis_size("hid")
    own_block = lax.axis_index(("exp", "hid"))
    unit_expert = (own_block * unit_count + jnp.arange(unit_count, dtype=jnp.int32)) // 2
    expert_ids = jnp.arange(expert_count, dtype=jnp.int32)
    unit_pick = (expert_ids[:, None] == unit_expert[None, :]).astype(jnp.bfloat16)
    combine = combine_table(router_logits, selected, expert_count)
    score_part, input_part, column_rows = unit_terms(
        lax.all_gather(tokens, ("exp", "hid"), axis=0, tiled=True),
        lax.all_gather(grad_out, ("exp", "hid"), axis=0, tiled=True),
        lax.all_gather(combine, ("exp", "hid"), axis=0, tiled=True),
        w_gate,
        w_up,
        w_down,
        unit_pick,
    )
    input_all = input_part
    used_all = column_rows
    scores, input_all, used_all = (score_part, input_all, used_all)
    input_sum = lax.psum_scatter(input_all, ("exp", "hid"), scatter_dimension=0, tiled=True)
    shaped = scores.reshape(spread_exp, spread_hid, tok_local, 1, unit_count)
    arrived = lax.all_to_all(
        lax.all_to_all(shaped, "exp", split_axis=0, concat_axis=3, tiled=True),
        "hid",
        split_axis=1,
        concat_axis=4,
        tiled=True,
    )
    expert_scores = jnp.sum(arrived.reshape(tok_local, expert_count, 2), axis=2)
    probs_all = softmax_rows(router_logits)
    mean_score = jnp.sum(probs_all * expert_scores, axis=1, keepdims=True)
    logit_grad = (probs_all * (expert_scores - mean_score)).astype(jnp.bfloat16)
    router_grad = lax.psum_scatter(
        jnp.einsum("tc,te->ce", tokens, logit_grad, preferred_element_type=jnp.float32),
        ("exp", "hid"),
        scatter_dimension=0,
        tiled=True,
    )
    router_part = jnp.einsum("te,de->td", logit_grad, router_w, preferred_element_type=jnp.float32)
    x_grad = (input_sum + router_part).astype(jnp.bfloat16)
    return (x_grad, router_grad)


def solution(mesh):
    placed = (
        P(("exp", "hid"), None),
        P(("exp", "hid"), None),
        P(("exp", "hid"), None),
        P(("exp", "hid"), None),
        P(),
        P(("exp", "hid"), None, None),
        P(("exp", "hid"), None, None),
        P(("exp", "hid"), None, None),
    )
    return jax.shard_map(
        on_device,
        mesh=mesh,
        in_specs=placed,
        out_specs=(P(("exp", "hid"), None), P(("exp", "hid"), None)),
        check_vma=False,
    )
```

profile of v0, /device:TPU:1, one launch (start us, length us, event | category | flops | bytes accessed | tf_op | source)
XLA Modules:
  0.0 1771.4 jit_solution(1746545466882803414)
XLA Ops:
  7.2 0.0 all-gather.8.cloned.1.call-start
  7.2 0.7 all-gather.8.cloned.1.call-update
  7.9 0.0 all-gather.6.cloned.1.call-start
  8.0 0.7 all-gather.6.cloned.1.call-update
  8.7 0.7 bitcast_or_fusion
  9.4 0.1 reshape.86
  9.5 1.4 gather_fusion
  10.9 0.1 reshape.89
  11.0 0.1 reduce_max.19
  11.1 0.2 fusion.30
  11.3 0.1 fusion.35
  11.4 0.2 fusion.28
  11.6 0.1 fusion.27
  11.7 0.1 select_reduce_fusion
  11.8 614.3 %all-gather = bf16[256,4,128]{2,1,0:T(4,128)(2,1)S(1)} all-gather(bf16[1,4,128]{2,1,0:T(4,128)(2,1)S(1)} %bitcast.132), channel_id=1, replica_groups=mesh['exp'=32,'hid'=8] {'exp','hid'}, dimensions={0}, use_global_device_ids=true | all-gather | bytes 263168 | tf_op jit(solution)/shard_map/all_gather | solution.py:55
  626.1 0.2 fusion.24
  626.3 97.9 %all-gather.8.cloned.1.call-done = bf16[256,4,2048]{2,1,0:T(4,128)(2,1)} async-done(((bf16[1,4,2048]{2,1,0:T(4,128)(2,1)}), bf16[256,4,2048]{2,1,0:T(4,128)(2,1)}) %all-gather.8.cloned.1.call-update) | async-done | bytes 4194320 | tf_op jit(solution)/shard_map/all_gather | solution.py:53
  724.2 6.9 reshape.102
  731.1 4.2 fusion.11
  735.3 3.0 fusion.14
  738.3 693.5 %all-gather.6.cloned.1.call-done = bf16[256,4,2048]{2,1,0:T(4,128)(2,1)} async-done(((bf16[1,4,2048]{2,1,0:T(4,128)(2,1)}), bf16[256,4,2048]{2,1,0:T(4,128)(2,1)}) %all-gather.6.cloned.1.call-update) | async-done | bytes 4194320 | tf_op jit(solution)/shard_map/all_gather | solution.py:54
  1431.9 6.9 reshape.100
  1438.8 6.2 fusion.1
  1445.0 0.1 reshape_transpose.3
  1445.1 0.9 copy.38
  1446.0 9.6 all-to-all-start
  1455.6 7.9 fusion.9
  1463.5 1.9 all-to-all-done
  1465.4 0.1 copy.39
  1465.5 0.5 broadcast.72
  1466.0 0.7 reduce.1
  1466.7 0.7 reshape.107
  1467.4 3.3 all-to-all-start.1
  1470.7 0.2 all-reduce.5.cloned.1.call-start
  1471.0 10.0 convolution_add_fusion
  1481.0 0.7 reduce.2
  1481.7 0.1 reshape.108
  1481.8 0.1 copy.41
  1481.9 0.2 reduce_sum.58
  1482.1 0.1 copy.43
  1482.1 0.2 multiply_reduce_fusion
  1482.3 0.1 multiply_convert_fusion.1
  1482.4 1.4 convolution_bitcast_fusion
  1483.8 0.0 all-reduce.5.cloned.1.call-update
  1483.8 277.8 %all-reduce.5.cloned.1.call-done = (f32[1024,2048]{1,0:T(8,128)}, f32[2048,128]{0,1:T(8,128)}) async-done(((f32[1024,2048]{1,0:T(8,128)}, f32[2048,128]{0,1:T(8,128)}), (f32[1024,2048]{1,0:T(8,128)}, f32[2048,128]{0,1:T(8,128)})) %all-reduce.5.cloned.1.call-update) | async-done | bytes 9437200
  1761.6 0.9 constant_dynamic-slice_fusion
  1762.5 0.7 copy.44
  1763.2 1.7 fusion
  (16 shorter events, 0.1 us)
Async XLA Ops:
  7.2 724.0 %copy-start = (bf16[1,2048,384]{2,1,0:T(8,128)(2,1)S(1)}, bf16[1,2048,384]{2,1,0:T(8,128)(2,1)}, u32[]{:S(2)}) copy-start(bf16[1,2048,384]{2,1,0:T(8,128)(2,1)} %param.13) | copy-start | bytes 4718596
  7.2 4.1 copy-start.6
  7.2 3.8 copy-start.1
  7.2 717.0 %all-gather.8.cloned.1.call-start = ((), (), s32[]{:S(2)}) async-start(), calls=%async_computation.3 | async-start | bytes 4210688 | tf_op jit(solution)/shard_map/all_gather | solution.py:53
  7.9 1423.9 %all-gather.6.cloned.1.call-start = ((), (), s32[]{:S(2)}) async-start(), calls=%async_computation.2 | async-start | bytes 4210688 | tf_op jit(solution)/shard_map/all_gather | solution.py:54
  731.1 4.2 copy-start.2
  731.1 4.2 copy-start.3
  1446.0 19.4 %all-to-all-start = ((f32[32,8,4,1,1]{1,2,4,3,0:T(4,128)}), f32[32,8,4,1,1]{1,2,4,3,0:T(4,128)S(1)}, u32[]{:S(2)}, u32[]{:S(2)}) async-start(f32[32,8,4,1,1]{1,2,4,3,0:T(4,128)} %copy.38), calls=%async_computation | async-start | bytes 131072 | tf_op jit(solution)/shard_map/all_to_all | solution.py:67
  1467.4 13.6 all-to-all-start.1
  1470.7 11.7 copy-start.5
  1470.7 290.9 %all-reduce.5.cloned.1.call-start = ((), (), s32[]{:S(2)}) async-start(), calls=%async_computation.4 | async-start | bytes 18874368
  1483.8 279.4 %copy-start.4 = (bf16[2048,128]{1,0:T(8,128)(2,1)S(1)}, bf16[2048,128]{1,0:T(8,128)(2,1)}, u32[]{:S(2)}) copy-start(bf16[2048,128]{1,0:T(8,128)(2,1)} %param.12) | copy-start | bytes 1572868
Sparse Core Ops, SparseCore 0:
  9.9 714.2 all-gather.7
  726.1 705.7 all-gather.5
  1484.0 277.5 all-reduce.4
where the time goes:
time: 1770 us
  waiting for transfers between devices  1070 us (60%)
  blocking collectives  614 us (35%)
  matrix products  34.6 us (2%)
  local copies, waits for them, and re-layouts  19.6 us (1%)
    all_gather x1, waiting for transfers between devices, on_device(): lax.all_gather(grad_out, ('exp', 'hid'), axis=0, tiled=True)  694 us
    all_gather x1, blocking collectives, on_device(): lax.all_gather(combine, ('exp', 'hid'), axis=0, tiled=True)  614 us
    unnamed x4, waiting for transfers between devices  279 us
    all_gather x1, waiting for transfers between devices, on_device(): lax.all_gather(tokens, ('exp', 'hid'), axis=0, tiled=True)  97.9 us
  transfers between devices with their start and end apart: 5, of which 4 were waited for; matrix products, arithmetic and copies ran while one was open for 2% of the time, Pallas kernels for 0%

commit v1 on v0

--- a/solution.py
+++ b/solution.py
@@ -49,20 +49,24 @@
     expert_ids = jnp.arange(expert_count, dtype=jnp.int32)
     unit_pick = (expert_ids[:, None] == unit_expert[None, :]).astype(jnp.bfloat16)
     combine = combine_table(router_logits, selected, expert_count)
+    packed = jnp.concatenate([tokens, grad_out, combine], axis=1)
+    gathered = lax.all_gather(lax.all_gather(packed, "hid", axis=0, tiled=True), "exp", axis=0, tiled=True)
     score_part, input_part, column_rows = unit_terms(
-        lax.all_gather(tokens, ("exp", "hid"), axis=0, tiled=True),
-        lax.all_gather(grad_out, ("exp", "hid"), axis=0, tiled=True),
-        lax.all_gather(combine, ("exp", "hid"), axis=0, tiled=True),
+        gathered[:, :model_width],
+        gathered[:, model_width : 2 * model_width],
+        gathered[:, 2 * model_width :],
         w_gate,
         w_up,
         w_down,
         unit_pick,
     )
-    input_all = input_part
-    used_all = column_rows
-    scores, input_all, used_all = (score_part, input_all, used_all)
-    input_sum = lax.psum_scatter(input_all, ("exp", "hid"), scatter_dimension=0, tiled=True)
-    shaped = scores.reshape(spread_exp, spread_hid, tok_local, 1, unit_count)
+    input_sum = lax.psum_scatter(
+        lax.psum_scatter(input_part, "exp", scatter_dimension=0, tiled=True),
+        "hid",
+        scatter_dimension=0,
+        tiled=True,
+    )
+    shaped = score_part.reshape(spread_exp, spread_hid, tok_local, 1, unit_count)
     arrived = lax.all_to_all(
         lax.all_to_all(shaped, "exp", split_axis=0, concat_axis=3, tiled=True),
         "hid",

time: 1770 us -> 609 us (0.34)
  blocking collectives: 614 us -> 24.1 us
  waiting for transfers between devices: 1070 us -> 519 us
    all_gather x2 -> x1, waiting for transfers between devices: 791 us -> 84.9 us  [on_device(): lax.all_gather(lax.all_gather(packed, 'hid', axis=0, tiled=True), 'exp',...]
    all_gather x1, blocking collectives: 614 us -> 24.1 us  [on_device(): lax.all_gather(packed, 'hid', axis=0, tiled=True)]
    reduce_scatter x0 -> x1, waiting for transfers between devices: none -> 86.9 us  [on_device(): lax.psum_scatter(input_part, 'exp', scatter_dimension=0, tiled=True)]
    unnamed x4 -> x6, waiting for transfers between devices: 279 us -> 333 us
  transfers between devices with their start and end apart: 5 -> 6, of which waited for: 4 -> 6; matrix products, arithmetic and copies ran while one was open for 2% -> 1% of each run, Pallas kernels for 0% -> 0%
where the time goes in v1:
time: 609 us; the launch traced here: 605 us
  waiting for transfers between devices  519 us (85%)
  blocking collectives  24.1 us (4%)
  matrix products  20.6 us (3%)
  starting transfers between devices  14.8 us (2%)
  between operations  14.6 us (2%)
  local copies, waits for them, and re-layouts  8.22 us (1%)
    unnamed x6, waiting for transfers between devices  333 us
    reduce_scatter x1, waiting for transfers between devices, on_device(): lax.psum_scatter(input_part, 'exp', scatter_dimension=0, tiled=True)  86.9 us
    all_gather x1, waiting for transfers between devices, on_device(): lax.all_gather(lax.all_gather(packed, 'hid', axis=0, tiled=True), 'exp',...  84.9 us
    all_gather x1, blocking collectives, on_device(): lax.all_gather(packed, 'hid', axis=0, tiled=True)  24.1 us
  transfers between devices with their start and end apart: 6, of which 6 were waited for; matrix products, arithmetic and copies ran while one was open for 1% of the time, Pallas kernels for 0%

profile of v1, /device:TPU:1, one launch (start us, length us, event | category | flops | bytes accessed | tf_op | source)
XLA Modules:
  0.0 605.1 jit_solution(16148703388574682319)
XLA Ops:
  7.2 0.0 all-gather.3.cloned.1.call-start
  7.3 0.8 bitcast_or_fusion
  8.0 0.1 reshape.86
  8.1 1.4 gather_fusion
  9.6 0.1 reshape.89
  9.7 0.1 fusion.40
  9.8 0.2 fusion.32
  10.0 0.1 fusion.31
  10.0 0.1 select_reduce_fusion
  10.2 24.1 %all-gather = bf16[8,4,4224]{2,1,0:T(4,128)(2,1)S(1)} all-gather(bf16[1,4,4224]{2,1,0:T(4,128)(2,1)S(1)} %maximum_bitcast_fusion), channel_id=1, replica_groups=mesh['exp'=32,'hid'=8] {'hid'}, dimensions={0}, use_global_device_ids=true | all-gather | bytes 304128 | tf_op jit(solution)/shard_map/all_gather | solution.py:53
  34.3 0.8 reshape.98
  35.1 0.0 reduce-scatter.3.cloned.1.call-start
  35.2 84.9 %all-gather.3.cloned.1.call-done = bf16[1024,4224]{1,0:T(8,128)(2,1)} async-done(((bf16[32,4224]{1,0:T(8,128)(2,1)}), bf16[1024,4224]{1,0:T(8,128)(2,1)}) %all-gather.3.cloned.1.call-update) | async-done | bytes 8650768 | tf_op jit(solution)/shard_map/all_gather | solution.py:53
  120.1 1.1 fusion.27
  121.2 4.2 fusion.2
  125.4 1.0 copy-done.7
  126.5 1.9 fusion.4
  128.3 2.0 fusion.7
  130.4 2.7 fusion.15
  133.1 5.7 convolution_add_fusion
  138.8 0.1 reshape_transpose.3
  138.9 0.9 copy.38
  139.8 10.4 %all-to-all-start = ((f32[32,8,4,1,1]{1,2,4,3,0:T(4,128)}), f32[32,8,4,1,1]{1,2,4,3,0:T(4,128)S(1)}, u32[]{:S(2)}, u32[]{:S(2)}) async-start(f32[32,8,4,1,1]{1,2,4,3,0:T(4,128)} %copy.38), calls=%async_computation.1 | async-start | bytes 131072 | tf_op jit(solution)/shard_map/all_to_all | solution.py:71
  150.2 0.1 reduce_max.19
  150.3 9.6 %all-to-all-done = f32[32,8,4,1,1]{1,2,4,3,0:T(4,128)S(1)} async-done(((f32[32,8,4,1,1]{1,2,4,3,0:T(4,128)}), f32[32,8,4,1,1]{1,2,4,3,0:T(4,128)S(1)}, u32[]{:S(2)}, u32[]{:S(2)}) %all-to-all-start) | async-done | bytes 4128 | tf_op jit(solution)/shard_map/all_to_all | solution.py:71
  160.0 0.1 copy.39
  160.1 0.5 broadcast.72
  160.6 0.8 reduce.1
  161.3 0.7 reshape.104
  162.0 4.3 all-to-all-start.1
  166.4 0.2 fusion.34
  166.6 4.7 all-to-all-done.1
  171.3 0.7 reduce.2
  171.9 0.1 reshape.105
  172.0 0.1 copy.41
  172.2 0.2 reduce_sum.58
  172.3 0.1 copy.43
  172.4 0.2 multiply_reduce_fusion
  172.6 0.1 multiply_convert_fusion.1
  172.7 1.3 convolution_bitcast_fusion
  174.0 0.0 all-reduce.5.cloned.1.call-start
  174.1 86.9 %reduce-scatter.3.cloned.1.call-done = f32[32,2048]{1,0:T(8,128)} async-done(((f32[1024,2048]{1,0:T(8,128)}), f32[32,2048]{1,0:T(8,128)}) %reduce-scatter.3.cloned.1.call-update) | async-done | bytes 262160 | tf_op jit(solution)/shard_map/reduce_scatter | solution.py:64
  261.1 0.6 dynamic-slice
  262.3 257.7 %all-reduce.7.cloned.1.call-done = f32[2048,128]{0,1:T(8,128)} async-done(((f32[2048,128]{0,1:T(8,128)}), f32[2048,128]{0,1:T(8,128)}) %all-reduce.7.cloned.1.call-update) | async-done | bytes 1048592
  520.1 0.9 constant_dynamic-slice_fusion
  521.0 0.7 copy.44
  521.6 75.2 %all-reduce.5.cloned.1.call-done = f32[32,2048]{1,0:T(8,128)} async-done(((f32[32,2048]{1,0:T(8,128)}), f32[32,2048]{1,0:T(8,128)}) %all-reduce.5.cloned.1.call-update) | async-done | bytes 262160
  596.9 1.7 fusion.6
  (26 shorter events, 0.2 us)
Async XLA Ops:
  7.2 114.1 %copy-start = (bf16[1,2048,384]{2,1,0:T(8,128)(2,1)S(1)}, bf16[1,2048,384]{2,1,0:T(8,128)(2,1)}, u32[]{:S(2)}) copy-start(bf16[1,2048,384]{2,1,0:T(8,128)(2,1)} %param.13) | copy-start | bytes 4718596
  7.2 2.5 copy-start.5
  7.2 3.0 copy-start.4
  7.2 3.0 copy-start.6
  7.2 112.9 %all-gather.3.cloned.1.call-start = ((), (), s32[]{:S(2)}) async-start(), calls=%async_computation.3 | async-start | bytes 8921088 | tf_op jit(solution)/shard_map/all_gather | solution.py:53
  35.1 225.9 %reduce-scatter.3.cloned.1.call-start = ((), (), s32[]{:S(2)}) async-start(), calls=%async_computation.4 | async-start | bytes 8650752 | tf_op jit(solution)/shard_map/reduce_scatter | solution.py:64
  121.2 4.2 copy-start.2
  121.2 5.2 copy-start.7
  126.5 1.9 copy-start.8
  138.8 11.4 %copy-start.1 = (f32[4,128]{1,0:T(4,128)S(1)}, f32[4,128]{1,0:T(4,128)}, u32[]{:S(2)}) copy-start(f32[4,128]{1,0:T(4,128)} %param.10) | copy-start | bytes 6148
  139.8 121.2 %copy-start.9 = (u32[256]{0:T(256)S(1)}, u32[256]{0:T(256)}, u32[]{:S(2)}) copy-start(u32[256]{0:T(256)} %constant.76) | copy-start | bytes 3076
  139.8 20.1 %all-to-all-start = ((f32[32,8,4,1,1]{1,2,4,3,0:T(4,128)}), f32[32,8,4,1,1]{1,2,4,3,0:T(4,128)S(1)}, u32[]{:S(2)}, u32[]{:S(2)}) async-start(f32[32,8,4,1,1]{1,2,4,3,0:T(4,128)} %copy.38), calls=%async_computation.1 | async-start | bytes 131072 | tf_op jit(solution)/shard_map/all_to_all | solution.py:71
  160.6 436.3 %copy-start.3 = (bf16[2048,128]{1,0:T(8,128)(2,1)S(1)}, bf16[2048,128]{1,0:T(8,128)(2,1)}, u32[]{:S(2)}) copy-start(bf16[2048,128]{1,0:T(8,128)(2,1)} %param.12) | copy-start | bytes 1572868
  162.0 9.2 %all-to-all-start.1 = ((f32[8,1,128]{2,1,0:T(1,128)}), f32[8,1,128]{2,1,0:T(1,128)S(1)}, u32[]{:S(2)}, u32[]{:S(2)}) async-start(f32[8,1,128]{2,1,0:T(1,128)} %reshape.104), calls=%async_computation.2 | async-start | bytes 8192 | tf_op jit(solution)/shard_map/all_to_all | solution.py:70
  166.3 353.7 %all-reduce.7.cloned.1.call-start = ((), (), s32[]{:S(2)}) async-start(), calls=%async_computation.6 | async-start | bytes 2097152
  174.0 422.8 %all-reduce.5.cloned.1.call-start = ((), (), s32[]{:S(2)}) async-start(), calls=%async_computation.5 | async-start | bytes 524288
Sparse Core Ops, SparseCore 0:
  35.2 84.8 all-gather.2
  138.9 122.0 reduce-scatter.2
  267.4 252.6 all-reduce.6
  522.5 74.2 all-reduce.4

commit v2 on v1

--- a/solution.py
+++ b/solution.py
@@ -78,12 +78,12 @@
     probs_all = softmax_rows(router_logits)
     mean_score = jnp.sum(probs_all * expert_scores, axis=1, keepdims=True)
     logit_grad = (probs_all * (expert_scores - mean_score)).astype(jnp.bfloat16)
-    router_grad = lax.psum_scatter(
-        jnp.einsum("tc,te->ce", tokens, logit_grad, preferred_element_type=jnp.float32),
-        ("exp", "hid"),
-        scatter_dimension=0,
-        tiled=True,
+    logit_all = lax.all_gather(
+        lax.all_gather(logit_grad, "hid", axis=0, tiled=True), "exp", axis=0, tiled=True
     )
+    grad_rows = model_width // (spread_exp * spread_hid)
+    token_cols = lax.dynamic_slice_in_dim(gathered, own_block * grad_rows, grad_rows, 1)
+    router_grad = jnp.einsum("tc,te->ce", token_cols, logit_all, preferred_element_type=jnp.float32)
     router_part = jnp.einsum("te,de->td", logit_grad, router_w, preferred_element_type=jnp.float32)
     x_grad = (input_sum + router_part).astype(jnp.bfloat16)
     return (x_grad, router_grad)

time: 609 us -> 349 us (0.57)
  waiting for transfers between devices: 519 us -> 203 us
  blocking collectives: 24.1 us -> 80.9 us
    unnamed x6 -> x4, waiting for transfers between devices: 333 us -> 28.9 us
    all_gather x0 -> x2, blocking collectives: none -> 56.8 us  [the longest x1 44.3 us: on_device(): lax.all_gather(lax.all_gather(logit_grad, 'hid', axis=0, tiled=True), 'ex...]
    reduce_scatter x1, waiting for transfers between devices: 86.9 us -> 76.1 us  [on_device(): lax.psum_scatter(input_part, 'exp', scatter_dimension=0, tiled=True)]
  transfers between devices with their start and end apart: 6 -> 5, of which waited for: 6 -> 5; matrix products, arithmetic and copies ran while one was open for 1% -> 2% of each run, Pallas kernels for 0% -> 0%
where the time goes in v2:
time: 349 us; the launch traced here: 344 us
  waiting for transfers between devices  203 us (58%)
  blocking collectives  80.9 us (23%)
  matrix products  21.2 us (6%)
  starting transfers between devices  14.7 us (4%)
  between operations  14.5 us (4%)
  local copies, waits for them, and re-layouts  6.62 us (2%)
    all_gather x1, waiting for transfers between devices, on_device(): lax.all_gather(lax.all_gather(packed, 'hid', axis=0, tiled=True), 'exp',...  84.9 us
    reduce_scatter x1, waiting for transfers between devices, on_device(): lax.psum_scatter(input_part, 'exp', scatter_dimension=0, tiled=True)  76.1 us
    all_gather x1, blocking collectives, on_device(): lax.all_gather(lax.all_gather(logit_grad, 'hid', axis=0, tiled=True), 'ex...  44.3 us
    unnamed x4, waiting for transfers between devices  28.9 us
    all_gather x1, blocking collectives, on_device(): lax.all_gather(packed, 'hid', axis=0, tiled=True)  24.1 us
    all_gather x1, blocking collectives, on_device(): lax.all_gather(logit_grad, 'hid', axis=0, tiled=True)  12.5 us
    all_to_all x1, starting transfers between devices, on_device(): lax.all_to_all(shaped, 'exp', split_axis=0, concat_axis=3, tiled=True)  10.2 us
    all_to_all x1, waiting for transfers between devices, on_device(): lax.all_to_all(shaped, 'exp', split_axis=0, concat_axis=3, tiled=True)  9.62 us
  transfers between devices with their start and end apart: 5, of which 5 were waited for; matrix products, arithmetic and copies ran while one was open for 2% of the time, Pallas kernels for 0%

profile of v2, /device:TPU:1, one launch (start us, length us, event | category | flops | bytes accessed | tf_op | source)
XLA Modules:
  0.0 344.3 jit_solution(8106569013968727870)
XLA Ops:
  7.2 0.0 all-gather.4.cloned.1.call-start
  7.3 0.8 bitcast_or_fusion
  8.0 0.1 reshape.86
  8.1 1.4 gather_fusion
  9.6 0.1 reshape.89
  9.7 0.1 fusion.43
  9.8 0.2 fusion.34
  10.0 0.1 fusion.33
  10.0 0.1 select_reduce_fusion
  10.2 24.1 %all-gather = bf16[8,4,4224]{2,1,0:T(4,128)(2,1)S(1)} all-gather(bf16[1,4,4224]{2,1,0:T(4,128)(2,1)S(1)} %maximum_bitcast_fusion), channel_id=1, replica_groups=mesh['exp'=32,'hid'=8] {'hid'}, dimensions={0}, use_global_device_ids=true | all-gather | bytes 304128 | tf_op jit(solution)/shard_map/all_gather | solution.py:53
  34.3 0.8 reshape.98
  35.1 0.0 all-gather.4.cloned.1.call-update
  35.1 0.0 reduce-scatter.2.cloned.1.call-start
  35.2 84.9 %all-gather.4.cloned.1.call-done = bf16[1024,4224]{1,0:T(8,128)(2,1)} async-done(((bf16[32,4224]{1,0:T(8,128)(2,1)}), bf16[1024,4224]{1,0:T(8,128)(2,1)}) %all-gather.4.cloned.1.call-update) | async-done | bytes 8650768 | tf_op jit(solution)/shard_map/all_gather | solution.py:53
  120.1 1.1 fusion.27
  121.2 4.2 %fusion.2 = f32[1024,384]{0,1:T(8,128)S(1)} fusion(bf16[1024,4224]{1,0:T(8,128)(2,1)} %all-gather.4.cloned.1.call-done, bf16[1,2048,384]{2,1,0:T(8,128)(2,1)S(1)} %copy-done), kind=kOutput, calls=%fused_computation.4 | convolution fusion | flops 1610612736 | bytes 7340032 | tf_op jit(solution)/shard_map/td,udf->utf/dot_general | solution.py:22
  125.4 1.0 copy-done.7
  126.5 1.9 fusion.4
  128.3 2.0 fusion.7
  130.4 2.7 fusion.15
  133.1 5.7 %convolution_add_fusion = f32[1024,2048]{1,0:T(8,128)} fusion(f32[1024,2048]{1,0:T(8,128)S(1)} %fusion.15, bf16[1,2048,384]{2,1,0:T(8,128)(2,1)S(1)} %copy-done.2, f32[1024,384]{0,1:T(8,128)S(1)} %get-tuple-element.7, f32[1024,384]{0,1:T(8,128)S(1)} %fusion.2, f32[1024]{0:T(1024)S(1)} %bitcast.121), kind=kOutput, calls=%fused_computation.1 | convolution fusion | flops 1615462400 | bytes 21499904 | tf_op jit(solution)/shard_map/utf,udf->td/dot_general | solution.py:35
  138.8 0.1 reshape_transpose.3
  139.0 0.9 copy.35
  139.8 10.2 %all-to-all-start = ((f32[32,8,4,1,1]{1,2,4,3,0:T(4,128)}), f32[32,8,4,1,1]{1,2,4,3,0:T(4,128)S(1)}, u32[]{:S(2)}, u32[]{:S(2)}) async-start(f32[32,8,4,1,1]{1,2,4,3,0:T(4,128)} %copy.35), calls=%async_computation.1 | async-start | bytes 131072 | tf_op jit(solution)/shard_map/all_to_all | solution.py:71
  150.1 0.1 reduce_max.19
  150.2 9.6 %all-to-all-done = f32[32,8,4,1,1]{1,2,4,3,0:T(4,128)S(1)} async-done(((f32[32,8,4,1,1]{1,2,4,3,0:T(4,128)}), f32[32,8,4,1,1]{1,2,4,3,0:T(4,128)S(1)}, u32[]{:S(2)}, u32[]{:S(2)}) %all-to-all-start) | async-done | bytes 4128 | tf_op jit(solution)/shard_map/all_to_all | solution.py:71
  159.8 0.1 copy.36
  159.9 0.5 broadcast.72
  160.5 0.7 reduce.1
  161.2 0.7 reshape.104
  161.8 4.3 %all-to-all-start.1 = ((f32[8,1,128]{2,1,0:T(1,128)}), f32[8,1,128]{2,1,0:T(1,128)S(1)}, u32[]{:S(2)}, u32[]{:S(2)}) async-start(f32[8,1,128]{2,1,0:T(1,128)} %reshape.104), calls=%async_computation.2 | async-start | bytes 8192 | tf_op jit(solution)/shard_map/all_to_all | solution.py:70
  166.1 0.0 all-reduce.3.cloned.1.call-start
  166.2 0.2 fusion.36
  166.4 0.6 dynamic-slice
  167.5 3.5 %all-to-all-done.1 = f32[8,1,128]{2,1,0:T(1,128)S(1)} async-done(((f32[8,1,128]{2,1,0:T(1,128)}), f32[8,1,128]{2,1,0:T(1,128)S(1)}, u32[]{:S(2)}, u32[]{:S(2)}) %all-to-all-start.1) | async-done | bytes 4128 | tf_op jit(solution)/shard_map/all_to_all | solution.py:70
  171.1 0.7 reduce.2
  171.7 0.1 reshape.105
  171.8 0.1 copy.38
  172.0 0.2 reduce_sum.58
  172.1 0.1 copy.40
  172.2 0.2 multiply_reduce_fusion
  172.4 0.1 multiply_convert_fusion.1
  172.5 12.5 %all-gather.1 = bf16[8,4,128]{2,1,0:T(4,128)(2,1)S(1)} all-gather(bf16[1,4,128]{2,1,0:T(4,128)(2,1)S(1)} %bitcast.126), channel_id=1, replica_groups=mesh['exp'=32,'hid'=8] {'hid'}, dimensions={0}, use_global_device_ids=true | all-gather | bytes 9216 | tf_op jit(solution)/shard_map/all_gather | solution.py:82
  185.0 76.1 %reduce-scatter.2.cloned.1.call-done = f32[32,2048]{1,0:T(8,128)} async-done(((f32[1024,2048]{1,0:T(8,128)}), f32[32,2048]{1,0:T(8,128)}) %reduce-scatter.2.cloned.1.call-update) | async-done | bytes 262160 | tf_op jit(solution)/shard_map/reduce_scatter | solution.py:64
  261.1 44.3 %all_gather.15 = bf16[1024,128]{1,0:T(8,128)(2,1)S(1)} all-gather(bf16[32,128]{1,0:T(8,128)(2,1)S(1)} %bitcast.125), channel_id=1, replica_groups=mesh['exp'=32,'hid'=8] {'exp'}, dimensions={0}, use_global_device_ids=true | all-gather | bytes 270336 | tf_op jit(solution)/shard_map/all_gather | solution.py:81
  305.4 1.9 fusion.29
  307.3 28.8 %all-reduce.3.cloned.1.call-done = f32[32,2048]{1,0:T(8,128)} async-done(((f32[32,2048]{1,0:T(8,128)}), f32[32,2048]{1,0:T(8,128)}) %all-reduce.3.cloned.1.call-update) | async-done | bytes 262160
  336.1 1.7 fusion.6
  (23 shorter events, 0.1 us)
Async XLA Ops:
  7.2 114.1 %copy-start = (bf16[1,2048,384]{2,1,0:T(8,128)(2,1)S(1)}, bf16[1,2048,384]{2,1,0:T(8,128)(2,1)}, u32[]{:S(2)}) copy-start(bf16[1,2048,384]{2,1,0:T(8,128)(2,1)} %param.13) | copy-start | bytes 4718596
  7.2 2.5 copy-start.4
  7.2 3.0 copy-start.5
  7.2 3.0 copy-start.6
  7.2 112.9 %all-gather.4.cloned.1.call-start = ((), (), s32[]{:S(2)}) async-start(), calls=%async_computation.3 | async-start | bytes 8921088 | tf_op jit(solution)/shard_map/all_gather | solution.py:53
  35.1 225.9 %reduce-scatter.2.cloned.1.call-start = ((), (), s32[]{:S(2)}) async-start(), calls=%async_computation.4 | async-start | bytes 8650752 | tf_op jit(solution)/shard_map/reduce_scatter | solution.py:64
  121.2 4.2 %copy-start.2 = (bf16[1,2048,384]{2,1,0:T(8,128)(2,1)S(1)}, bf16[1,2048,384]{2,1,0:T(8,128)(2,1)}, u32[]{:S(2)}) copy-start(bf16[1,2048,384]{2,1,0:T(8,128)(2,1)} %param.14) | copy-start | bytes 4718596
  121.2 5.2 %copy-start.7 = (bf16[1024,4224]{1,0:T(8,128)(2,1)S(1)}, bf16[1024,4224]{1,0:T(8,128)(2,1)}, u32[]{:S(2)}) copy-start(bf16[1024,4224]{1,0:T(8,128)(2,1)} %all-gather.4.cloned.1.call-done) | copy-start | bytes 25952260
  126.5 1.9 copy-start.8
  138.8 11.3 %copy-start.1 = (f32[4,128]{1,0:T(4,128)S(1)}, f32[4,128]{1,0:T(4,128)}, u32[]{:S(2)}) copy-start(f32[4,128]{1,0:T(4,128)} %param.10) | copy-start | bytes 6148
  138.8 27.6 %copy-start.9 = (u32[256]{0:T(256)S(1)}, u32[256]{0:T(256)}, u32[]{:S(2)}) copy-start(u32[256]{0:T(256)} %constant.79) | copy-start | bytes 3076
  138.8 197.3 %copy-start.3 = (bf16[2048,128]{1,0:T(8,128)(2,1)S(1)}, bf16[2048,128]{1,0:T(8,128)(2,1)}, u32[]{:S(2)}) copy-start(bf16[2048,128]{1,0:T(8,128)(2,1)} %param.12) | copy-start | bytes 1572868
  139.8 20.0 %all-to-all-start = ((f32[32,8,4,1,1]{1,2,4,3,0:T(4,128)}), f32[32,8,4,1,1]{1,2,4,3,0:T(4,128)S(1)}, u32[]{:S(2)}, u32[]{:S(2)}) async-start(f32[32,8,4,1,1]{1,2,4,3,0:T(4,128)} %copy.35), calls=%async_computation.1 | async-start | bytes 131072 | tf_op jit(solution)/shard_map/all_to_all | solution.py:71
  161.8 9.2 %all-to-all-start.1 = ((f32[8,1,128]{2,1,0:T(1,128)}), f32[8,1,128]{2,1,0:T(1,128)S(1)}, u32[]{:S(2)}, u32[]{:S(2)}) async-start(f32[8,1,128]{2,1,0:T(1,128)} %reshape.104), calls=%async_computation.2 | async-start | bytes 8192 | tf_op jit(solution)/shard_map/all_to_all | solution.py:70
  166.1 170.0 %all-reduce.3.cloned.1.call-start = ((), (), s32[]{:S(2)}) async-start(), calls=%async_computation.5 | async-start | bytes 524288
Sparse Core Ops, SparseCore 0:
  35.2 84.8 all-gather.3
  138.9 122.0 reduce-scatter.1
  263.8 72.2 all-reduce.2

commit v3 on v2

--- a/solution.py
+++ b/solution.py
@@ -18,24 +18,42 @@
     return jnp.sum(weights[:, :, None] * matched, axis=1).astype(jnp.bfloat16)
 
 
-def unit_terms(x_rows, g_rows, c_rows, w_gate, w_up, w_down, unit_pick):
+CAP = 4
+
+
+def slot_rows(column, group_rows):
+    shaped = column.reshape(column.shape[:-1] + (-1, group_rows))
+    place = jnp.arange(group_rows, dtype=jnp.int32)
+    key = jnp.where(shaped != 0, 2 * group_rows - place, -place)
+    return lax.top_k(key, CAP)[1]
+
+
+def dense_terms(x_rows, g_rows, w_gate, w_up, w_down):
     gate_pre = jnp.einsum("td,udf->utf", x_rows, w_gate, preferred_element_type=jnp.float32)
     up_pre = jnp.einsum("td,udf->utf", x_rows, w_up, preferred_element_type=jnp.float32)
     back_grad = jnp.einsum("td,ufd->utf", g_rows, w_down, preferred_element_type=jnp.float32)
     sig_gate = jax.nn.sigmoid(gate_pre)
     act_gate = gate_pre * sig_gate
     score_part = jnp.sum(act_gate * up_pre * back_grad, axis=2).T
-    column_rows = jnp.dot(c_rows, unit_pick, preferred_element_type=jnp.float32)
-    weighted = column_rows.T[:, :, None] * back_grad
-    grad_gate = (weighted * up_pre * sig_gate * (1.0 + gate_pre * (1.0 - sig_gate))).astype(
-        jnp.bfloat16
-    )
+    return score_part, gate_pre, up_pre, back_grad
+
+
+def sparse_terms(gate_pre, up_pre, back_grad, column, w_gate, w_up, group_rows):
+    picked = slot_rows(column, group_rows)
+    groups = picked.shape[1]
+    starts = (jnp.arange(groups, dtype=jnp.int32) * group_rows)[None, :, None]
+    rows = (picked + starts).reshape(picked.shape[0], -1)
+    take = lambda a: jnp.take_along_axis(a, rows[:, :, None], axis=1)
+    gate_s, up_s, back_s = take(gate_pre), take(up_pre), take(back_grad)
+    col_s = jnp.take_along_axis(column, rows, axis=1)
+    sig_gate = jax.nn.sigmoid(gate_s)
+    act_gate = gate_s * sig_gate
+    weighted = col_s[:, :, None] * back_s
+    grad_gate = (weighted * up_s * sig_gate * (1.0 + gate_s * (1.0 - sig_gate))).astype(jnp.bfloat16)
     grad_up = (weighted * act_gate).astype(jnp.bfloat16)
-    input_part = jnp.einsum("utf,udf->td", grad_gate, w_gate, preferred_element_type=jnp.float32)
-    input_part = input_part + jnp.einsum(
-        "utf,udf->td", grad_up, w_up, preferred_element_type=jnp.float32
-    )
-    return (score_part, input_part, column_rows)
+    part = jnp.einsum("usf,udf->usd", grad_gate, w_gate, preferred_element_type=jnp.float32)
+    part = part + jnp.einsum("usf,udf->usd", grad_up, w_up, preferred_element_type=jnp.float32)
+    return part.reshape(part.shape[0], groups, CAP, part.shape[-1])
 
 
 def on_device(tokens, grad_out, router_logits, selected, router_w, w_gate, w_up, w_down):
@@ -44,6 +62,9 @@
     expert_count = router_logits.shape[1]
     spread_exp = lax.axis_size("exp")
     spread_hid = lax.axis_size("hid")
+    group_rows = spread_hid * tok_local
+    own_exp = lax.axis_index("exp")
+    own_hid = lax.axis_index("hid")
     own_block = lax.axis_index(("exp", "hid"))
     unit_expert = (own_block * unit_count + jnp.arange(unit_count, dtype=jnp.int32)) // 2
     expert_ids = jnp.arange(expert_count, dtype=jnp.int32)
@@ -51,21 +72,28 @@
     combine = combine_table(router_logits, selected, expert_count)
     packed = jnp.concatenate([tokens, grad_out, combine], axis=1)
     gathered = lax.all_gather(lax.all_gather(packed, "hid", axis=0, tiled=True), "exp", axis=0, tiled=True)
-    score_part, input_part, column_rows = unit_terms(
-        gathered[:, :model_width],
-        gathered[:, model_width : 2 * model_width],
-        gathered[:, 2 * model_width :],
-        w_gate,
-        w_up,
-        w_down,
-        unit_pick,
+    combine_all = gathered[:, 2 * model_width :]
+    score_part, gate_pre, up_pre, back_grad = dense_terms(
+        gathered[:, :model_width], gathered[:, model_width : 2 * model_width], w_gate, w_up, w_down
     )
-    input_sum = lax.psum_scatter(
-        lax.psum_scatter(input_part, "exp", scatter_dimension=0, tiled=True),
-        "hid",
-        scatter_dimension=0,
-        tiled=True,
+    column = jnp.dot(combine_all, unit_pick, preferred_element_type=jnp.float32).T
+    part = sparse_terms(gate_pre, up_pre, back_grad, column, w_gate, w_up, group_rows)
+    arrived_part = lax.all_to_all(jnp.swapaxes(part, 0, 1), "exp", split_axis=0, concat_axis=0, tiled=True)
+    sender_block = (jnp.arange(spread_exp, dtype=jnp.int32) * spread_hid + own_hid)[:, None]
+    sender_expert = (sender_block * unit_count + jnp.arange(unit_count, dtype=jnp.int32)[None, :]) // 2
+    own_combine = lax.dynamic_slice_in_dim(combine_all, own_exp * group_rows, group_rows, 0)
+    sender_pick = (expert_ids[:, None] == sender_expert.reshape(1, -1)).astype(jnp.bfloat16)
+    sender_column = jnp.dot(own_combine, sender_pick, preferred_element_type=jnp.float32).T
+    sender_rows = slot_rows(sender_column, group_rows).reshape(-1)
+    place = (sender_rows[:, None] == jnp.arange(group_rows, dtype=jnp.int32)[None, :]).astype(jnp.float32)
+    group_sum = jnp.einsum(
+        "sj,sd->jd", place, arrived_part.reshape(-1, model_width), precision=lax.Precision.HIGHEST,
+        preferred_element_type=jnp.float32,
     )
+    spread_rows = lax.all_to_all(
+        group_sum.reshape(spread_hid, tok_local, model_width), "hid", split_axis=0, concat_axis=0, tiled=True
+    )
+    input_sum = jnp.sum(spread_rows, axis=0)
     shaped = score_part.reshape(spread_exp, spread_hid, tok_local, 1, unit_count)
     arrived = lax.all_to_all(
         lax.all_to_all(shaped, "exp", split_axis=0, concat_axis=3, tiled=True),

time: 349 us -> 299 us (0.86); the launches traced: 344 us -> 299 us
  waiting for transfers between devices: 203 us -> 112 us
  local copies, waits for them, and re-layouts: 6.62 us -> 24.3 us
  starting transfers between devices: 14.7 us -> 30.1 us
  matrix products: 21.2 us -> 26.4 us
  blocking collectives: 80.9 us -> 85.6 us
    reduce_scatter x1 -> x0, waiting for transfers between devices: 76.1 us -> none  [on_device(): lax.psum_scatter(input_part, 'exp', scatter_dimension=0, tiled=True)]
    unnamed x4 -> x1, waiting for transfers between devices: 28.9 us -> 0.02 us
    all_to_all x0 -> x2, waiting for transfers between devices: none -> 22 us  [the longest x1 21.9 us: on_device(): lax.all_to_all(jnp.swapaxes(part, 0, 1), 'exp', split_axis=0, concat_axis...]
    all_to_all x0 -> x2, starting transfers between devices: none -> 15.5 us  [the longest x1 9.96 us: on_device(): lax.all_to_all(group_sum.reshape(spread_hid, tok_local, model_width), 'hi...]
    another operation x0 -> x4, local copies, waits for them, and re-layouts: none -> 9.45 us  [the longest x3 6.86 us: sparse_terms(): take = lambda a: jnp.take_along_axis(a, rows[:, :, None], axis=1)]
    dot_general x6 -> x8, matrix products: 17.6 us -> 23.7 us  [the longest x1 6.17 us: dense_terms(): jnp.einsum('td,ufd->utf', g_rows, w_down, preferred_element_type=jnp.floa...]
    gather x0 -> x4, local copies, waits for them, and re-layouts: none -> 6.04 us  [the longest x3 4.57 us: sparse_terms(): take = lambda a: jnp.take_along_axis(a, rows[:, :, None], axis=1)]
    all_to_all x1, waiting for transfers between devices: 9.62 us -> 4.86 us  [on_device(): lax.all_to_all(shaped, 'exp', split_axis=0, concat_axis=3, tiled=True)]
  transfers between devices with their start and end apart: 5 -> 5, of which waited for: 5 -> 3; matrix products, arithmetic and copies ran while one was open for 2% -> 5% of each run, Pallas kernels for 0% -> 0%
where the time goes in v3:
time: 299 us
  waiting for transfers between devices  112 us (37%)
  blocking collectives  85.6 us (29%)
  starting transfers between devices  30.1 us (10%)
  matrix products  26.4 us (9%)
  local copies, waits for them, and re-layouts  24.3 us (8%)
  between operations  14.3 us (5%)
  other arithmetic  5.93 us (2%)
    all_gather x1, waiting for transfers between devices, on_device(): lax.all_gather(lax.all_gather(packed, 'hid', axis=0, tiled=True), 'exp',...  85 us
    all_gather x1, blocking collectives, on_device(): lax.all_gather(lax.all_gather(logit_grad, 'hid', axis=0, tiled=True), 'ex...  46.1 us
    all_gather x1, blocking collectives, on_device(): lax.all_gather(packed, 'hid', axis=0, tiled=True)  24.1 us
    all_to_all x1, waiting for transfers between devices, on_device(): lax.all_to_all(jnp.swapaxes(part, 0, 1), 'exp', split_axis=0, concat_axis...  21.9 us
    all_gather x1, blocking collectives, on_device(): lax.all_gather(logit_grad, 'hid', axis=0, tiled=True)  15.4 us
    all_to_all x1, starting transfers between devices, on_device(): lax.all_to_all(shaped, 'exp', split_axis=0, concat_axis=3, tiled=True)  10.3 us
    all_to_all x1, starting transfers between devices, on_device(): lax.all_to_all(group_sum.reshape(spread_hid, tok_local, model_width), 'hi...  9.96 us
    another operation x3, local copies, waits for them, and re-layouts, sparse_terms(): take = lambda a: jnp.take_along_axis(a, rows[:, :, None], axis=1)  6.86 us
  transfers between devices with their start and end apart: 5, of which 3 were waited for; matrix products, arithmetic and copies ran while one was open for 5% of the time, Pallas kernels for 0%

profile of v3, /device:TPU:1, one launch (start us, length us, event | category | flops | bytes accessed | tf_op | source)
XLA Modules:
  0.0 298.5 jit_solution(2743726140676566130)
XLA Ops:
  7.3 0.8 bitcast_or_fusion
  8.1 1.4 gather_fusion.1
  9.8 0.2 fusion.45
  10.2 24.1 %all-gather = bf16[8,4,4224]{2,1,0:T(4,128)(2,1)S(1)} all-gather(bf16[1,4,4224]{2,1,0:T(4,128)(2,1)S(1)} %maximum_bitcast_fusion), channel_id=1, replica_groups=mesh['exp'=32,'hid'=8] {'hid'}, dimensions={0}, use_global_device_ids=true | all-gather | bytes 304128 | tf_op jit(solution)/shard_map/all_gather | solution.py:74
  34.3 0.8 reshape.433
  35.1 85.0 %all-gather.4.cloned.1.call-done = bf16[1024,4224]{1,0:T(8,128)(2,1)} async-done(((bf16[32,4224]{1,0:T(8,128)(2,1)}), bf16[1024,4224]{1,0:T(8,128)(2,1)}) %all-gather.4.cloned.1.call-update) | async-done | bytes 8650768 | tf_op jit(solution)/shard_map/all_gather | solution.py:74
  120.1 1.1 fusion.41
  121.5 0.8 top_k.24
  122.7 0.6 reshape.364
  123.3 1.5 gather_fusion
  124.8 5.2 %fusion.4 = f32[1024,384]{0,1:T(8,128)} fusion(bf16[1024,4224]{1,0:T(8,128)(2,1)} %all-gather.4.cloned.1.call-done, bf16[1,2048,384]{2,1,0:T(8,128)(2,1)S(1)} %copy-done.2), kind=kOutput, calls=%fused_computation.9 | convolution fusion | flops 1610612736 | bytes 7340032 | tf_op jit(solution)/shard_map/td,udf->utf/dot_general | solution.py:33
  130.0 1.9 copy.84
  131.9 5.2 %fusion.2 = f32[1024,384]{0,1:T(8,128)} fusion(bf16[1024,4224]{1,0:T(8,128)(2,1)} %all-gather.4.cloned.1.call-done, bf16[1,2048,384]{2,1,0:T(8,128)(2,1)S(1)} %copy-done), kind=kOutput, calls=%fused_computation.7 | convolution fusion | flops 1610612736 | bytes 7340032 | tf_op jit(solution)/shard_map/td,udf->utf/dot_general | solution.py:32
  137.1 3.1 %copy.85 = f32[1024,384]{1,0:T(8,128)} copy(f32[1024,384]{0,1:T(8,128)} %fusion.2) | data formatting | bytes 3145728 | tf_op jit(solution)/shard_map/jit(take_along_axis)/Arg_0.9 | solution.py:46
  140.2 1.4 gather_fusion.3
  141.6 2.4 gather_fusion.4
  144.0 6.2 %fusion.7 = (f32[1024]{0:T(1024)S(1)}, f32[1024,384]{0,1:T(8,128)}) fusion(f32[1024,384]{0,1:T(8,128)S(1)} %copy-done.3, f32[1024,384]{0,1:T(8,128)} %fusion.2, bf16[1,384,2048]{2,1,0:T(8,128)(2,1)} %param.17, bf16[1024,4224]{1,0:T(8,128)(2,1)} %all-gather.4.cloned.1.call-done), kind=kOutput, calls=%fused_computation.15 | convolution fusion | flops 1613364224 | bytes 10489856 | tf_op jit(solution)/shard_map/td,ufd->utf/dot_general | solution.py:34
  150.2 0.1 reshape_transpose.4
  150.3 0.9 copy.88
  151.2 10.3 %all-to-all-start.2 = ((f32[32,8,4,1,1]{1,2,4,3,0:T(4,128)}), f32[32,8,4,1,1]{1,2,4,3,0:T(4,128)}, u32[]{:S(2)}, u32[]{:S(2)}) async-start(f32[32,8,4,1,1]{1,2,4,3,0:T(4,128)} %copy.88), calls=%async_computation.2 | async-start | bytes 131072 | tf_op jit(solution)/shard_map/all_to_all | solution.py:99
  161.5 1.9 copy.83
  163.4 0.8 gather_fusion.2
  164.1 0.7 and_select_fusion
  164.8 1.6 fusion.11
  166.4 4.9 %all-to-all-done.2 = f32[32,8,4,1,1]{1,2,4,3,0:T(4,128)} async-done(((f32[32,8,4,1,1]{1,2,4,3,0:T(4,128)}), f32[32,8,4,1,1]{1,2,4,3,0:T(4,128)}, u32[]{:S(2)}, u32[]{:S(2)}) %all-to-all-start.2) | async-done | bytes 4128 | tf_op jit(solution)/shard_map/all_to_all | solution.py:99
  171.3 0.9 copy.89
  172.2 0.5 broadcast.335
  172.8 0.7 reduce.1
  173.4 0.7 reshape.455
  174.1 4.3 %all-to-all-start.3 = ((f32[8,1,128]{2,1,0:T(1,128)}), f32[8,1,128]{2,1,0:T(1,128)S(1)}, u32[]{:S(2)}, u32[]{:S(2)}) async-start(f32[8,1,128]{2,1,0:T(1,128)} %reshape.455), calls=%async_computation.3 | async-start | bytes 8192 | tf_op jit(solution)/shard_map/all_to_all | solution.py:98
  178.4 3.0 %convolution_add_fusion = f32[128,2048]{1,0:T(8,128)} fusion(f32[128,2048]{1,0:T(8,128)S(1)} %fusion.11, bf16[1,2048,384]{2,1,0:T(8,128)(2,1)} %param.16, f32[128,384]{1,0:T(8,128)S(1)} %gather_fusion.4, f32[128,384]{1,0:T(8,128)S(1)} %gather_fusion.2, f32[128]{0:T(128)S(1)} %and_select_fusion, pred[128]{0:T(512)(128)(4,1)S(1)} %and_bitcast_fusion), kind=kOutput, calls=%fused_computation.11 | convolution fusion | flops 202031104 | bytes 4063872 | tf_op jit(solution)/shard_map/usf,udf->usd/dot_general | solution.py:55
  181.5 2.6 transpose_reshape.3
  184.1 5.5 %all-to-all-start = ((f32[32,1,4,2048]{3,2,1,0:T(4,128)}), f32[32,1,4,2048]{3,2,1,0:T(4,128)}, u32[]{:S(2)}, u32[]{:S(2)}) async-start(f32[32,1,4,2048]{3,2,1,0:T(4,128)} %bitcast.34), calls=%async_computation | async-start | bytes 2097152 | tf_op jit(solution)/shard_map/all_to_all | solution.py:81
  189.8 0.2 fusion.47
  190.0 0.2 fusion.18
  190.2 0.8 top_k.17
  191.3 0.7 reduce.2
  192.1 0.1 copy.91
  192.2 0.2 reduce_sum.68
  192.4 0.2 multiply_reduce_fusion
  192.6 21.9 %all-to-all-done = f32[32,1,4,2048]{3,2,1,0:T(4,128)} async-done(((f32[32,1,4,2048]{3,2,1,0:T(4,128)}), f32[32,1,4,2048]{3,2,1,0:T(4,128)}, u32[]{:S(2)}, u32[]{:S(2)}) %all-to-all-start) | async-done | bytes 1048608 | tf_op jit(solution)/shard_map/all_to_all | solution.py:81
  214.6 1.6 reshape.453
  216.2 1.2 fusion.38
  217.4 10.0 %all-to-all-start.1 = ((f32[8,4,2048]{2,1,0:T(4,128)}), f32[8,4,2048]{2,1,0:T(4,128)S(1)}, u32[]{:S(2)}, u32[]{:S(2)}) async-start(f32[8,4,2048]{2,1,0:T(4,128)} %fusion.38), calls=%async_computation.1 | async-start | bytes 524288 | tf_op jit(solution)/shard_map/all_to_all | solution.py:93
  227.4 15.4 %all-gather.1 = bf16[8,4,128]{2,1,0:T(4,128)(2,1)S(1)} all-gather(bf16[1,4,128]{2,1,0:T(4,128)(2,1)S(1)} %bitcast.152), channel_id=1, replica_groups=mesh['exp'=32,'hid'=8] {'hid'}, dimensions={0}, use_global_device_ids=true | all-gather | bytes 9216 | tf_op jit(solution)/shard_map/all_gather | solution.py:110
  242.8 46.1 %all_gather.15 = bf16[1024,128]{1,0:T(8,128)(2,1)S(1)} all-gather(bf16[32,128]{1,0:T(8,128)(2,1)S(1)} %bitcast.151), channel_id=1, replica_groups=mesh['exp'=32,'hid'=8] {'exp'}, dimensions={0}, use_global_device_ids=true | all-gather | bytes 270336 | tf_op jit(solution)/shard_map/all_gather | solution.py:109
  288.9 1.9 fusion.19
  290.8 0.9 fusion.6
  (58 shorter events, 1.9 us)
Async XLA Ops:
  7.2 124.7 %copy-start = (bf16[1,2048,384]{2,1,0:T(8,128)(2,1)S(1)}, bf16[1,2048,384]{2,1,0:T(8,128)(2,1)}, u32[]{:S(2)}) copy-start(bf16[1,2048,384]{2,1,0:T(8,128)(2,1)} %param.15) | copy-start | bytes 4718596
  7.2 2.5 copy-start.5
  7.2 3.0 copy-start.6
  7.2 3.0 copy-start.7
  7.2 112.9 %all-gather.4.cloned.1.call-start = ((), (), s32[]{:S(2)}) async-start(), calls=%async_computation.4 | async-start | bytes 8921088 | tf_op jit(solution)/shard_map/all_gather | solution.py:74
  9.6 115.2 %copy-start.2 = (bf16[1,2048,384]{2,1,0:T(8,128)(2,1)S(1)}, bf16[1,2048,384]{2,1,0:T(8,128)(2,1)}, u32[]{:S(2)}) copy-start(bf16[1,2048,384]{2,1,0:T(8,128)(2,1)} %param.16) | copy-start | bytes 4718596
  141.6 2.4 copy-start.3
  151.2 20.1 %all-to-all-start.2 = ((f32[32,8,4,1,1]{1,2,4,3,0:T(4,128)}), f32[32,8,4,1,1]{1,2,4,3,0:T(4,128)}, u32[]{:S(2)}, u32[]{:S(2)}) async-start(f32[32,8,4,1,1]{1,2,4,3,0:T(4,128)} %copy.88), calls=%async_computation.2 | async-start | bytes 131072 | tf_op jit(solution)/shard_map/all_to_all | solution.py:99
  174.1 9.9 %all-to-all-start.3 = ((f32[8,1,128]{2,1,0:T(1,128)}), f32[8,1,128]{2,1,0:T(1,128)S(1)}, u32[]{:S(2)}, u32[]{:S(2)}) async-start(f32[8,1,128]{2,1,0:T(1,128)} %reshape.455), calls=%async_computation.3 | async-start | bytes 8192 | tf_op jit(solution)/shard_map/all_to_all | solution.py:98
  184.1 5.6 %copy-start.1 = (f32[4,128]{1,0:T(4,128)S(1)}, f32[4,128]{1,0:T(4,128)}, u32[]{:S(2)}) copy-start(f32[4,128]{1,0:T(4,128)} %param.12) | copy-start | bytes 6148
  184.1 5.9 %slice-start = ((bf16[1024,4224]{1,0:T(8,128)(2,1)}), bf16[1024,128]{1,0:T(8,128)(2,1)S(1)}, s32[]{:S(2)}) async-start(bf16[1024,4224]{1,0:T(8,128)(2,1)} %all-gather.4.cloned.1.call-done), calls=%async_computation.5 | async-start | bytes 524288 | tf_op jit(solution)/shard_map/slice | solution.py:75
  184.1 30.5 %all-to-all-start = ((f32[32,1,4,2048]{3,2,1,0:T(4,128)}), f32[32,1,4,2048]{3,2,1,0:T(4,128)}, u32[]{:S(2)}, u32[]{:S(2)}) async-start(f32[32,1,4,2048]{3,2,1,0:T(4,128)} %bitcast.34), calls=%async_computation | async-start | bytes 2097152 | tf_op jit(solution)/shard_map/all_to_all | solution.py:81
  216.2 74.6 %copy-start.4 = (bf16[2048,128]{1,0:T(8,128)(2,1)S(1)}, bf16[2048,128]{1,0:T(8,128)(2,1)}, u32[]{:S(2)}) copy-start(bf16[2048,128]{1,0:T(8,128)(2,1)} %param.14) | copy-start | bytes 1572868
  217.4 73.4 %all-to-all-start.1 = ((f32[8,4,2048]{2,1,0:T(4,128)}), f32[8,4,2048]{2,1,0:T(4,128)S(1)}, u32[]{:S(2)}, u32[]{:S(2)}) async-start(f32[8,4,2048]{2,1,0:T(4,128)} %fusion.38), calls=%async_computation.1 | async-start | bytes 524288 | tf_op jit(solution)/shard_map/all_to_all | solution.py:93
Sparse Core Ops, SparseCore 0:
  35.2 84.8 all-gather.3

commit v4 on v3

--- a/solution.py
+++ b/solution.py
@@ -78,7 +78,11 @@
     )
     column = jnp.dot(combine_all, unit_pick, preferred_element_type=jnp.float32).T
     part = sparse_terms(gate_pre, up_pre, back_grad, column, w_gate, w_up, group_rows)
-    arrived_part = lax.all_to_all(jnp.swapaxes(part, 0, 1), "exp", split_axis=0, concat_axis=0, tiled=True)
+    lane = 128
+    score_grp = jnp.swapaxes(score_part.T.reshape(unit_count, spread_exp, CAP, group_rows // CAP), 0, 1)
+    score_grp = jnp.pad(score_grp, ((0, 0), (0, 0), (0, 0), (0, lane - group_rows // CAP)))
+    sent = jnp.concatenate([jnp.swapaxes(part, 0, 1), score_grp], axis=3)
+    arrived_part = lax.all_to_all(sent, "exp", split_axis=0, concat_axis=0, tiled=True)
     sender_block = (jnp.arange(spread_exp, dtype=jnp.int32) * spread_hid + own_hid)[:, None]
     sender_expert = (sender_block * unit_count + jnp.arange(unit_count, dtype=jnp.int32)[None, :]) // 2
     own_combine = lax.dynamic_slice_in_dim(combine_all, own_exp * group_rows, group_rows, 0)
@@ -87,29 +91,30 @@
     sender_rows = slot_rows(sender_column, group_rows).reshape(-1)
     place = (sender_rows[:, None] == jnp.arange(group_rows, dtype=jnp.int32)[None, :]).astype(jnp.float32)
     group_sum = jnp.einsum(
-        "sj,sd->jd", place, arrived_part.reshape(-1, model_width), precision=lax.Precision.HIGHEST,
-        preferred_element_type=jnp.float32,
+        "sj,sd->jd", place, arrived_part[..., :model_width].reshape(-1, model_width),
+        precision=lax.Precision.HIGHEST, preferred_element_type=jnp.float32,
     )
-    spread_rows = lax.all_to_all(
-        group_sum.reshape(spread_hid, tok_local, model_width), "hid", split_axis=0, concat_axis=0, tiled=True
-    )
-    input_sum = jnp.sum(spread_rows, axis=0)
-    shaped = score_part.reshape(spread_exp, spread_hid, tok_local, 1, unit_count)
-    arrived = lax.all_to_all(
-        lax.all_to_all(shaped, "exp", split_axis=0, concat_axis=3, tiled=True),
-        "hid",
-        split_axis=1,
-        concat_axis=4,
-        tiled=True,
-    )
-    expert_scores = jnp.sum(arrived.reshape(tok_local, expert_count, 2), axis=2)
+    got_scores = arrived_part[..., model_width : model_width + group_rows // CAP]
+    got_scores = got_scores.reshape(spread_exp, unit_count, spread_hid, tok_local)
+    score_cols = spread_exp * unit_count
+    score_width = -(-score_cols // lane) * lane
+    hid_scores = jnp.transpose(got_scores, (2, 3, 0, 1)).reshape(spread_hid, tok_local, score_cols)
+    hid_scores = jnp.pad(hid_scores, ((0, 0), (0, 0), (0, score_width - score_cols)))
+    hid_sent = jnp.concatenate([group_sum.reshape(spread_hid, tok_local, model_width), hid_scores], axis=2)
+    spread_rows = lax.all_to_all(hid_sent, "hid", split_axis=0, concat_axis=0, tiled=True)
+    input_sum = jnp.sum(spread_rows[..., :model_width], axis=0)
+    own_scores = spread_rows[..., model_width : model_width + score_cols]
+    own_scores = own_scores.reshape(spread_hid, tok_local, spread_exp, unit_count)
+    unit_scores = jnp.transpose(own_scores, (1, 2, 0, 3)).reshape(tok_local, -1)
+    expert_scores = jnp.sum(unit_scores.reshape(tok_local, expert_count, 2), axis=2)
     probs_all = softmax_rows(router_logits)
     mean_score = jnp.sum(probs_all * expert_scores, axis=1, keepdims=True)
     logit_grad = (probs_all * (expert_scores - mean_score)).astype(jnp.bfloat16)
-    logit_all = lax.all_gather(
-        lax.all_gather(logit_grad, "hid", axis=0, tiled=True), "exp", axis=0, tiled=True
-    )
-    grad_rows = model_width // (spread_exp * spread_hid)
+    devices = spread_exp * spread_hid
+    logit_all = lax.all_to_all(
+        jnp.broadcast_to(logit_grad[None], (devices,) + logit_grad.shape), ("exp", "hid"), 0, 0, tiled=True
+    ).reshape(-1, expert_count)
+    grad_rows = model_width // devices
     token_cols = lax.dynamic_slice_in_dim(gathered, own_block * grad_rows, grad_rows, 1)
     router_grad = jnp.einsum("tc,te->ce", token_cols, logit_all, preferred_element_type=jnp.float32)
     router_part = jnp.einsum("te,de->td", logit_grad, router_w, preferred_element_type=jnp.float32)

time: 299 us -> 251 us (0.84)
  blocking collectives: 85.6 us -> 24.1 us
  waiting for transfers between devices: 112 us -> 134 us
  starting transfers between devices: 30.1 us -> 23.6 us
    all_gather x2 -> x0, blocking collectives: 61.5 us -> none  [the longest x1 46.1 us: on_device(): lax.all_gather(lax.all_gather(logit_grad, 'hid', axis=0, tiled=True), 'ex...]
    all_to_all x4 -> x3, waiting for transfers between devices: 26.8 us -> 49.1 us  [the longest x1 28.5 us: on_device(): lax.all_to_all(sent, 'exp', split_axis=0, concat_axis=0, tiled=True)]
    all_to_all x4 -> x3, starting transfers between devices: 30.1 us -> 23.5 us  [the longest x1 10.4 us: on_device(): lax.all_to_all(sent, 'exp', split_axis=0, concat_axis=0, tiled=True)]
  transfers between devices with their start and end apart: 5 -> 4, of which waited for: 3 -> 4; matrix products, arithmetic and copies ran while one was open for 5% -> 1% of each run, Pallas kernels for 0% -> 0%
where the time goes in v4:
time: 251 us; the launch traced here: 250 us
  waiting for transfers between devices  134 us (53%)
  blocking collectives  24.1 us (10%)
  starting transfers between devices  23.6 us (9%)
  matrix products  23.5 us (9%)
  local copies, waits for them, and re-layouts  23.4 us (9%)
  between operations  14.4 us (6%)
  other arithmetic  7.08 us (3%)
    all_gather x1, waiting for transfers between devices, on_device(): lax.all_gather(lax.all_gather(packed, 'hid', axis=0, tiled=True), 'exp',...  85 us
    all_to_all x1, waiting for transfers between devices, on_device(): lax.all_to_all(sent, 'exp', split_axis=0, concat_axis=0, tiled=True)  28.5 us
    all_gather x1, blocking collectives, on_device(): lax.all_gather(packed, 'hid', axis=0, tiled=True)  24.1 us
    all_to_all x1, waiting for transfers between devices, on_device(): lax.all_to_all(jnp.broadcast_to(logit_grad[None], (devices,) + logit_grad...  14.8 us
    all_to_all x1, starting transfers between devices, on_device(): lax.all_to_all(sent, 'exp', split_axis=0, concat_axis=0, tiled=True)  10.4 us
    all_to_all x1, starting transfers between devices, on_device(): lax.all_to_all(jnp.broadcast_to(logit_grad[None], (devices,) + logit_grad...  9.1 us
    another operation x3, local copies, waits for them, and re-layouts, sparse_terms(): take = lambda a: jnp.take_along_axis(a, rows[:, :, None], axis=1)  6.86 us
    dot_general x1, matrix products, dense_terms(): jnp.einsum('td,ufd->utf', g_rows, w_down, preferred_element_type=jnp.floa...  6.17 us
  transfers between devices with their start and end apart: 4, of which 4 were waited for; matrix products, arithmetic and copies ran while one was open for 1% of the time, Pallas kernels for 0%

profile of v4, /device:TPU:1, one launch (start us, length us, event | category | flops | bytes accessed | tf_op | source)
XLA Modules:
  0.0 250.1 jit_solution(14854167661253626803)
XLA Ops:
  7.3 0.8 bitcast_or_fusion
  8.1 1.4 gather_fusion.1
  9.7 0.1 fusion.62
  9.8 0.2 fusion.47
  10.2 24.1 %all-gather = bf16[8,4,4224]{2,1,0:T(4,128)(2,1)S(1)} all-gather(bf16[1,4,4224]{2,1,0:T(4,128)(2,1)S(1)} %maximum_bitcast_fusion), channel_id=1, replica_groups=mesh['exp'=32,'hid'=8] {'hid'}, dimensions={0}, use_global_device_ids=true | all-gather | bytes 304128 | tf_op jit(solution)/shard_map/all_gather | solution.py:74
  34.3 0.8 reshape.445
  35.1 85.0 %all-gather.3.cloned.1.call-done = bf16[1024,4224]{1,0:T(8,128)(2,1)} async-done(((bf16[32,4224]{1,0:T(8,128)(2,1)}), bf16[1024,4224]{1,0:T(8,128)(2,1)}) %all-gather.3.cloned.1.call-update) | async-done | bytes 8650768 | tf_op jit(solution)/shard_map/all_gather | solution.py:74
  120.1 1.1 fusion.43
  121.5 0.8 top_k.24
  122.4 0.1 reshape.376
  122.7 0.6 reshape.373
  123.3 1.5 gather_fusion
  124.8 5.3 %fusion.4 = f32[1024,384]{0,1:T(8,128)} fusion(bf16[1024,4224]{1,0:T(8,128)(2,1)} %all-gather.3.cloned.1.call-done, bf16[1,2048,384]{2,1,0:T(8,128)(2,1)S(1)} %copy-done.2), kind=kOutput, calls=%fused_computation.9 | convolution fusion | flops 1610612736 | bytes 7340032 | tf_op jit(solution)/shard_map/td,udf->utf/dot_general | solution.py:33
  130.0 1.9 copy.90
  131.9 5.2 %fusion.2 = f32[1024,384]{0,1:T(8,128)} fusion(bf16[1024,4224]{1,0:T(8,128)(2,1)} %all-gather.3.cloned.1.call-done, bf16[1,2048,384]{2,1,0:T(8,128)(2,1)S(1)} %copy-done), kind=kOutput, calls=%fused_computation.7 | convolution fusion | flops 1610612736 | bytes 7340032 | tf_op jit(solution)/shard_map/td,udf->utf/dot_general | solution.py:32
  137.1 3.1 %copy.91 = f32[1024,384]{1,0:T(8,128)} copy(f32[1024,384]{0,1:T(8,128)} %fusion.2) | data formatting | bytes 3145728 | tf_op jit(solution)/shard_map/jit(take_along_axis)/Arg_0.9 | solution.py:46
  140.2 1.4 gather_fusion.3
  141.6 2.4 gather_fusion.4
  144.0 6.2 %fusion.7 = (f32[1024]{0:T(1024)S(1)}, f32[1024,384]{0,1:T(8,128)}) fusion(f32[1024,384]{0,1:T(8,128)S(1)} %copy-done.4, f32[1024,384]{0,1:T(8,128)} %fusion.2, bf16[1,384,2048]{2,1,0:T(8,128)(2,1)} %param.17, bf16[1024,4224]{1,0:T(8,128)(2,1)} %all-gather.3.cloned.1.call-done), kind=kOutput, calls=%fused_computation.15 | convolution fusion | flops 1613364224 | bytes 10489856 | tf_op jit(solution)/shard_map/td,ufd->utf/dot_general | solution.py:34
  150.2 0.1 transpose_reshape.7
  150.3 0.6 pad_bitcast_fusion
  150.9 1.9 copy.89
  152.8 0.8 gather_fusion.2
  153.6 0.7 and_select_fusion
  154.3 1.7 fusion.11
  156.0 0.7 convolution_add_fusion
  156.7 1.3 transpose_reshape.6
  158.0 2.6 %pad_maximum_fusion = f32[32,1,4,2176]{3,2,1,0:T(4,128)} fusion(f32[32,1,4,128]{3,2,1,0:T(4,128)S(1)} %copy-done.6, f32[32,1,4,2048]{3,2,1,0:T(4,128)} %bitcast.146), kind=kLoop, calls=%fused_computation.28 | loop fusion | flops 278528 | bytes 2228224 | tf_op jit(solution)/shard_map/concatenate | solution.py:84
  160.5 10.4 %all-to-all-start = ((f32[32,1,4,2176]{3,2,1,0:T(4,128)}), f32[32,1,4,2176]{3,2,1,0:T(4,128)S(1)}, u32[]{:S(2)}, u32[]{:S(2)}) async-start(f32[32,1,4,2176]{3,2,1,0:T(4,128)} %pad_maximum_fusion), calls=%async_computation | async-start | bytes 2228224 | tf_op jit(solution)/shard_map/all_to_all | solution.py:85
  171.0 0.2 fusion.18
  171.2 0.8 top_k.17
  172.2 28.5 %all-to-all-done = f32[32,1,4,2176]{3,2,1,0:T(4,128)S(1)} async-done(((f32[32,1,4,2176]{3,2,1,0:T(4,128)}), f32[32,1,4,2176]{3,2,1,0:T(4,128)S(1)}, u32[]{:S(2)}, u32[]{:S(2)}) %all-to-all-start) | async-done | bytes 1114144 | tf_op jit(solution)/shard_map/all_to_all | solution.py:85
  200.8 1.2 slice.45
  202.0 1.6 reshape.463
  203.6 0.5 fusion.38
  204.2 0.8 copy.96
  205.0 4.0 %all-to-all-start.1 = ((f32[8,4,2176]{2,1,0:T(4,128)}), f32[8,4,2176]{2,1,0:T(4,128)S(1)}, u32[]{:S(2)}, u32[]{:S(2)}) async-start(f32[8,4,2176]{2,1,0:T(4,128)} %copy.96), calls=%async_computation.1 | async-start | bytes 557056 | tf_op jit(solution)/shard_map/all_to_all | solution.py:104
  209.0 0.1 reduce_max.19
  209.1 0.2 fusion.49
  209.3 5.8 %all-to-all-done.1 = f32[8,4,2176]{2,1,0:T(4,128)S(1)} async-done(((f32[8,4,2176]{2,1,0:T(4,128)}), f32[8,4,2176]{2,1,0:T(4,128)S(1)}, u32[]{:S(2)}, u32[]{:S(2)}) %all-to-all-start.1) | async-done | bytes 278560 | tf_op jit(solution)/shard_map/all_to_all | solution.py:104
  215.2 0.1 copy.97
  215.3 0.2 reduce_sum.68
  215.5 0.2 multiply_reduce_fusion
  215.8 0.8 broadcast_in_dim.59
  216.6 9.1 %all-to-all-start.2 = ((bf16[256,4,128]{2,1,0:T(4,128)(2,1)}), bf16[256,4,128]{2,1,0:T(4,128)(2,1)S(1)}, u32[]{:S(2)}, u32[]{:S(2)}) async-start(bf16[256,4,128]{2,1,0:T(4,128)(2,1)} %broadcast_in_dim.59), calls=%async_computation.2 | async-start | bytes 524288 | tf_op jit(solution)/shard_map/all_to_all | solution.py:114
  225.8 0.9 fusion.6
  226.6 14.8 %all-to-all-done.2 = bf16[256,4,128]{2,1,0:T(4,128)(2,1)S(1)} async-done(((bf16[256,4,128]{2,1,0:T(4,128)(2,1)}), bf16[256,4,128]{2,1,0:T(4,128)(2,1)S(1)}, u32[]{:S(2)}, u32[]{:S(2)}) %all-to-all-start.2) | async-done | bytes 262176 | tf_op jit(solution)/shard_map/all_to_all | solution.py:114
  241.4 1.9 fusion.19
  (59 shorter events, 1.5 us)
Async XLA Ops:
  7.2 124.7 %copy-start = (bf16[1,2048,384]{2,1,0:T(8,128)(2,1)S(1)}, bf16[1,2048,384]{2,1,0:T(8,128)(2,1)}, u32[]{:S(2)}) copy-start(bf16[1,2048,384]{2,1,0:T(8,128)(2,1)} %param.15) | copy-start | bytes 4718596
  7.2 2.5 copy-start.7
  7.2 3.0 %copy-start.8 = (bf16[4,2048]{1,0:T(4,128)(2,1)S(1)}, bf16[4,2048]{1,0:T(4,128)(2,1)}, u32[]{:S(2)}) copy-start(bf16[4,2048]{1,0:T(4,128)(2,1)} %param.11) | copy-start | bytes 49156
  7.2 3.0 %copy-start.9 = (bf16[4,2048]{1,0:T(4,128)(2,1)S(1)}, bf16[4,2048]{1,0:T(4,128)(2,1)}, u32[]{:S(2)}) copy-start(bf16[4,2048]{1,0:T(4,128)(2,1)} %param.10) | copy-start | bytes 49156
  7.2 112.9 %all-gather.3.cloned.1.call-start = ((), (), s32[]{:S(2)}) async-start(), calls=%async_computation.3 | async-start | bytes 8921088 | tf_op jit(solution)/shard_map/all_gather | solution.py:74
  9.6 115.2 %copy-start.2 = (bf16[1,2048,384]{2,1,0:T(8,128)(2,1)S(1)}, bf16[1,2048,384]{2,1,0:T(8,128)(2,1)}, u32[]{:S(2)}) copy-start(bf16[1,2048,384]{2,1,0:T(8,128)(2,1)} %param.16) | copy-start | bytes 4718596
  141.6 2.4 copy-start.4
  154.3 1.7 copy-start.3
  156.7 1.3 copy-start.6
  160.5 10.4 %slice-start = ((bf16[1024,4224]{1,0:T(8,128)(2,1)}), bf16[1024,128]{1,0:T(8,128)(2,1)S(1)}, s32[]{:S(2)}) async-start(bf16[1024,4224]{1,0:T(8,128)(2,1)} %all-gather.3.cloned.1.call-done), calls=%async_computation.4 | async-start | bytes 524288 | tf_op jit(solution)/shard_map/slice | solution.py:75
  160.5 40.2 %all-to-all-start = ((f32[32,1,4,2176]{3,2,1,0:T(4,128)}), f32[32,1,4,2176]{3,2,1,0:T(4,128)S(1)}, u32[]{:S(2)}, u32[]{:S(2)}) async-start(f32[32,1,4,2176]{3,2,1,0:T(4,128)} %pad_maximum_fusion), calls=%async_computation | async-start | bytes 2228224 | tf_op jit(solution)/shard_map/all_to_all | solution.py:85
  203.6 5.4 %copy-start.1 = (f32[4,128]{1,0:T(4,128)S(1)}, f32[4,128]{1,0:T(4,128)}, u32[]{:S(2)}) copy-start(f32[4,128]{1,0:T(4,128)} %param.12) | copy-start | bytes 6148
  204.1 21.6 %copy-start.5 = (bf16[2048,128]{1,0:T(8,128)(2,1)S(1)}, bf16[2048,128]{1,0:T(8,128)(2,1)}, u32[]{:S(2)}) copy-start(bf16[2048,128]{1,0:T(8,128)(2,1)} %param.14) | copy-start | bytes 1572868
  205.0 10.2 %all-to-all-start.1 = ((f32[8,4,2176]{2,1,0:T(4,128)}), f32[8,4,2176]{2,1,0:T(4,128)S(1)}, u32[]{:S(2)}, u32[]{:S(2)}) async-start(f32[8,4,2176]{2,1,0:T(4,128)} %copy.96), calls=%async_computation.1 | async-start | bytes 557056 | tf_op jit(solution)/shard_map/all_to_all | solution.py:104
  216.6 24.8 %all-to-all-start.2 = ((bf16[256,4,128]{2,1,0:T(4,128)(2,1)}), bf16[256,4,128]{2,1,0:T(4,128)(2,1)S(1)}, u32[]{:S(2)}, u32[]{:S(2)}) async-start(bf16[256,4,128]{2,1,0:T(4,128)(2,1)} %broadcast_in_dim.59), calls=%async_computation.2 | async-start | bytes 524288 | tf_op jit(solution)/shard_map/all_to_all | solution.py:114
Sparse Core Ops, SparseCore 0:
  35.2 84.8 all-gather.2

commit v5 on v4

--- a/solution.py
+++ b/solution.py
@@ -1,7 +1,55 @@
+import functools
 import jax
 import jax.numpy as jnp
 from jax import lax
 from jax.sharding import PartitionSpec as P
+from jax.experimental import pallas as pl
+from jax.experimental.pallas import tpu as pltpu
+
+
+def hid_gather_kernel(n, x_ref, out_ref, local_sem, send_sem, recv_sem):
+    me = lax.axis_index("hid")
+    row = lax.axis_index("exp")
+    mesh_ids = pl.DeviceIdType.MESH
+    barrier = pltpu.get_barrier_semaphore()
+    for k in range(1, n):
+        peer = lax.rem(me + k, n)
+        pl.semaphore_signal(barrier, inc=1, device_id=(row, peer), device_id_type=mesh_ids)
+    pl.semaphore_wait(barrier, n - 1)
+    local = pltpu.make_async_copy(x_ref, out_ref.at[me], local_sem)
+    local.start()
+    copies = []
+    for k in range(1, n):
+        peer = lax.rem(me + k, n)
+        copy = pltpu.make_async_remote_copy(
+            src_ref=x_ref,
+            dst_ref=out_ref.at[me],
+            send_sem=send_sem.at[k],
+            recv_sem=recv_sem.at[k],
+            device_id=(row, peer),
+            device_id_type=mesh_ids,
+        )
+        copy.start()
+        copies.append(copy)
+    local.wait()
+    for copy in copies:
+        copy.wait()
+
+
+def hid_gather(block):
+    n = lax.axis_size("hid")
+    return pl.pallas_call(
+        functools.partial(hid_gather_kernel, n),
+        out_shape=jax.ShapeDtypeStruct((n,) + block.shape, block.dtype),
+        in_specs=[pl.BlockSpec(memory_space=pltpu.VMEM)],
+        out_specs=pl.BlockSpec(memory_space=pltpu.VMEM),
+        scratch_shapes=[
+            pltpu.SemaphoreType.DMA,
+            pltpu.SemaphoreType.DMA((n,)),
+            pltpu.SemaphoreType.DMA((n,)),
+        ],
+        compiler_params=pltpu.CompilerParams(collective_id=0, has_side_effects=True),
+    )(block).reshape((n * block.shape[0],) + block.shape[1:])
 
 
 def softmax_rows(values):
@@ -71,7 +119,7 @@
     unit_pick = (expert_ids[:, None] == unit_expert[None, :]).astype(jnp.bfloat16)
     combine = combine_table(router_logits, selected, expert_count)
     packed = jnp.concatenate([tokens, grad_out, combine], axis=1)
-    gathered = lax.all_gather(lax.all_gather(packed, "hid", axis=0, tiled=True), "exp", axis=0, tiled=True)
+    gathered = lax.all_gather(hid_gather(packed), "exp", axis=0, tiled=True)
     combine_all = gathered[:, 2 * model_width :]
     score_part, gate_pre, up_pre, back_grad = dense_terms(
         gathered[:, :model_width], gathered[:, model_width : 2 * model_width], w_gate, w_up, w_down

time: 251 us -> 234 us (0.932)
  blocking collectives: 24.1 us -> 0 us
  Pallas kernels: 0 us -> 11.4 us
  waiting for transfers between devices: 134 us -> 128 us
    all_gather x1 -> x0, blocking collectives: 24.1 us -> none  [on_device(): lax.all_gather(packed, 'hid', axis=0, tiled=True)]
    pallas_call x0 -> x1, Pallas kernels: none -> 11.4 us  [hid_gather(): pl.pallas_call(functools.partial(hid_gather_kernel, n), out_shape=jax.Sha...]
    all_gather x1, waiting for transfers between devices: 85 us -> 78.9 us  [on_device(): gathered = lax.all_gather(hid_gather(packed), 'exp', axis=0, tiled=True)]
where the time goes in v5:
time: 234 us; the launch traced here: 233 us
  waiting for transfers between devices  128 us (55%)
  local copies, waits for them, and re-layouts  24.3 us (10%)
  matrix products  23.5 us (10%)
  starting transfers between devices  23.4 us (10%)
  between operations  14.4 us (6%)
  Pallas kernels  11.4 us (5%)
  other arithmetic  7.68 us (3%)
    all_gather x1, waiting for transfers between devices, on_device(): gathered = lax.all_gather(hid_gather(packed), 'exp', axis=0, tiled=True)  78.9 us
    all_to_all x1, waiting for transfers between devices, on_device(): lax.all_to_all(sent, 'exp', split_axis=0, concat_axis=0, tiled=True)  28.5 us
    all_to_all x1, waiting for transfers between devices, on_device(): lax.all_to_all(jnp.broadcast_to(logit_grad[None], (devices,) + logit_grad...  14.8 us
    pallas_call x1, Pallas kernels, hid_gather(): pl.pallas_call(functools.partial(hid_gather_kernel, n), out_shape=jax.Sha...  11.4 us
    all_to_all x1, starting transfers between devices, on_device(): lax.all_to_all(sent, 'exp', split_axis=0, concat_axis=0, tiled=True)  10.4 us
    all_to_all x1, starting transfers between devices, on_device(): lax.all_to_all(jnp.broadcast_to(logit_grad[None], (devices,) + logit_grad...  8.97 us
    another operation x3, local copies, waits for them, and re-layouts, sparse_terms(): take = lambda a: jnp.take_along_axis(a, rows[:, :, None], axis=1)  6.86 us
    dot_general x1, matrix products, dense_terms(): jnp.einsum('td,ufd->utf', g_rows, w_down, preferred_element_type=jnp.floa...  6.17 us
  transfers between devices with their start and end apart: 4, of which 4 were waited for; matrix products, arithmetic and copies ran while one was open for 1% of the time, Pallas kernels for 0%

profile of v5, /device:TPU:1, one launch (start us, length us, event | category | flops | bytes accessed | tf_op | source)
XLA Modules:
  0.0 232.8 jit_solution(16025426910365338632)
XLA Ops:
  7.3 0.8 bitcast_or_fusion
  8.1 1.4 gather_fusion.1
  9.7 0.1 fusion.62
  9.8 0.2 fusion.47
  10.2 0.6 pad_maximum_fusion.1.x_ref
  10.8 11.4 %shard_map.95 = bf16[8,4,4224]{2,1,0:T(4,128)(2,1)} custom-call(bf16[4,4224]{1,0:T(4,128)(2,1)} %pad_maximum_fusion.1.x_ref), custom_call_target="tpu_custom_call" | custom-call | tf_op jit(solution)/shard_map/pallas_call | solution.py:41
  22.2 1.7 reshape.376
  24.0 78.9 %all-gather.2.cloned.1.call-done = bf16[1024,4224]{1,0:T(8,128)(2,1)} async-done(((bf16[32,4224]{1,0:T(8,128)(2,1)}), bf16[1024,4224]{1,0:T(8,128)(2,1)}) %all-gather.2.cloned.1.call-update) | async-done | bytes 8650768 | tf_op jit(solution)/shard_map/all_gather | solution.py:122
  103.0 1.1 fusion.43
  104.4 0.8 top_k.24
  105.5 0.6 reshape.377
  106.1 1.5 gather_fusion
  107.6 5.3 %fusion.4 = f32[1024,384]{0,1:T(8,128)} fusion(bf16[1024,4224]{1,0:T(8,128)(2,1)} %all-gather.2.cloned.1.call-done, bf16[1,2048,384]{2,1,0:T(8,128)(2,1)S(1)} %copy-done.2), kind=kOutput, calls=%fused_computation.9 | convolution fusion | flops 1610612736 | bytes 7340032 | tf_op jit(solution)/shard_map/td,udf->utf/dot_general | solution.py:81
  112.9 1.9 copy.90
  114.8 5.2 %fusion.2 = f32[1024,384]{0,1:T(8,128)} fusion(bf16[1024,4224]{1,0:T(8,128)(2,1)} %all-gather.2.cloned.1.call-done, bf16[1,2048,384]{2,1,0:T(8,128)(2,1)S(1)} %copy-done), kind=kOutput, calls=%fused_computation.7 | convolution fusion | flops 1610612736 | bytes 7340032 | tf_op jit(solution)/shard_map/td,udf->utf/dot_general | solution.py:80
  119.9 3.1 %copy.91 = f32[1024,384]{1,0:T(8,128)} copy(f32[1024,384]{0,1:T(8,128)} %fusion.2) | data formatting | bytes 3145728 | tf_op jit(solution)/shard_map/jit(take_along_axis)/Arg_0.9 | solution.py:94
  123.1 1.4 gather_fusion.3
  124.5 2.4 %gather_fusion.4 = f32[128,384]{1,0:T(8,128)S(1)} fusion(f32[1024,384]{1,0:T(8,128)} %copy.91, s32[1024]{0:T(1024)S(1)} %pad_clamp_fusion), kind=kCustom, calls=%fused_computation.2.clone | custom fusion | bytes 393728 | tf_op jit(solution)/shard_map/jit(take_along_axis)/gather | solution.py:94
  126.9 6.2 %fusion.7 = (f32[1024]{0:T(1024)S(1)}, f32[1024,384]{0,1:T(8,128)}) fusion(f32[1024,384]{0,1:T(8,128)S(1)} %copy-done.4, f32[1024,384]{0,1:T(8,128)} %fusion.2, bf16[1,384,2048]{2,1,0:T(8,128)(2,1)} %param.17, bf16[1024,4224]{1,0:T(8,128)(2,1)} %all-gather.2.cloned.1.call-done), kind=kOutput, calls=%fused_computation.15 | convolution fusion | flops 1613364224 | bytes 10489856 | tf_op jit(solution)/shard_map/td,ufd->utf/dot_general | solution.py:82
  133.0 0.1 transpose_reshape.7
  133.2 0.6 pad_bitcast_fusion
  133.8 1.9 copy.89
  135.7 0.8 gather_fusion.2
  136.4 0.7 and_select_fusion
  137.1 1.7 fusion.11
  138.9 0.7 convolution_add_fusion
  139.6 1.3 transpose_reshape.6
  140.8 2.6 %pad_maximum_fusion = f32[32,1,4,2176]{3,2,1,0:T(4,128)} fusion(f32[32,1,4,128]{3,2,1,0:T(4,128)S(1)} %copy-done.6, f32[32,1,4,2048]{3,2,1,0:T(4,128)} %bitcast.144), kind=kLoop, calls=%fused_computation.28 | loop fusion | flops 278528 | bytes 2228224 | tf_op jit(solution)/shard_map/concatenate | solution.py:132
  143.4 10.4 %all-to-all-start = ((f32[32,1,4,2176]{3,2,1,0:T(4,128)}), f32[32,1,4,2176]{3,2,1,0:T(4,128)S(1)}, u32[]{:S(2)}, u32[]{:S(2)}) async-start(f32[32,1,4,2176]{3,2,1,0:T(4,128)} %pad_maximum_fusion), calls=%async_computation | async-start | bytes 2228224 | tf_op jit(solution)/shard_map/all_to_all | solution.py:133
  153.8 0.2 fusion.18
  154.1 0.8 top_k.17
  155.1 28.5 %all-to-all-done = f32[32,1,4,2176]{3,2,1,0:T(4,128)S(1)} async-done(((f32[32,1,4,2176]{3,2,1,0:T(4,128)}), f32[32,1,4,2176]{3,2,1,0:T(4,128)S(1)}, u32[]{:S(2)}, u32[]{:S(2)}) %all-to-all-start) | async-done | bytes 1114144 | tf_op jit(solution)/shard_map/all_to_all | solution.py:133
  183.7 1.2 slice.45
  184.9 1.6 reshape.465
  186.5 0.5 fusion.38
  187.0 0.8 copy.96
  187.8 4.0 %all-to-all-start.1 = ((f32[8,4,2176]{2,1,0:T(4,128)}), f32[8,4,2176]{2,1,0:T(4,128)S(1)}, u32[]{:S(2)}, u32[]{:S(2)}) async-start(f32[8,4,2176]{2,1,0:T(4,128)} %copy.96), calls=%async_computation.1 | async-start | bytes 557056 | tf_op jit(solution)/shard_map/all_to_all | solution.py:152
  191.8 0.1 reduce_max.19
  191.9 0.2 fusion.49
  192.1 5.8 %all-to-all-done.1 = f32[8,4,2176]{2,1,0:T(4,128)S(1)} async-done(((f32[8,4,2176]{2,1,0:T(4,128)}), f32[8,4,2176]{2,1,0:T(4,128)S(1)}, u32[]{:S(2)}, u32[]{:S(2)}) %all-to-all-start.1) | async-done | bytes 278560 | tf_op jit(solution)/shard_map/all_to_all | solution.py:152
  197.9 0.1 copy.97
  198.1 0.2 reduce_sum.68
  198.3 0.2 multiply_reduce_fusion
  198.6 0.8 broadcast_in_dim.59
  199.4 9.0 %all-to-all-start.2 = ((bf16[256,4,128]{2,1,0:T(4,128)(2,1)}), bf16[256,4,128]{2,1,0:T(4,128)(2,1)S(1)}, u32[]{:S(2)}, u32[]{:S(2)}) async-start(bf16[256,4,128]{2,1,0:T(4,128)(2,1)} %broadcast_in_dim.59), calls=%async_computation.2 | async-start | bytes 524288 | tf_op jit(solution)/shard_map/all_to_all | solution.py:162
  208.4 0.9 fusion.6
  209.3 14.8 %all-to-all-done.2 = bf16[256,4,128]{2,1,0:T(4,128)(2,1)S(1)} async-done(((bf16[256,4,128]{2,1,0:T(4,128)(2,1)}), bf16[256,4,128]{2,1,0:T(4,128)(2,1)S(1)}, u32[]{:S(2)}, u32[]{:S(2)}) %all-to-all-start.2) | async-done | bytes 262176 | tf_op jit(solution)/shard_map/all_to_all | solution.py:162
  224.1 1.9 fusion.19
  (59 shorter events, 1.6 us)
Async XLA Ops:
  7.2 107.6 %copy-start = (bf16[1,2048,384]{2,1,0:T(8,128)(2,1)S(1)}, bf16[1,2048,384]{2,1,0:T(8,128)(2,1)}, u32[]{:S(2)}) copy-start(bf16[1,2048,384]{2,1,0:T(8,128)(2,1)} %param.15) | copy-start | bytes 4718596
  7.2 2.5 %copy-start.7 = (s32[4,8]{1,0:T(4,128)S(1)}, s32[4,8]{1,0:T(4,128)}, u32[]{:S(2)}) copy-start(s32[4,8]{1,0:T(4,128)} %param.13) | copy-start | bytes 388
  7.2 3.0 %copy-start.8 = (bf16[4,2048]{1,0:T(4,128)(2,1)S(1)}, bf16[4,2048]{1,0:T(4,128)(2,1)}, u32[]{:S(2)}) copy-start(bf16[4,2048]{1,0:T(4,128)(2,1)} %param.11) | copy-start | bytes 49156
  7.2 3.0 %copy-start.9 = (bf16[4,2048]{1,0:T(4,128)(2,1)S(1)}, bf16[4,2048]{1,0:T(4,128)(2,1)}, u32[]{:S(2)}) copy-start(bf16[4,2048]{1,0:T(4,128)(2,1)} %param.10) | copy-start | bytes 49156
  7.2 95.8 %all-gather.2.cloned.1.call-start = ((), (), s32[]{:S(2)}) async-start(), calls=%async_computation.3 | async-start | bytes 8921088 | tf_op jit(solution)/shard_map/all_gather | solution.py:122
  9.6 98.1 %copy-start.2 = (bf16[1,2048,384]{2,1,0:T(8,128)(2,1)S(1)}, bf16[1,2048,384]{2,1,0:T(8,128)(2,1)}, u32[]{:S(2)}) copy-start(bf16[1,2048,384]{2,1,0:T(8,128)(2,1)} %param.16) | copy-start | bytes 4718596
  124.5 2.4 %copy-start.4 = (f32[1024,384]{0,1:T(8,128)S(1)}, f32[1024,384]{0,1:T(8,128)}, u32[]{:S(2)}) copy-start(f32[1024,384]{0,1:T(8,128)} %fusion.4) | copy-start | bytes 4718596
  137.1 1.7 copy-start.3
  139.5 1.3 copy-start.6
  143.4 10.4 %slice-start = ((bf16[1024,4224]{1,0:T(8,128)(2,1)}), bf16[1024,128]{1,0:T(8,128)(2,1)S(1)}, s32[]{:S(2)}) async-start(bf16[1024,4224]{1,0:T(8,128)(2,1)} %all-gather.2.cloned.1.call-done), calls=%async_computation.4 | async-start | bytes 524288 | tf_op jit(solution)/shard_map/slice | solution.py:123
  143.4 40.2 %all-to-all-start = ((f32[32,1,4,2176]{3,2,1,0:T(4,128)}), f32[32,1,4,2176]{3,2,1,0:T(4,128)S(1)}, u32[]{:S(2)}, u32[]{:S(2)}) async-start(f32[32,1,4,2176]{3,2,1,0:T(4,128)} %pad_maximum_fusion), calls=%async_computation | async-start | bytes 2228224 | tf_op jit(solution)/shard_map/all_to_all | solution.py:133
  186.5 5.3 %copy-start.1 = (f32[4,128]{1,0:T(4,128)S(1)}, f32[4,128]{1,0:T(4,128)}, u32[]{:S(2)}) copy-start(f32[4,128]{1,0:T(4,128)} %param.12) | copy-start | bytes 6148
  187.0 21.4 %copy-start.5 = (bf16[2048,128]{1,0:T(8,128)(2,1)S(1)}, bf16[2048,128]{1,0:T(8,128)(2,1)}, u32[]{:S(2)}) copy-start(bf16[2048,128]{1,0:T(8,128)(2,1)} %param.14) | copy-start | bytes 1572868
  187.8 10.1 %all-to-all-start.1 = ((f32[8,4,2176]{2,1,0:T(4,128)}), f32[8,4,2176]{2,1,0:T(4,128)S(1)}, u32[]{:S(2)}, u32[]{:S(2)}) async-start(f32[8,4,2176]{2,1,0:T(4,128)} %copy.96), calls=%async_computation.1 | async-start | bytes 557056 | tf_op jit(solution)/shard_map/all_to_all | solution.py:152
  199.4 24.7 %all-to-all-start.2 = ((bf16[256,4,128]{2,1,0:T(4,128)(2,1)}), bf16[256,4,128]{2,1,0:T(4,128)(2,1)S(1)}, u32[]{:S(2)}, u32[]{:S(2)}) async-start(bf16[256,4,128]{2,1,0:T(4,128)(2,1)} %broadcast_in_dim.59), calls=%async_computation.2 | async-start | bytes 524288 | tf_op jit(solution)/shard_map/all_to_all | solution.py:162
Sparse Core Ops, SparseCore 0:
  24.1 78.8 all-gather.1

commit v6 on v5

--- a/solution.py
+++ b/solution.py
@@ -76,6 +76,19 @@
     return lax.top_k(key, CAP)[1]
 
 
+def split3(value):
+    hi = value.astype(jnp.bfloat16)
+    rest = value - hi.astype(jnp.float32)
+    mid = rest.astype(jnp.bfloat16)
+    lo = (rest - mid.astype(jnp.float32)).astype(jnp.bfloat16)
+    return jnp.concatenate([hi, mid, lo], axis=-1)
+
+
+def join3(pieces, width):
+    part = lambda i: pieces[..., i * width : (i + 1) * width].astype(jnp.float32)
+    return (part(0) + part(1)) + part(2)
+
+
 def dense_terms(x_rows, g_rows, w_gate, w_up, w_down):
     gate_pre = jnp.einsum("td,udf->utf", x_rows, w_gate, preferred_element_type=jnp.float32)
     up_pre = jnp.einsum("td,udf->utf", x_rows, w_up, preferred_element_type=jnp.float32)
@@ -128,8 +141,9 @@
     part = sparse_terms(gate_pre, up_pre, back_grad, column, w_gate, w_up, group_rows)
     lane = 128
     score_grp = jnp.swapaxes(score_part.T.reshape(unit_count, spread_exp, CAP, group_rows // CAP), 0, 1)
-    score_grp = jnp.pad(score_grp, ((0, 0), (0, 0), (0, 0), (0, lane - group_rows // CAP)))
-    sent = jnp.concatenate([jnp.swapaxes(part, 0, 1), score_grp], axis=3)
+    score_grp = split3(score_grp)
+    score_grp = jnp.pad(score_grp, ((0, 0), (0, 0), (0, 0), (0, lane - score_grp.shape[3])))
+    sent = jnp.concatenate([jnp.swapaxes(part, 0, 1).astype(jnp.bfloat16), score_grp], axis=3)
     arrived_part = lax.all_to_all(sent, "exp", split_axis=0, concat_axis=0, tiled=True)
     sender_block = (jnp.arange(spread_exp, dtype=jnp.int32) * spread_hid + own_hid)[:, None]
     sender_expert = (sender_block * unit_count + jnp.arange(unit_count, dtype=jnp.int32)[None, :]) // 2
@@ -137,21 +151,24 @@
     sender_pick = (expert_ids[:, None] == sender_expert.reshape(1, -1)).astype(jnp.bfloat16)
     sender_column = jnp.dot(own_combine, sender_pick, preferred_element_type=jnp.float32).T
     sender_rows = slot_rows(sender_column, group_rows).reshape(-1)
-    place = (sender_rows[:, None] == jnp.arange(group_rows, dtype=jnp.int32)[None, :]).astype(jnp.float32)
+    place = (sender_rows[:, None] == jnp.arange(group_rows, dtype=jnp.int32)[None, :]).astype(jnp.bfloat16)
     group_sum = jnp.einsum(
         "sj,sd->jd", place, arrived_part[..., :model_width].reshape(-1, model_width),
-        precision=lax.Precision.HIGHEST, preferred_element_type=jnp.float32,
-    )
-    got_scores = arrived_part[..., model_width : model_width + group_rows // CAP]
+        preferred_element_type=jnp.float32,
+    )
+    got_scores = join3(arrived_part[..., model_width:], group_rows // CAP)
     got_scores = got_scores.reshape(spread_exp, unit_count, spread_hid, tok_local)
     score_cols = spread_exp * unit_count
-    score_width = -(-score_cols // lane) * lane
     hid_scores = jnp.transpose(got_scores, (2, 3, 0, 1)).reshape(spread_hid, tok_local, score_cols)
-    hid_scores = jnp.pad(hid_scores, ((0, 0), (0, 0), (0, score_width - score_cols)))
-    hid_sent = jnp.concatenate([group_sum.reshape(spread_hid, tok_local, model_width), hid_scores], axis=2)
+    hid_scores = split3(hid_scores)
+    score_width = -(-hid_scores.shape[2] // lane) * lane
+    hid_scores = jnp.pad(hid_scores, ((0, 0), (0, 0), (0, score_width - hid_scores.shape[2])))
+    hid_sent = jnp.concatenate(
+        [group_sum.reshape(spread_hid, tok_local, model_width).astype(jnp.bfloat16), hid_scores], axis=2
+    )
     spread_rows = lax.all_to_all(hid_sent, "hid", split_axis=0, concat_axis=0, tiled=True)
-    input_sum = jnp.sum(spread_rows[..., :model_width], axis=0)
-    own_scores = spread_rows[..., model_width : model_width + score_cols]
+    input_sum = jnp.sum(spread_rows[..., :model_width].astype(jnp.float32), axis=0)
+    own_scores = join3(spread_rows[..., model_width:], score_cols)
     own_scores = own_scores.reshape(spread_hid, tok_local, spread_exp, unit_count)
     unit_scores = jnp.transpose(own_scores, (1, 2, 0, 3)).reshape(tok_local, -1)
     expert_scores = jnp.sum(unit_scores.reshape(tok_local, expert_count, 2), axis=2)

time: 234 us -> 216 us (0.923)
  waiting for transfers between devices: 128 us -> 116 us
  local copies, waits for them, and re-layouts: 24.3 us -> 21.2 us
    all_to_all x1, waiting for transfers between devices: 28.5 us -> 17.4 us  [on_device(): lax.all_to_all(sent, 'exp', split_axis=0, concat_axis=0, tiled=True)]
where the time goes in v6:
time: 216 us; the launch traced here: 215 us
  waiting for transfers between devices  116 us (54%)
  matrix products  23.3 us (11%)
  starting transfers between devices  22.2 us (10%)
  local copies, waits for them, and re-layouts  21.2 us (10%)
  between operations  14.4 us (7%)
  Pallas kernels  11.4 us (5%)
  other arithmetic  6.47 us (3%)
    all_gather x1, waiting for transfers between devices, on_device(): gathered = lax.all_gather(hid_gather(packed), 'exp', axis=0, tiled=True)  78.9 us
    all_to_all x1, waiting for transfers between devices, on_device(): lax.all_to_all(sent, 'exp', split_axis=0, concat_axis=0, tiled=True)  17.4 us
    all_to_all x1, waiting for transfers between devices, on_device(): lax.all_to_all(jnp.broadcast_to(logit_grad[None], (devices,) + logit_grad...  14.8 us
    pallas_call x1, Pallas kernels, hid_gather(): pl.pallas_call(functools.partial(hid_gather_kernel, n), out_shape=jax.Sha...  11.4 us
    all_to_all x1, starting transfers between devices, on_device(): lax.all_to_all(sent, 'exp', split_axis=0, concat_axis=0, tiled=True)  10.2 us
    all_to_all x1, starting transfers between devices, on_device(): lax.all_to_all(jnp.broadcast_to(logit_grad[None], (devices,) + logit_grad...  7.9 us
    another operation x3, local copies, waits for them, and re-layouts, sparse_terms(): take = lambda a: jnp.take_along_axis(a, rows[:, :, None], axis=1)  6.86 us
    dot_general x1, matrix products, dense_terms(): jnp.einsum('td,ufd->utf', g_rows, w_down, preferred_element_type=jnp.floa...  6.17 us
  transfers between devices with their start and end apart: 4, of which 4 were waited for; matrix products, arithmetic and copies ran while one was open for 1% of the time, Pallas kernels for 0%

profile of v6, /device:TPU:1, one launch (start us, length us, event | category | flops | bytes accessed | tf_op | source)
XLA Modules:
  0.0 215.2 jit_solution(5390724259440182955)
XLA Ops:
  7.3 0.8 bitcast_or_fusion
  8.1 1.4 gather_fusion.1
  9.7 0.1 fusion.71
  9.8 0.2 fusion.56
  10.2 0.6 pad_maximum_fusion.1.x_ref
  10.8 11.4 %shard_map.95 = bf16[8,4,4224]{2,1,0:T(4,128)(2,1)} custom-call(bf16[4,4224]{1,0:T(4,128)(2,1)} %pad_maximum_fusion.1.x_ref), custom_call_target="tpu_custom_call" | custom-call | tf_op jit(solution)/shard_map/pallas_call | solution.py:41
  22.2 1.7 reshape.449
  24.0 78.9 %all-gather.2.cloned.1.call-done = bf16[1024,4224]{1,0:T(8,128)(2,1)} async-done(((bf16[32,4224]{1,0:T(8,128)(2,1)}), bf16[1024,4224]{1,0:T(8,128)(2,1)}) %all-gather.2.cloned.1.call-update) | async-done | bytes 8650768 | tf_op jit(solution)/shard_map/all_gather | solution.py:135
  103.0 1.1 fusion.52
  104.4 0.8 top_k.24
  105.5 0.6 reshape.450
  106.1 1.5 gather_fusion
  107.6 5.3 %fusion.4 = f32[1024,384]{0,1:T(8,128)} fusion(bf16[1024,4224]{1,0:T(8,128)(2,1)} %all-gather.2.cloned.1.call-done, bf16[1,2048,384]{2,1,0:T(8,128)(2,1)S(1)} %copy-done.3), kind=kOutput, calls=%fused_computation.9 | convolution fusion | flops 1610612736 | bytes 7340032 | tf_op jit(solution)/shard_map/td,udf->utf/dot_general | solution.py:94
  112.9 1.9 copy.94
  114.8 5.2 %fusion.2 = f32[1024,384]{0,1:T(8,128)} fusion(bf16[1024,4224]{1,0:T(8,128)(2,1)} %all-gather.2.cloned.1.call-done, bf16[1,2048,384]{2,1,0:T(8,128)(2,1)S(1)} %copy-done), kind=kOutput, calls=%fused_computation.7 | convolution fusion | flops 1610612736 | bytes 7340032 | tf_op jit(solution)/shard_map/td,udf->utf/dot_general | solution.py:93
  119.9 3.1 %copy.95 = f32[1024,384]{1,0:T(8,128)} copy(f32[1024,384]{0,1:T(8,128)} %fusion.2) | data formatting | bytes 3145728 | tf_op jit(solution)/shard_map/jit(take_along_axis)/Arg_0.9 | solution.py:107
  123.1 1.4 gather_fusion.3
  124.5 2.4 %gather_fusion.4 = f32[128,384]{1,0:T(8,128)S(1)} fusion(f32[1024,384]{1,0:T(8,128)} %copy.95, s32[1024]{0:T(1024)S(1)} %pad_clamp_fusion), kind=kCustom, calls=%fused_computation.2.clone | custom fusion | bytes 393728 | tf_op jit(solution)/shard_map/jit(take_along_axis)/gather | solution.py:107
  126.9 6.2 %fusion.8 = (f32[1024]{0:T(1024)S(1)}, f32[1024,384]{0,1:T(8,128)}) fusion(f32[1024,384]{0,1:T(8,128)S(1)} %copy-done.2, f32[1024,384]{0,1:T(8,128)} %fusion.2, bf16[1,384,2048]{2,1,0:T(8,128)(2,1)} %param.17, bf16[1024,4224]{1,0:T(8,128)(2,1)} %all-gather.2.cloned.1.call-done), kind=kOutput, calls=%fused_computation.17 | convolution fusion | flops 1613364224 | bytes 10489856 | tf_op jit(solution)/shard_map/td,ufd->utf/dot_general | solution.py:95
  133.1 0.1 transpose_reshape.4
  133.3 0.7 copy.111
  134.0 1.9 copy.93
  135.9 0.8 gather_fusion.2
  136.6 0.7 and_select_fusion
  137.3 1.7 fusion.12
  139.0 0.7 fusion.6
  139.7 0.2 convert_element_type.151
  139.9 1.1 fusion.21
  141.1 10.2 %all-to-all-start = ((bf16[32,1,4,2176]{3,2,1,0:T(4,128)(2,1)}), bf16[32,1,4,2176]{3,2,1,0:T(4,128)(2,1)S(1)}, u32[]{:S(2)}, u32[]{:S(2)}) async-start(bf16[32,1,4,2176]{3,2,1,0:T(4,128)(2,1)} %fusion.21), calls=%async_computation | async-start | bytes 1114112 | tf_op jit(solution)/shard_map/all_to_all | solution.py:147
  151.4 0.2 fusion.20
  151.6 0.8 top_k.17
  152.6 17.4 %all-to-all-done = bf16[32,1,4,2176]{3,2,1,0:T(4,128)(2,1)S(1)} async-done(((bf16[32,1,4,2176]{3,2,1,0:T(4,128)(2,1)}), bf16[32,1,4,2176]{3,2,1,0:T(4,128)(2,1)S(1)}, u32[]{:S(2)}, u32[]{:S(2)}) %all-to-all-start) | async-done | bytes 557088 | tf_op jit(solution)/shard_map/all_to_all | solution.py:147
  170.5 0.3 slice.69
  170.7 0.1 reshape.538
  170.9 0.2 convolution_convert_fusion
  171.2 0.7 copy.104
  171.9 4.0 %all-to-all-start.1 = ((bf16[8,4,2176]{2,1,0:T(4,128)(2,1)}), bf16[8,4,2176]{2,1,0:T(4,128)(2,1)S(1)}, u32[]{:S(2)}, u32[]{:S(2)}) async-start(bf16[8,4,2176]{2,1,0:T(4,128)(2,1)} %copy.104), calls=%async_computation.1 | async-start | bytes 278528 | tf_op jit(solution)/shard_map/all_to_all | solution.py:169
  175.9 0.1 reduce_max.19
  176.0 0.2 fusion.58
  176.2 5.2 %all-to-all-done.1 = bf16[8,4,2176]{2,1,0:T(4,128)(2,1)S(1)} async-done(((bf16[8,4,2176]{2,1,0:T(4,128)(2,1)}), bf16[8,4,2176]{2,1,0:T(4,128)(2,1)S(1)}, u32[]{:S(2)}, u32[]{:S(2)}) %all-to-all-start.1) | async-done | bytes 139296 | tf_op jit(solution)/shard_map/all_to_all | solution.py:169
  181.5 0.1 copy.105
  181.6 0.2 reduce_sum.68
  181.8 0.2 multiply_reduce_fusion
  182.1 0.8 broadcast_in_dim.59
  182.9 7.9 %all-to-all-start.2 = ((bf16[256,4,128]{2,1,0:T(4,128)(2,1)}), bf16[256,4,128]{2,1,0:T(4,128)(2,1)S(1)}, u32[]{:S(2)}, u32[]{:S(2)}) async-start(bf16[256,4,128]{2,1,0:T(4,128)(2,1)} %broadcast_in_dim.59), calls=%async_computation.2 | async-start | bytes 524288 | tf_op jit(solution)/shard_map/all_to_all | solution.py:179
  190.9 0.9 fusion.7
  191.7 14.8 %all-to-all-done.2 = bf16[256,4,128]{2,1,0:T(4,128)(2,1)S(1)} async-done(((bf16[256,4,128]{2,1,0:T(4,128)(2,1)}), bf16[256,4,128]{2,1,0:T(4,128)(2,1)S(1)}, u32[]{:S(2)}, u32[]{:S(2)}) %all-to-all-start.2) | async-done | bytes 262176 | tf_op jit(solution)/shard_map/all_to_all | solution.py:179
  206.5 1.9 fusion.22
  (67 shorter events, 2.2 us)
Async XLA Ops:
  7.2 107.6 %copy-start = (bf16[1,2048,384]{2,1,0:T(8,128)(2,1)S(1)}, bf16[1,2048,384]{2,1,0:T(8,128)(2,1)}, u32[]{:S(2)}) copy-start(bf16[1,2048,384]{2,1,0:T(8,128)(2,1)} %param.15) | copy-start | bytes 4718596
  7.2 2.5 %copy-start.7 = (s32[4,8]{1,0:T(4,128)S(1)}, s32[4,8]{1,0:T(4,128)}, u32[]{:S(2)}) copy-start(s32[4,8]{1,0:T(4,128)} %param.13) | copy-start | bytes 388
  7.2 3.0 %copy-start.8 = (bf16[4,2048]{1,0:T(4,128)(2,1)S(1)}, bf16[4,2048]{1,0:T(4,128)(2,1)}, u32[]{:S(2)}) copy-start(bf16[4,2048]{1,0:T(4,128)(2,1)} %param.11) | copy-start | bytes 49156
  7.2 3.0 %copy-start.9 = (bf16[4,2048]{1,0:T(4,128)(2,1)S(1)}, bf16[4,2048]{1,0:T(4,128)(2,1)}, u32[]{:S(2)}) copy-start(bf16[4,2048]{1,0:T(4,128)(2,1)} %param.10) | copy-start | bytes 49156
  7.2 95.8 %all-gather.2.cloned.1.call-start = ((), (), s32[]{:S(2)}) async-start(), calls=%async_computation.3 | async-start | bytes 8921088 | tf_op jit(solution)/shard_map/all_gather | solution.py:135
  9.6 98.1 %copy-start.3 = (bf16[1,2048,384]{2,1,0:T(8,128)(2,1)S(1)}, bf16[1,2048,384]{2,1,0:T(8,128)(2,1)}, u32[]{:S(2)}) copy-start(bf16[1,2048,384]{2,1,0:T(8,128)(2,1)} %param.16) | copy-start | bytes 4718596
  124.5 2.4 %copy-start.2 = (f32[1024,384]{0,1:T(8,128)S(1)}, f32[1024,384]{0,1:T(8,128)}, u32[]{:S(2)}) copy-start(f32[1024,384]{0,1:T(8,128)} %fusion.4) | copy-start | bytes 4718596
  137.3 1.7 copy-start.4
  139.0 0.9 copy-start.6
  139.9 11.4 %slice-start = ((bf16[1024,4224]{1,0:T(8,128)(2,1)}), bf16[1024,128]{1,0:T(8,128)(2,1)S(1)}, s32[]{:S(2)}) async-start(bf16[1024,4224]{1,0:T(8,128)(2,1)} %all-gather.2.cloned.1.call-done), calls=%async_computation.4 | async-start | bytes 524288 | tf_op jit(solution)/shard_map/slice | solution.py:136
  141.1 29.0 %all-to-all-start = ((bf16[32,1,4,2176]{3,2,1,0:T(4,128)(2,1)}), bf16[32,1,4,2176]{3,2,1,0:T(4,128)(2,1)S(1)}, u32[]{:S(2)}, u32[]{:S(2)}) async-start(bf16[32,1,4,2176]{3,2,1,0:T(4,128)(2,1)} %fusion.21), calls=%async_computation | async-start | bytes 1114112 | tf_op jit(solution)/shard_map/all_to_all | solution.py:147
  170.4 5.5 %copy-start.1 = (f32[4,128]{1,0:T(4,128)S(1)}, f32[4,128]{1,0:T(4,128)}, u32[]{:S(2)}) copy-start(f32[4,128]{1,0:T(4,128)} %param.12) | copy-start | bytes 6148
  170.9 20.0 %copy-start.5 = (bf16[2048,128]{1,0:T(8,128)(2,1)S(1)}, bf16[2048,128]{1,0:T(8,128)(2,1)}, u32[]{:S(2)}) copy-start(bf16[2048,128]{1,0:T(8,128)(2,1)} %param.14) | copy-start | bytes 1572868
  171.9 9.5 %all-to-all-start.1 = ((bf16[8,4,2176]{2,1,0:T(4,128)(2,1)}), bf16[8,4,2176]{2,1,0:T(4,128)(2,1)S(1)}, u32[]{:S(2)}, u32[]{:S(2)}) async-start(bf16[8,4,2176]{2,1,0:T(4,128)(2,1)} %copy.104), calls=%async_computation.1 | async-start | bytes 278528 | tf_op jit(solution)/shard_map/all_to_all | solution.py:169
  182.9 23.6 %all-to-all-start.2 = ((bf16[256,4,128]{2,1,0:T(4,128)(2,1)}), bf16[256,4,128]{2,1,0:T(4,128)(2,1)S(1)}, u32[]{:S(2)}, u32[]{:S(2)}) async-start(bf16[256,4,128]{2,1,0:T(4,128)(2,1)} %broadcast_in_dim.59), calls=%async_computation.2 | async-start | bytes 524288 | tf_op jit(solution)/shard_map/all_to_all | solution.py:179
Sparse Core Ops, SparseCore 0:
  24.1 78.8 all-gather.1

commit v7 on v6

--- a/solution.py
+++ b/solution.py
@@ -131,12 +131,14 @@
     expert_ids = jnp.arange(expert_count, dtype=jnp.int32)
     unit_pick = (expert_ids[:, None] == unit_expert[None, :]).astype(jnp.bfloat16)
     combine = combine_table(router_logits, selected, expert_count)
-    packed = jnp.concatenate([tokens, grad_out, combine], axis=1)
-    gathered = lax.all_gather(hid_gather(packed), "exp", axis=0, tiled=True)
-    combine_all = gathered[:, 2 * model_width :]
-    score_part, gate_pre, up_pre, back_grad = dense_terms(
-        gathered[:, :model_width], gathered[:, model_width : 2 * model_width], w_gate, w_up, w_down
-    )
+    packed = jnp.concatenate([tokens, combine, grad_out], axis=1)
+    near = hid_gather(packed)
+    split_at = model_width + expert_count
+    front = lax.all_gather(near[:, :split_at], "exp", axis=0, tiled=True)
+    back = lax.all_gather(near[:, split_at:], "exp", axis=0, tiled=True)
+    tokens_all = front[:, :model_width]
+    combine_all = front[:, model_width:]
+    score_part, gate_pre, up_pre, back_grad = dense_terms(tokens_all, back, w_gate, w_up, w_down)
     column = jnp.dot(combine_all, unit_pick, preferred_element_type=jnp.float32).T
     part = sparse_terms(gate_pre, up_pre, back_grad, column, w_gate, w_up, group_rows)
     lane = 128
@@ -180,7 +182,7 @@
         jnp.broadcast_to(logit_grad[None], (devices,) + logit_grad.shape), ("exp", "hid"), 0, 0, tiled=True
     ).reshape(-1, expert_count)
     grad_rows = model_width // devices
-    token_cols = lax.dynamic_slice_in_dim(gathered, own_block * grad_rows, grad_rows, 1)
+    token_cols = lax.dynamic_slice_in_dim(tokens_all, own_block * grad_rows, grad_rows, 1)
     router_grad = jnp.einsum("tc,te->ce", token_cols, logit_all, preferred_element_type=jnp.float32)
     router_part = jnp.einsum("te,de->td", logit_grad, router_w, preferred_element_type=jnp.float32)
     x_grad = (input_sum + router_part).astype(jnp.bfloat16)

time: 216 us -> 240 us (1.11)
  waiting for transfers between devices: 116 us -> 138 us
  local copies, waits for them, and re-layouts: 21.2 us -> 26.5 us
  starting transfers between devices: 22.2 us -> 18.6 us
    all_gather x1 -> x2, waiting for transfers between devices: 78.9 us -> 105 us  [the longest x1 63.6 us: on_device(): front = lax.all_gather(near[:, :split_at], 'exp', axis=0, tiled=True)]
    slice x2 -> x5, local copies, waits for them, and re-layouts: 0.01 us -> 6.12 us  [the longest x1 4.8 us: on_device(): tokens_all = front[:, :model_width]]
    all_to_all x1, waiting for transfers between devices: 14.8 us -> 10.1 us  [on_device(): lax.all_to_all(jnp.broadcast_to(logit_grad[None], (devices,) + logit_grad...]
    all_to_all x1, starting transfers between devices: 10.2 us -> 6.08 us  [on_device(): lax.all_to_all(sent, 'exp', split_axis=0, concat_axis=0, tiled=True)]
  transfers between devices with their start and end apart: 4 -> 5, of which waited for: 4 -> 5; matrix products, arithmetic and copies ran while one was open for 1% -> 11% of each run, Pallas kernels for 0% -> 0%
where the time goes in v7:
time: 240 us
  waiting for transfers between devices  138 us (58%)
  local copies, waits for them, and re-layouts  26.5 us (11%)
  matrix products  23.9 us (10%)
  starting transfers between devices  18.6 us (8%)
  between operations  14.5 us (6%)
  Pallas kernels  11.4 us (5%)
  other arithmetic  7.02 us (3%)
    all_gather x1, waiting for transfers between devices, on_device(): front = lax.all_gather(near[:, :split_at], 'exp', axis=0, tiled=True)  63.6 us
    all_gather x1, waiting for transfers between devices, on_device(): back = lax.all_gather(near[:, split_at:], 'exp', axis=0, tiled=True)  41.2 us
    all_to_all x1, waiting for transfers between devices, on_device(): lax.all_to_all(sent, 'exp', split_axis=0, concat_axis=0, tiled=True)  17.4 us
    pallas_call x1, Pallas kernels, hid_gather(): pl.pallas_call(functools.partial(hid_gather_kernel, n), out_shape=jax.Sha...  11.4 us
    all_to_all x1, waiting for transfers between devices, on_device(): lax.all_to_all(jnp.broadcast_to(logit_grad[None], (devices,) + logit_grad...  10.1 us
    another operation x3, local copies, waits for them, and re-layouts, sparse_terms(): take = lambda a: jnp.take_along_axis(a, rows[:, :, None], axis=1)  6.84 us
    dot_general x1, matrix products, dense_terms(): jnp.einsum('td,ufd->utf', g_rows, w_down, preferred_element_type=jnp.floa...  6.67 us
    all_to_all x1, starting transfers between devices, on_device(): lax.all_to_all(jnp.broadcast_to(logit_grad[None], (devices,) + logit_grad...  6.63 us
  transfers between devices with their start and end apart: 5, of which 5 were waited for; matrix products, arithmetic and copies ran while one was open for 11% of the time, Pallas kernels for 0%

profile of v7, /device:TPU:1, one launch (start us, length us, event | category | flops | bytes accessed | tf_op | source)
XLA Modules:
  0.0 239.5 jit_solution(17859942790782460952)
XLA Ops:
  7.3 0.8 bitcast_or_fusion
  8.1 1.4 gather_fusion.1
  9.8 0.2 fusion.53
  10.2 0.6 pad_maximum_fusion.1.x_ref
  10.8 11.4 %shard_map.95 = bf16[8,4,4224]{2,1,0:T(4,128)(2,1)} custom-call(bf16[4,4224]{1,0:T(4,128)(2,1)} %pad_maximum_fusion.1.x_ref), custom_call_target="tpu_custom_call" | custom-call | tf_op jit(solution)/shard_map/pallas_call | solution.py:41
  22.2 1.0 reshape.449
  23.3 0.7 slice.70
  24.0 0.7 slice.72
  24.7 63.6 %all-gather.3.cloned.1.call-done = bf16[1024,2176]{1,0:T(8,128)(2,1)} async-done(((bf16[32,2176]{1,0:T(8,128)(2,1)}), bf16[1024,2176]{1,0:T(8,128)(2,1)}) %all-gather.3.cloned.1.call-update) | async-done | bytes 4456464 | tf_op jit(solution)/shard_map/all_gather | solution.py:137
  88.4 1.1 fusion.49
  89.8 0.8 top_k.24
  90.8 0.6 reshape.451
  91.4 0.6 reshape.450
  92.0 5.3 %fusion.11 = f32[1024,384]{0,1:T(8,128)} fusion(bf16[1,2048,384]{2,1,0:T(8,128)(2,1)S(1)} %copy-done.2, bf16[1024,2176]{1,0:T(8,128)(2,1)} %all-gather.3.cloned.1.call-done), kind=kOutput, calls=%fused_computation.23 | convolution fusion | flops 1610612736 | bytes 7340032 | tf_op jit(solution)/shard_map/td,udf->utf/dot_general | solution.py:94
  97.3 1.9 copy.94
  99.2 5.3 %fusion.8 = f32[1024,384]{0,1:T(8,128)} fusion(bf16[1,2048,384]{2,1,0:T(8,128)(2,1)S(1)} %copy-done, bf16[1024,2176]{1,0:T(8,128)(2,1)} %all-gather.3.cloned.1.call-done), kind=kOutput, calls=%fused_computation.20 | convolution fusion | flops 1610612736 | bytes 7340032 | tf_op jit(solution)/shard_map/td,udf->utf/dot_general | solution.py:93
  104.5 3.1 %copy.95 = f32[1024,384]{1,0:T(8,128)} copy(f32[1024,384]{0,1:T(8,128)} %fusion.8) | data formatting | bytes 3145728 | tf_op jit(solution)/shard_map/jit(take_along_axis)/Arg_0.9 | solution.py:107
  107.6 41.2 %all-gather.5.cloned.1.call-done = bf16[1024,2048]{1,0:T(8,128)(2,1)} async-done(((bf16[32,2048]{1,0:T(8,128)(2,1)}), bf16[1024,2048]{1,0:T(8,128)(2,1)}) %all-gather.5.cloned.1.call-update) | async-done | bytes 4194320 | tf_op jit(solution)/shard_map/all_gather | solution.py:138
  148.8 6.7 %fusion.2 = (f32[1024]{0:T(1024)S(1)}, f32[1024,384]{0,1:T(8,128)}) fusion(f32[1024,384]{0,1:T(8,128)} %fusion.11, f32[1024,384]{0,1:T(8,128)} %fusion.8, bf16[1024,2048]{1,0:T(8,128)(2,1)} %all-gather.5.cloned.1.call-done, bf16[1,384,2048]{2,1,0:T(8,128)(2,1)} %param.17), kind=kOutput, calls=%fused_computation.11 | convolution fusion | flops 1613364224 | bytes 10489856 | tf_op jit(solution)/shard_map/td,ufd->utf/dot_general | solution.py:95
  155.7 0.7 copy.111
  156.4 1.4 gather_fusion.3
  157.9 2.2 gather_fusion.4
  160.1 1.9 copy.93
  162.0 0.8 gather_fusion.2
  162.8 0.7 fusion.56
  163.4 1.0 gather_fusion
  164.4 0.6 and_select_fusion
  165.0 1.7 fusion.6
  166.8 0.7 fusion
  167.5 0.2 convert_element_type.151
  167.7 1.1 fusion.18
  168.8 6.1 %all-to-all-start = ((bf16[32,1,4,2176]{3,2,1,0:T(4,128)(2,1)}), bf16[32,1,4,2176]{3,2,1,0:T(4,128)(2,1)S(1)}, u32[]{:S(2)}, u32[]{:S(2)}) async-start(bf16[32,1,4,2176]{3,2,1,0:T(4,128)(2,1)} %fusion.18), calls=%async_computation | async-start | bytes 1114112 | tf_op jit(solution)/shard_map/all_to_all | solution.py:149
  174.9 0.2 fusion.17
  175.2 0.8 top_k.17
  176.2 17.4 %all-to-all-done = bf16[32,1,4,2176]{3,2,1,0:T(4,128)(2,1)S(1)} async-done(((bf16[32,1,4,2176]{3,2,1,0:T(4,128)(2,1)}), bf16[32,1,4,2176]{3,2,1,0:T(4,128)(2,1)S(1)}, u32[]{:S(2)}, u32[]{:S(2)}) %all-to-all-start) | async-done | bytes 557088 | tf_op jit(solution)/shard_map/all_to_all | solution.py:149
  194.0 0.3 slice.74
  194.5 0.2 convolution_convert_fusion
  194.8 0.7 copy.104
  195.5 5.8 %all-to-all-start.1 = ((bf16[8,4,2176]{2,1,0:T(4,128)(2,1)}), bf16[8,4,2176]{2,1,0:T(4,128)(2,1)S(1)}, u32[]{:S(2)}, u32[]{:S(2)}) async-start(bf16[8,4,2176]{2,1,0:T(4,128)(2,1)} %copy.104), calls=%async_computation.1 | async-start | bytes 278528 | tf_op jit(solution)/shard_map/all_to_all | solution.py:171
  201.3 0.2 fusion.55
  201.5 5.3 %all-to-all-done.1 = bf16[8,4,2176]{2,1,0:T(4,128)(2,1)S(1)} async-done(((bf16[8,4,2176]{2,1,0:T(4,128)(2,1)}), bf16[8,4,2176]{2,1,0:T(4,128)(2,1)S(1)}, u32[]{:S(2)}, u32[]{:S(2)}) %all-to-all-start.1) | async-done | bytes 139296 | tf_op jit(solution)/shard_map/all_to_all | solution.py:171
  207.3 0.2 multiply_reduce_fusion
  207.5 0.8 broadcast_in_dim.59
  208.3 6.6 %all-to-all-start.2 = ((bf16[256,4,128]{2,1,0:T(4,128)(2,1)}), bf16[256,4,128]{2,1,0:T(4,128)(2,1)S(1)}, u32[]{:S(2)}, u32[]{:S(2)}) async-start(bf16[256,4,128]{2,1,0:T(4,128)(2,1)} %broadcast_in_dim.59), calls=%async_computation.2 | async-start | bytes 524288 | tf_op jit(solution)/shard_map/all_to_all | solution.py:181
  215.0 4.8 %slice.73 = bf16[1024,2048]{1,0:T(8,128)(2,1)} slice(bf16[1024,2176]{1,0:T(8,128)(2,1)} %all-gather.3.cloned.1.call-done), slice={[0:1024], [0:2048]} | slice | bytes 8388608 | tf_op jit(solution)/shard_map/slice | solution.py:139
  219.9 0.9 fusion.1
  220.7 10.1 %all-to-all-done.2 = bf16[256,4,128]{2,1,0:T(4,128)(2,1)S(1)} async-done(((bf16[256,4,128]{2,1,0:T(4,128)(2,1)}), bf16[256,4,128]{2,1,0:T(4,128)(2,1)S(1)}, u32[]{:S(2)}, u32[]{:S(2)}) %all-to-all-start.2) | async-done | bytes 262176 | tf_op jit(solution)/shard_map/all_to_all | solution.py:181
  230.8 1.9 fusion.19
  (75 shorter events, 3.0 us)
Async XLA Ops:
  7.2 92.0 %copy-start = (bf16[1,2048,384]{2,1,0:T(8,128)(2,1)S(1)}, bf16[1,2048,384]{2,1,0:T(8,128)(2,1)}, u32[]{:S(2)}) copy-start(bf16[1,2048,384]{2,1,0:T(8,128)(2,1)} %param.15) | copy-start | bytes 4718596
  7.2 2.5 %copy-start.6 = (s32[4,8]{1,0:T(4,128)S(1)}, s32[4,8]{1,0:T(4,128)}, u32[]{:S(2)}) copy-start(s32[4,8]{1,0:T(4,128)} %param.13) | copy-start | bytes 388
  7.2 3.0 %copy-start.7 = (bf16[4,2048]{1,0:T(4,128)(2,1)S(1)}, bf16[4,2048]{1,0:T(4,128)(2,1)}, u32[]{:S(2)}) copy-start(bf16[4,2048]{1,0:T(4,128)(2,1)} %param.11) | copy-start | bytes 49156
  7.2 3.0 %copy-start.8 = (bf16[4,2048]{1,0:T(4,128)(2,1)S(1)}, bf16[4,2048]{1,0:T(4,128)(2,1)}, u32[]{:S(2)}) copy-start(bf16[4,2048]{1,0:T(4,128)(2,1)} %param.10) | copy-start | bytes 49156
  7.2 81.2 %all-gather.3.cloned.1.call-start = ((), (), s32[]{:S(2)}) async-start(), calls=%async_computation.3 | async-start | bytes 4595712 | tf_op jit(solution)/shard_map/all_gather | solution.py:137
  9.6 82.5 %copy-start.2 = (bf16[1,2048,384]{2,1,0:T(8,128)(2,1)S(1)}, bf16[1,2048,384]{2,1,0:T(8,128)(2,1)}, u32[]{:S(2)}) copy-start(bf16[1,2048,384]{2,1,0:T(8,128)(2,1)} %param.16) | copy-start | bytes 4718596
  23.9 124.9 %all-gather.5.cloned.1.call-start = ((), (), s32[]{:S(2)}) async-start(), calls=%async_computation.4 | async-start | bytes 4325376 | tf_op jit(solution)/shard_map/all_gather | solution.py:138
  24.7 65.0 %copy-start.9 = (s32[32]{0:T(128)}, s32[32]{0:T(128)S(1)}, u32[]{:S(2)}) copy-start(s32[32]{0:T(128)S(1)} %get-tuple-element.26) | copy-start | bytes 388
  165.0 1.7 copy-start.3
  166.8 0.9 copy-start.5
  167.7 7.2 %slice-start = ((bf16[1024,2176]{1,0:T(8,128)(2,1)}), bf16[1024,128]{1,0:T(8,128)(2,1)S(1)}, s32[]{:S(2)}) async-start(bf16[1024,2176]{1,0:T(8,128)(2,1)} %all-gather.3.cloned.1.call-done), calls=%async_computation.5 | async-start | bytes 524288 | tf_op jit(solution)/shard_map/slice | solution.py:140
  167.7 7.2 %copy-start.10 = (s32[32]{0:T(128)S(1)}, s32[32]{0:T(128)}, u32[]{:S(2)}) copy-start(s32[32]{0:T(128)} %copy-done.9) | copy-start | bytes 388
  168.8 24.8 %all-to-all-start = ((bf16[32,1,4,2176]{3,2,1,0:T(4,128)(2,1)}), bf16[32,1,4,2176]{3,2,1,0:T(4,128)(2,1)S(1)}, u32[]{:S(2)}, u32[]{:S(2)}) async-start(bf16[32,1,4,2176]{3,2,1,0:T(4,128)(2,1)} %fusion.18), calls=%async_computation | async-start | bytes 1114112 | tf_op jit(solution)/shard_map/all_to_all | solution.py:149
  194.0 7.2 %copy-start.1 = (f32[4,128]{1,0:T(4,128)S(1)}, f32[4,128]{1,0:T(4,128)}, u32[]{:S(2)}) copy-start(f32[4,128]{1,0:T(4,128)} %param.12) | copy-start | bytes 6148
  195.5 11.3 %all-to-all-start.1 = ((bf16[8,4,2176]{2,1,0:T(4,128)(2,1)}), bf16[8,4,2176]{2,1,0:T(4,128)(2,1)S(1)}, u32[]{:S(2)}, u32[]{:S(2)}) async-start(bf16[8,4,2176]{2,1,0:T(4,128)(2,1)} %copy.104), calls=%async_computation.1 | async-start | bytes 278528 | tf_op jit(solution)/shard_map/all_to_all | solution.py:171
  208.3 22.5 %all-to-all-start.2 = ((bf16[256,4,128]{2,1,0:T(4,128)(2,1)}), bf16[256,4,128]{2,1,0:T(4,128)(2,1)S(1)}, u32[]{:S(2)}, u32[]{:S(2)}) async-start(bf16[256,4,128]{2,1,0:T(4,128)(2,1)} %broadcast_in_dim.59), calls=%async_computation.2 | async-start | bytes 524288 | tf_op jit(solution)/shard_map/all_to_all | solution.py:181
  215.0 4.9 %copy-start.4 = (bf16[2048,128]{1,0:T(8,128)(2,1)S(1)}, bf16[2048,128]{1,0:T(8,128)(2,1)}, u32[]{:S(2)}) copy-start(bf16[2048,128]{1,0:T(8,128)(2,1)} %param.14) | copy-start | bytes 1572868
Sparse Core Ops, SparseCore 0:
  24.1 64.2 all-gather.2
  90.9 57.8 all-gather.4

commit v8 on v6

--- a/solution.py
+++ b/solution.py
@@ -34,6 +34,53 @@
     local.wait()
     for copy in copies:
         copy.wait()
+
+
+def exchange_kernel(axis, n, x_ref, out_ref, local_sem, send_sem, recv_sem):
+    me = lax.axis_index(axis)
+    own_exp = lax.axis_index("exp")
+    own_hid = lax.axis_index("hid")
+    mesh_ids = pl.DeviceIdType.MESH
+    where = lambda peer: (peer, own_hid) if axis == "exp" else (own_exp, peer)
+    barrier = pltpu.get_barrier_semaphore()
+    for k in range(1, n):
+        peer = lax.rem(me + k, n)
+        pl.semaphore_signal(barrier, inc=1, device_id=where(peer), device_id_type=mesh_ids)
+    pl.semaphore_wait(barrier, n - 1)
+    local = pltpu.make_async_copy(x_ref.at[me], out_ref.at[me], local_sem)
+    local.start()
+    copies = []
+    for k in range(1, n):
+        peer = lax.rem(me + k, n)
+        copy = pltpu.make_async_remote_copy(
+            src_ref=x_ref.at[peer],
+            dst_ref=out_ref.at[me],
+            send_sem=send_sem.at[k],
+            recv_sem=recv_sem.at[k],
+            device_id=where(peer),
+            device_id_type=mesh_ids,
+        )
+        copy.start()
+        copies.append(copy)
+    local.wait()
+    for copy in copies:
+        copy.wait()
+
+
+def exchange(chunks, axis, kernel_id):
+    n = chunks.shape[0]
+    return pl.pallas_call(
+        functools.partial(exchange_kernel, axis, n),
+        out_shape=jax.ShapeDtypeStruct(chunks.shape, chunks.dtype),
+        in_specs=[pl.BlockSpec(memory_space=pltpu.VMEM)],
+        out_specs=pl.BlockSpec(memory_space=pltpu.VMEM),
+        scratch_shapes=[
+            pltpu.SemaphoreType.DMA,
+            pltpu.SemaphoreType.DMA((n,)),
+            pltpu.SemaphoreType.DMA((n,)),
+        ],
+        compiler_params=pltpu.CompilerParams(collective_id=kernel_id, has_side_effects=True),
+    )(chunks)
 
 
 def hid_gather(block):
@@ -144,7 +191,7 @@
     score_grp = split3(score_grp)
     score_grp = jnp.pad(score_grp, ((0, 0), (0, 0), (0, 0), (0, lane - score_grp.shape[3])))
     sent = jnp.concatenate([jnp.swapaxes(part, 0, 1).astype(jnp.bfloat16), score_grp], axis=3)
-    arrived_part = lax.all_to_all(sent, "exp", split_axis=0, concat_axis=0, tiled=True)
+    arrived_part = exchange(sent, "exp", 1)
     sender_block = (jnp.arange(spread_exp, dtype=jnp.int32) * spread_hid + own_hid)[:, None]
     sender_expert = (sender_block * unit_count + jnp.arange(unit_count, dtype=jnp.int32)[None, :]) // 2
     own_combine = lax.dynamic_slice_in_dim(combine_all, own_exp * group_rows, group_rows, 0)
@@ -166,7 +213,7 @@
     hid_sent = jnp.concatenate(
         [group_sum.reshape(spread_hid, tok_local, model_width).astype(jnp.bfloat16), hid_scores], axis=2
     )
-    spread_rows = lax.all_to_all(hid_sent, "hid", split_axis=0, concat_axis=0, tiled=True)
+    spread_rows = exchange(hid_sent, "hid", 2)
     input_sum = jnp.sum(spread_rows[..., :model_width].astype(jnp.float32), axis=0)
     own_scores = join3(spread_rows[..., model_width:], score_cols)
     own_scores = own_scores.reshape(spread_hid, tok_local, spread_exp, unit_count)

time: 216 us -> 217 us (level)
  Pallas kernels: 11.4 us -> 45.5 us
  waiting for transfers between devices: 116 us -> 91.4 us
  starting transfers between devices: 22.2 us -> 10.1 us
  other arithmetic: 6.47 us -> 12.2 us
    pallas_call x0 -> x2, Pallas kernels: none -> 34.1 us  [exchange(): pl.pallas_call(functools.partial(exchange_kernel, axis, n), out_shape=jax...]
    all_to_all x2 -> x0, waiting for transfers between devices: 22.6 us -> none  [the longest x1 17.4 us: on_device(): lax.all_to_all(sent, 'exp', split_axis=0, concat_axis=0, tiled=True)]
    all_to_all x2 -> x0, starting transfers between devices: 14.2 us -> none  [the longest x1 10.2 us: on_device(): lax.all_to_all(sent, 'exp', split_axis=0, concat_axis=0, tiled=True)]
  transfers between devices with their start and end apart: 4 -> 2, of which waited for: 4 -> 2; matrix products, arithmetic and copies ran while one was open for 1% -> 1% of each run, Pallas kernels for 0% -> 0%
where the time goes in v8:
time: 217 us; the launch traced here: 216 us
  waiting for transfers between devices  91.4 us (42%)
  Pallas kernels  45.5 us (21%)
  matrix products  23.3 us (11%)
  local copies, waits for them, and re-layouts  19.4 us (9%)
  between operations  14.5 us (7%)
  other arithmetic  12.2 us (6%)
  starting transfers between devices  10.1 us (5%)
    all_gather x1, waiting for transfers between devices, on_device(): gathered = lax.all_gather(hid_gather(packed), 'exp', axis=0, tiled=True)  77.6 us
    pallas_call x2, Pallas kernels, exchange(): pl.pallas_call(functools.partial(exchange_kernel, axis, n), out_shape=jax...  34.1 us
    all_to_all x1, waiting for transfers between devices, on_device(): lax.all_to_all(jnp.broadcast_to(logit_grad[None], (devices,) + logit_grad...  13.9 us
    pallas_call x1, Pallas kernels, hid_gather(): pl.pallas_call(functools.partial(hid_gather_kernel, n), out_shape=jax.Sha...  11.4 us
    all_to_all x1, starting transfers between devices, on_device(): lax.all_to_all(jnp.broadcast_to(logit_grad[None], (devices,) + logit_grad...  10 us
    another operation x3, local copies, waits for them, and re-layouts, sparse_terms(): take = lambda a: jnp.take_along_axis(a, rows[:, :, None], axis=1)  6.86 us
    dot_general x1, matrix products, dense_terms(): jnp.einsum('td,ufd->utf', g_rows, w_down, preferred_element_type=jnp.floa...  6.22 us
    dot_general x1, matrix products, dense_terms(): jnp.einsum('td,udf->utf', x_rows, w_up, preferred_element_type=jnp.float32)  5.26 us
  transfers between devices with their start and end apart: 2, of which 2 were waited for; matrix products, arithmetic and copies ran while one was open for 1% of the time, Pallas kernels for 0%

profile of v8, /device:TPU:1, one launch (start us, length us, event | category | flops | bytes accessed | tf_op | source)
XLA Modules:
  0.0 216.5 jit_solution(4597890566292579243)
XLA Ops:
  7.3 0.8 bitcast_or_fusion
  8.1 1.5 gather_fusion.1
  9.9 0.2 fusion.57
  10.2 0.6 pad_maximum_fusion.2.x_ref
  10.9 11.4 %shard_map.95 = bf16[8,4,4224]{2,1,0:T(4,128)(2,1)} custom-call(bf16[4,4224]{1,0:T(4,128)(2,1)} %pad_maximum_fusion.2.x_ref), custom_call_target="tpu_custom_call" | custom-call | tf_op jit(solution)/shard_map/pallas_call | solution.py:88
  22.3 1.7 reshape.449
  24.1 0.1 reduce_max.19
  24.2 0.5 and_select_fusion.2
  24.8 0.7 fusion.59
  25.5 77.6 %all-gather.2.cloned.1.call-done = bf16[1024,4224]{1,0:T(8,128)(2,1)} async-done(((bf16[32,4224]{1,0:T(8,128)(2,1)}), bf16[1024,4224]{1,0:T(8,128)(2,1)}) %all-gather.2.cloned.1.call-update) | async-done | bytes 8650768 | tf_op jit(solution)/shard_map/all_gather | solution.py:182
  103.0 1.1 fusion.53
  104.5 0.8 top_k.24
  105.5 0.5 and_bitcast_fusion
  106.1 0.6 reshape.450
  106.7 1.5 gather_fusion
  108.2 5.3 %fusion.4 = f32[1024,384]{0,1:T(8,128)} fusion(bf16[1024,4224]{1,0:T(8,128)(2,1)} %all-gather.2.cloned.1.call-done, bf16[1,2048,384]{2,1,0:T(8,128)(2,1)S(1)} %copy-done.3), kind=kOutput, calls=%fused_computation.9 | convolution fusion | flops 1610612736 | bytes 7340032 | tf_op jit(solution)/shard_map/td,udf->utf/dot_general | solution.py:141
  113.5 1.9 copy.89
  115.3 5.2 %fusion.2 = f32[1024,384]{0,1:T(8,128)} fusion(bf16[1024,4224]{1,0:T(8,128)(2,1)} %all-gather.2.cloned.1.call-done, bf16[1,2048,384]{2,1,0:T(8,128)(2,1)S(1)} %copy-done), kind=kOutput, calls=%fused_computation.7 | convolution fusion | flops 1610612736 | bytes 7340032 | tf_op jit(solution)/shard_map/td,udf->utf/dot_general | solution.py:140
  120.5 3.1 %copy.90 = f32[1024,384]{1,0:T(8,128)} copy(f32[1024,384]{0,1:T(8,128)} %fusion.2) | data formatting | bytes 3145728 | tf_op jit(solution)/shard_map/jit(take_along_axis)/Arg_0.9 | solution.py:154
  123.6 1.4 gather_fusion.3
  125.1 2.4 %gather_fusion.4 = f32[128,384]{1,0:T(8,128)S(1)} fusion(f32[1024,384]{1,0:T(8,128)} %copy.90, s32[1024]{0:T(1024)S(1)} %pad_clamp_fusion), kind=kCustom, calls=%fused_computation.2.clone | custom fusion | bytes 393728 | tf_op jit(solution)/shard_map/jit(take_along_axis)/gather | solution.py:154
  127.5 6.2 %fusion.8 = (f32[1024]{0:T(1024)S(1)}, f32[1024,384]{0,1:T(8,128)}) fusion(f32[1024,384]{0,1:T(8,128)S(1)} %copy-done.2, f32[1024,384]{0,1:T(8,128)} %fusion.2, bf16[1,384,2048]{2,1,0:T(8,128)(2,1)} %param.17, bf16[1024,4224]{1,0:T(8,128)(2,1)} %all-gather.2.cloned.1.call-done), kind=kOutput, calls=%fused_computation.17 | convolution fusion | flops 1613364224 | bytes 10489856 | tf_op jit(solution)/shard_map/td,ufd->utf/dot_general | solution.py:142
  134.0 0.6 fusion.40
  134.7 1.9 copy.88
  136.5 0.8 gather_fusion.2
  137.3 0.7 and_select_fusion
  138.0 1.8 fusion.12
  139.8 0.7 fusion.6
  140.5 0.2 convert_element_type.151
  140.8 1.1 pad_maximum_fusion.x_ref
  141.9 26.5 %shard_map.96 = bf16[32,1,4,2176]{3,2,1,0:T(4,128)(2,1)} custom-call(bf16[32,1,4,2176]{3,2,1,0:T(4,128)(2,1)} %pad_maximum_fusion.x_ref), custom_call_target="tpu_custom_call" | custom-call | tf_op jit(solution)/shard_map/pallas_call | solution.py:72
  168.4 1.0 convert_add_fusion
  169.6 0.2 fusion.19
  169.8 0.8 top_k.17
  170.9 0.1 reshape.538
  171.1 0.2 convolution_convert_fusion
  171.4 0.7 pad_maximum_fusion.1.x_ref
  172.1 7.6 %shard_map.97 = bf16[8,4,2176]{2,1,0:T(4,128)(2,1)} custom-call(bf16[8,4,2176]{2,1,0:T(4,128)(2,1)} %pad_maximum_fusion.1.x_ref), custom_call_target="tpu_custom_call" | custom-call | tf_op jit(solution)/shard_map/pallas_call | solution.py:72
  179.7 0.9 add_bitcast_fusion
  180.6 0.1 copy.97
  180.7 0.2 reduce_sum.68
  181.0 0.2 multiply_reduce_fusion
  181.2 0.8 broadcast_in_dim.59
  182.0 10.0 %all-to-all-start = ((bf16[256,4,128]{2,1,0:T(4,128)(2,1)}), bf16[256,4,128]{2,1,0:T(4,128)(2,1)S(1)}, u32[]{:S(2)}, u32[]{:S(2)}) async-start(bf16[256,4,128]{2,1,0:T(4,128)(2,1)} %broadcast_in_dim.59), calls=%async_computation | async-start | bytes 524288 | tf_op jit(solution)/shard_map/all_to_all | solution.py:226
  192.1 1.0 convert_reduce_fusion
  193.0 0.9 fusion.7
  193.9 13.9 %all-to-all-done = bf16[256,4,128]{2,1,0:T(4,128)(2,1)S(1)} async-done(((bf16[256,4,128]{2,1,0:T(4,128)(2,1)}), bf16[256,4,128]{2,1,0:T(4,128)(2,1)S(1)}, u32[]{:S(2)}, u32[]{:S(2)}) %all-to-all-start) | async-done | bytes 262176 | tf_op jit(solution)/shard_map/all_to_all | solution.py:226
  207.8 1.9 fusion.20
  (83 shorter events, 2.3 us)
Async XLA Ops:
  7.2 108.2 %copy-start = (bf16[1,2048,384]{2,1,0:T(8,128)(2,1)S(1)}, bf16[1,2048,384]{2,1,0:T(8,128)(2,1)}, u32[]{:S(2)}) copy-start(bf16[1,2048,384]{2,1,0:T(8,128)(2,1)} %param.15) | copy-start | bytes 4718596
  7.2 2.6 %copy-start.10 = (s32[4,8]{1,0:T(4,128)S(1)}, s32[4,8]{1,0:T(4,128)}, u32[]{:S(2)}) copy-start(s32[4,8]{1,0:T(4,128)} %param.13) | copy-start | bytes 388
  7.2 3.0 %copy-start.11 = (bf16[4,2048]{1,0:T(4,128)(2,1)S(1)}, bf16[4,2048]{1,0:T(4,128)(2,1)}, u32[]{:S(2)}) copy-start(bf16[4,2048]{1,0:T(4,128)(2,1)} %param.11) | copy-start | bytes 49156
  7.2 3.0 %copy-start.12 = (bf16[4,2048]{1,0:T(4,128)(2,1)S(1)}, bf16[4,2048]{1,0:T(4,128)(2,1)}, u32[]{:S(2)}) copy-start(bf16[4,2048]{1,0:T(4,128)(2,1)} %param.10) | copy-start | bytes 49156
  7.2 95.8 %all-gather.2.cloned.1.call-start = ((), (), s32[]{:S(2)}) async-start(), calls=%async_computation.1 | async-start | bytes 8921088 | tf_op jit(solution)/shard_map/all_gather | solution.py:182
  8.1 16.0 %copy-start.1 = (f32[4,128]{1,0:T(4,128)S(1)}, f32[4,128]{1,0:T(4,128)}, u32[]{:S(2)}) copy-start(f32[4,128]{1,0:T(4,128)} %param.12) | copy-start | bytes 6148
  9.6 98.5 %copy-start.3 = (bf16[1,2048,384]{2,1,0:T(8,128)(2,1)S(1)}, bf16[1,2048,384]{2,1,0:T(8,128)(2,1)}, u32[]{:S(2)}) copy-start(bf16[1,2048,384]{2,1,0:T(8,128)(2,1)} %param.16) | copy-start | bytes 4718596
  24.8 79.6 %copy-start.15 = (s32[32]{0:T(128)}, s32[32]{0:T(128)S(1)}, u32[]{:S(2)}) copy-start(s32[32]{0:T(128)S(1)} %get-tuple-element.21) | copy-start | bytes 388
  24.8 79.6 %copy-start.17 = (s32[32]{0:T(128)}, s32[32]{0:T(128)S(1)}, u32[]{:S(2)}) copy-start(s32[32]{0:T(128)S(1)} %get-tuple-element.22) | copy-start | bytes 388
  125.1 2.4 %copy-start.2 = (f32[1024,384]{0,1:T(8,128)S(1)}, f32[1024,384]{0,1:T(8,128)}, u32[]{:S(2)}) copy-start(f32[1024,384]{0,1:T(8,128)} %fusion.4) | copy-start | bytes 4718596
  134.0 0.7 copy-start.6
  138.0 1.8 copy-start.4
  138.0 1.8 copy-start.13
  139.8 0.9 copy-start.7
  139.8 0.9 copy-start.8
  139.8 0.9 copy-start.9
  141.9 27.6 %slice-start.1 = ((bf16[1024,4224]{1,0:T(8,128)(2,1)}), bf16[1024,128]{1,0:T(8,128)(2,1)S(1)}, s32[]{:S(2)}) async-start(bf16[1024,4224]{1,0:T(8,128)(2,1)} %all-gather.2.cloned.1.call-done), calls=%async_computation.3 | async-start | bytes 524288 | tf_op jit(solution)/shard_map/slice | solution.py:183
  141.9 27.6 %copy-start.16 = (s32[32]{0:T(128)S(1)}, s32[32]{0:T(128)}, u32[]{:S(2)}) copy-start(s32[32]{0:T(128)} %copy-done.15) | copy-start | bytes 388
  141.9 27.6 %copy-start.18 = (s32[32]{0:T(128)S(1)}, s32[32]{0:T(128)}, u32[]{:S(2)}) copy-start(s32[32]{0:T(128)} %copy-done.17) | copy-start | bytes 388
  141.9 27.6 %copy-start.19 = (s32[32]{0:T(128)S(1)}, s32[32]{0:T(128)}, u32[]{:S(2)}) copy-start(s32[32]{0:T(128)} %and_select_fusion.2) | copy-start | bytes 388
  168.4 2.5 %slice-start = ((bf16[32,1,4,2176]{3,2,1,0:T(4,128)(2,1)}), bf16[32,1,4,2048]{3,2,1,0:T(4,128)(2,1)S(1)}, s32[]{:S(2)}) async-start(bf16[32,1,4,2176]{3,2,1,0:T(4,128)(2,1)} %shard_map.96), calls=%async_computation.2 | async-start | bytes 1048576 | tf_op jit(solution)/shard_map/slice | solution.py:203
  169.6 11.4 %copy-start.14 = (f32[4]{0:T(128)S(1)}, f32[4]{0:T(128)}, u32[]{:S(2)}) copy-start(f32[4]{0:T(128)} %fusion.59) | copy-start | bytes 52
  171.0 22.1 %copy-start.5 = (bf16[2048,128]{1,0:T(8,128)(2,1)S(1)}, bf16[2048,128]{1,0:T(8,128)(2,1)}, u32[]{:S(2)}) copy-start(bf16[2048,128]{1,0:T(8,128)(2,1)} %param.14) | copy-start | bytes 1572868
  182.0 25.7 %all-to-all-start = ((bf16[256,4,128]{2,1,0:T(4,128)(2,1)}), bf16[256,4,128]{2,1,0:T(4,128)(2,1)S(1)}, u32[]{:S(2)}, u32[]{:S(2)}) async-start(bf16[256,4,128]{2,1,0:T(4,128)(2,1)} %broadcast_in_dim.59), calls=%async_computation | async-start | bytes 524288 | tf_op jit(solution)/shard_map/all_to_all | solution.py:226
Sparse Core Ops, SparseCore 0:
  24.2 78.8 all-gather.1

commit v9 on v8

--- a/solution.py
+++ b/solution.py
@@ -136,14 +136,49 @@
     return (part(0) + part(1)) + part(2)
 
 
-def dense_terms(x_rows, g_rows, w_gate, w_up, w_down):
-    gate_pre = jnp.einsum("td,udf->utf", x_rows, w_gate, preferred_element_type=jnp.float32)
-    up_pre = jnp.einsum("td,udf->utf", x_rows, w_up, preferred_element_type=jnp.float32)
-    back_grad = jnp.einsum("td,ufd->utf", g_rows, w_down, preferred_element_type=jnp.float32)
-    sig_gate = jax.nn.sigmoid(gate_pre)
-    act_gate = gate_pre * sig_gate
-    score_part = jnp.sum(act_gate * up_pre * back_grad, axis=2).T
-    return score_part, gate_pre, up_pre, back_grad
+def dense_kernel(x_ref, g_ref, wg_ref, wu_ref, wd_ref, gate_ref, up_ref, back_ref, score_ref):
+    x = x_ref[...]
+    gate_pre = jnp.dot(x, wg_ref[...], preferred_element_type=jnp.float32)
+    up_pre = jnp.dot(x, wu_ref[...], preferred_element_type=jnp.float32)
+    back_grad = lax.dot_general(
+        g_ref[...], wd_ref[...], (((1,), (1,)), ((), ())), preferred_element_type=jnp.float32
+    )
+    sig_gate = 1.0 / (1.0 + jnp.exp(-gate_pre))
+    gate_ref[...] = gate_pre
+    up_ref[...] = up_pre
+    back_ref[...] = back_grad
+    score_ref[...] = jnp.sum(gate_pre * sig_gate * up_pre * back_grad, axis=1, keepdims=True)
+
+
+def dense_unit(gathered, gate_w, up_w, down_w, tile=256):
+    tokens_n = gathered.shape[0]
+    width, hidden = gate_w.shape
+    rows = lambda i: (i, 0)
+    fixed = lambda i: (0, 0)
+    f32 = jnp.float32
+    return pl.pallas_call(
+        dense_kernel,
+        grid=(tokens_n // tile,),
+        out_shape=[
+            jax.ShapeDtypeStruct((tokens_n, hidden), f32),
+            jax.ShapeDtypeStruct((tokens_n, hidden), f32),
+            jax.ShapeDtypeStruct((tokens_n, hidden), f32),
+            jax.ShapeDtypeStruct((tokens_n, 1), f32),
+        ],
+        in_specs=[
+            pl.BlockSpec((tile, width), rows),
+            pl.BlockSpec((tile, width), lambda i: (i, 1)),
+            pl.BlockSpec((width, hidden), fixed),
+            pl.BlockSpec((width, hidden), fixed),
+            pl.BlockSpec((hidden, width), fixed),
+        ],
+        out_specs=[
+            pl.BlockSpec((tile, hidden), rows),
+            pl.BlockSpec((tile, hidden), rows),
+            pl.BlockSpec((tile, hidden), rows),
+            pl.BlockSpec((tile, 1), rows),
+        ],
+    )(gathered, gathered, gate_w, up_w, down_w)
 
 
 def sparse_terms(gate_pre, up_pre, back_grad, column, w_gate, w_up, group_rows):
@@ -181,9 +216,9 @@
     packed = jnp.concatenate([tokens, grad_out, combine], axis=1)
     gathered = lax.all_gather(hid_gather(packed), "exp", axis=0, tiled=True)
     combine_all = gathered[:, 2 * model_width :]
-    score_part, gate_pre, up_pre, back_grad = dense_terms(
-        gathered[:, :model_width], gathered[:, model_width : 2 * model_width], w_gate, w_up, w_down
-    )
+    dense = [dense_unit(gathered, w_gate[i], w_up[i], w_down[i]) for i in range(unit_count)]
+    gate_pre, up_pre, back_grad = (jnp.stack([d[j] for d in dense]) for j in range(3))
+    score_part = jnp.concatenate([d[3] for d in dense], axis=1)
     column = jnp.dot(combine_all, unit_pick, preferred_element_type=jnp.float32).T
     part = sparse_terms(gate_pre, up_pre, back_grad, column, w_gate, w_up, group_rows)
     lane = 128

time: 217 us -> 204 us (0.940)
  matrix products: 23.3 us -> 5.6 us
  Pallas kernels: 45.5 us -> 56.8 us
  local copies, waits for them, and re-layouts: 19.4 us -> 13.1 us
    dot_general x3 -> x0, matrix products: 16.7 us -> none  [the longest x1 6.22 us: dense_terms(): jnp.einsum('td,ufd->utf', g_rows, w_down, preferred_element_type=jnp.floa...]
    pallas_call x0 -> x1, Pallas kernels: none -> 11.5 us  [dense_unit(): pl.pallas_call(dense_kernel, grid=(tokens_n // tile,), out_shape=[jax.Sha...]
    another operation x3 -> x0, local copies, waits for them, and re-layouts: 6.86 us -> none  [sparse_terms(): take = lambda a: jnp.take_along_axis(a, rows[:, :, None], axis=1)]
where the time goes in v9:
time: 204 us; the launch traced here: 203 us
  waiting for transfers between devices  92.5 us (45%)
  Pallas kernels  56.8 us (28%)
  between operations  14.4 us (7%)
  local copies, waits for them, and re-layouts  13.1 us (6%)
  other arithmetic  10.7 us (5%)
  starting transfers between devices  10.1 us (5%)
  matrix products  5.6 us (3%)
    all_gather x1, waiting for transfers between devices, on_device(): gathered = lax.all_gather(hid_gather(packed), 'exp', axis=0, tiled=True)  78.6 us
    pallas_call x2, Pallas kernels, exchange(): pl.pallas_call(functools.partial(exchange_kernel, axis, n), out_shape=jax...  33.9 us
    all_to_all x1, waiting for transfers between devices, on_device(): lax.all_to_all(jnp.broadcast_to(logit_grad[None], (devices,) + logit_grad...  13.9 us
    pallas_call x1, Pallas kernels, dense_unit(): pl.pallas_call(dense_kernel, grid=(tokens_n // tile,), out_shape=[jax.Sha...  11.5 us
    pallas_call x1, Pallas kernels, hid_gather(): pl.pallas_call(functools.partial(hid_gather_kernel, n), out_shape=jax.Sha...  11.4 us
    all_to_all x1, starting transfers between devices, on_device(): lax.all_to_all(jnp.broadcast_to(logit_grad[None], (devices,) + logit_grad...  10 us
    gather x3, local copies, waits for them, and re-layouts, sparse_terms(): take = lambda a: jnp.take_along_axis(a, rows[:, :, None], axis=1)  5.37 us
  transfers between devices with their start and end apart: 2, of which 2 were waited for; matrix products, arithmetic and copies ran while one was open for 1% of the time, Pallas kernels for 0%

profile of v9, /device:TPU:1, one launch (start us, length us, event | category | flops | bytes accessed | tf_op | source)
XLA Modules:
  0.0 203.2 jit_solution(13744809003783057206)
XLA Ops:
  7.3 0.7 bitcast_or_fusion
  8.1 1.5 gather_fusion.1
  9.7 0.1 fusion.59
  9.8 0.2 fusion.42
  10.2 0.6 pad_maximum_fusion.2.x_ref
  10.8 11.4 %shard_map.95 = bf16[8,4,4224]{2,1,0:T(4,128)(2,1)} custom-call(bf16[4,4224]{1,0:T(4,128)(2,1)} %pad_maximum_fusion.2.x_ref), custom_call_target="tpu_custom_call" | custom-call | tf_op jit(solution)/shard_map/pallas_call | solution.py:88
  22.3 1.7 reshape.431
  24.0 0.1 reduce_max.19
  24.2 0.2 fusion.44
  24.4 78.6 %all-gather.2.cloned.1.call-done.x_ref.g_ref = bf16[1024,4224]{1,0:T(8,128)(2,1)} async-done(((bf16[32,4224]{1,0:T(8,128)(2,1)}), bf16[1024,4224]{1,0:T(8,128)(2,1)}) %all-gather.2.cloned.1.call-update) | async-done | bytes 8650768 | tf_op jit(solution)/shard_map/all_gather | solution.py:217
  103.0 1.1 fusion.38
  104.4 0.8 top_k.24
  105.3 0.1 reshape.434
  105.4 0.1 reshape.433
  105.5 0.1 reshape.432
  105.6 11.5 %shard_map.96 = (f32[1024,384]{1,0:T(8,128)}, f32[1024,384]{1,0:T(8,128)}, f32[1024,384]{1,0:T(8,128)}, f32[1024,1]{1,0:T(8,128)}) custom-call(bf16[1024,4224]{1,0:T(8,128)(2,1)} %all-gather.2.cloned.1.call-done.x_ref.g_ref, bf16[1024,4224]{1,0:T(8,128)(2,1)} %all-gather.2.cloned.1.call-done.x_ref.g_ref, bf16[2048,384]{1,0:T(8,128)(2,1)} %bitcast.104, ...), custom_call_target="tpu_custom_call" | custom-call | tf_op jit(solution)/shard_map/pallas_call | solution.py:159
  117.1 1.4 reduce
  118.5 0.1 transpose_reshape_transpose.3
  118.7 0.1 copy.76
  118.9 2.2 %gather_fusion.3 = f32[128,384]{1,0:T(8,128)S(1)} fusion(f32[1024,384]{1,0:T(8,128)} %get-tuple-element.16, s32[1024]{0:T(1024)S(1)} %pad_clamp_fusion), kind=kCustom, calls=%fused_computation.1.clone | custom fusion | bytes 393728 | tf_op jit(solution)/shard_map/jit(take_along_axis)/gather | solution.py:189
  121.1 0.8 gather_fusion.4
  121.9 2.4 %gather_fusion.2 = f32[128,384]{1,0:T(8,128)S(1)} fusion(f32[1024,384]{1,0:T(8,128)} %get-tuple-element.15, s32[1024]{0:T(1024)S(1)} %pad_clamp_fusion), kind=kCustom, calls=%fused_computation.clone | custom fusion | bytes 393728 | tf_op jit(solution)/shard_map/jit(take_along_axis)/gather | solution.py:189
  124.3 1.0 gather_fusion
  125.3 0.7 fusion.12
  126.0 0.7 copy-done.3
  126.7 0.7 fusion
  127.4 0.2 convert_element_type.151
  127.6 0.1 fusion.28
  127.7 1.1 pad_maximum_fusion.x_ref
  128.8 26.3 %shard_map.97 = bf16[32,1,4,2176]{3,2,1,0:T(4,128)(2,1)} custom-call(bf16[32,1,4,2176]{3,2,1,0:T(4,128)(2,1)} %pad_maximum_fusion.x_ref), custom_call_target="tpu_custom_call" | custom-call | tf_op jit(solution)/shard_map/pallas_call | solution.py:72
  155.2 1.0 convert_add_fusion
  156.3 0.1 reshape.517
  156.4 0.2 fusion.3
  156.7 0.8 top_k.17
  157.6 0.1 eq.76
  157.7 0.2 convolution_convert_fusion
  158.0 0.7 pad_maximum_fusion.1.x_ref
  158.8 7.6 %shard_map.98 = bf16[8,4,2176]{2,1,0:T(4,128)(2,1)} custom-call(bf16[8,4,2176]{2,1,0:T(4,128)(2,1)} %pad_maximum_fusion.1.x_ref), custom_call_target="tpu_custom_call" | custom-call | tf_op jit(solution)/shard_map/pallas_call | solution.py:72
  166.4 0.9 add_bitcast_fusion
  167.3 0.1 copy.79
  167.4 0.2 reduce_sum.58
  167.6 0.2 multiply_reduce_fusion
  167.9 0.8 broadcast_in_dim.59
  168.7 10.0 %all-to-all-start = ((bf16[256,4,128]{2,1,0:T(4,128)(2,1)}), bf16[256,4,128]{2,1,0:T(4,128)(2,1)S(1)}, u32[]{:S(2)}, u32[]{:S(2)}) async-start(bf16[256,4,128]{2,1,0:T(4,128)(2,1)} %broadcast_in_dim.59), calls=%async_computation | async-start | bytes 524288 | tf_op jit(solution)/shard_map/all_to_all | solution.py:261
  178.7 1.0 convert_reduce_fusion
  179.7 0.9 fusion.1
  180.6 13.9 %all-to-all-done = bf16[256,4,128]{2,1,0:T(4,128)(2,1)S(1)} async-done(((bf16[256,4,128]{2,1,0:T(4,128)(2,1)}), bf16[256,4,128]{2,1,0:T(4,128)(2,1)S(1)}, u32[]{:S(2)}, u32[]{:S(2)}) %all-to-all-start) | async-done | bytes 262176 | tf_op jit(solution)/shard_map/all_to_all | solution.py:261
  194.4 1.9 fusion.4
  (55 shorter events, 1.5 us)
Async XLA Ops:
  7.2 172.6 %copy-start = (bf16[2048,128]{1,0:T(8,128)(2,1)S(1)}, bf16[2048,128]{1,0:T(8,128)(2,1)}, u32[]{:S(2)}) copy-start(bf16[2048,128]{1,0:T(8,128)(2,1)} %param.14) | copy-start | bytes 1572868
  7.2 2.5 %copy-start.5 = (s32[4,8]{1,0:T(4,128)S(1)}, s32[4,8]{1,0:T(4,128)}, u32[]{:S(2)}) copy-start(s32[4,8]{1,0:T(4,128)} %param.13) | copy-start | bytes 388
  7.2 3.0 %copy-start.6 = (bf16[4,2048]{1,0:T(4,128)(2,1)S(1)}, bf16[4,2048]{1,0:T(4,128)(2,1)}, u32[]{:S(2)}) copy-start(bf16[4,2048]{1,0:T(4,128)(2,1)} %param.11) | copy-start | bytes 49156
  7.2 3.0 %copy-start.7 = (bf16[4,2048]{1,0:T(4,128)(2,1)S(1)}, bf16[4,2048]{1,0:T(4,128)(2,1)}, u32[]{:S(2)}) copy-start(bf16[4,2048]{1,0:T(4,128)(2,1)} %param.10) | copy-start | bytes 49156
  7.2 95.8 %all-gather.2.cloned.1.call-start = ((), (), s32[]{:S(2)}) async-start(), calls=%async_computation.1 | async-start | bytes 8921088 | tf_op jit(solution)/shard_map/all_gather | solution.py:217
  8.1 16.0 %copy-start.1 = (f32[4,128]{1,0:T(4,128)S(1)}, f32[4,128]{1,0:T(4,128)}, u32[]{:S(2)}) copy-start(f32[4,128]{1,0:T(4,128)} %param.12) | copy-start | bytes 6148
  117.1 4.0 %copy-start.4 = (f32[1024,384]{1,0:T(8,128)S(1)}, f32[1024,384]{1,0:T(8,128)}, u32[]{:S(2)}) copy-start(f32[1024,384]{1,0:T(8,128)} %get-tuple-element.17) | copy-start | bytes 4718596
  121.9 3.4 %copy-start.2 = (bf16[1,2048,384]{2,1,0:T(8,128)(2,1)S(1)}, bf16[1,2048,384]{2,1,0:T(8,128)(2,1)}, u32[]{:S(2)}) copy-start(bf16[1,2048,384]{2,1,0:T(8,128)(2,1)} %param.15) | copy-start | bytes 4718596
  125.3 1.4 copy-start.3
  155.1 1.1 slice-start.1
  155.2 1.2 slice-start
  168.7 25.7 %all-to-all-start = ((bf16[256,4,128]{2,1,0:T(4,128)(2,1)}), bf16[256,4,128]{2,1,0:T(4,128)(2,1)S(1)}, u32[]{:S(2)}, u32[]{:S(2)}) async-start(bf16[256,4,128]{2,1,0:T(4,128)(2,1)} %broadcast_in_dim.59), calls=%async_computation | async-start | bytes 524288 | tf_op jit(solution)/shard_map/all_to_all | solution.py:261
Sparse Core Ops, SparseCore 0:
  24.1 78.8 all-gather.1

commit v10 on v9

--- a/solution.py
+++ b/solution.py
@@ -136,7 +136,7 @@
     return (part(0) + part(1)) + part(2)
 
 
-def dense_kernel(x_ref, g_ref, wg_ref, wu_ref, wd_ref, gate_ref, up_ref, back_ref, score_ref):
+def dense_kernel(x_ref, g_ref, wg_ref, wu_ref, wd_ref, score_ref):
     x = x_ref[...]
     gate_pre = jnp.dot(x, wg_ref[...], preferred_element_type=jnp.float32)
     up_pre = jnp.dot(x, wu_ref[...], preferred_element_type=jnp.float32)
@@ -144,9 +144,6 @@
         g_ref[...], wd_ref[...], (((1,), (1,)), ((), ())), preferred_element_type=jnp.float32
     )
     sig_gate = 1.0 / (1.0 + jnp.exp(-gate_pre))
-    gate_ref[...] = gate_pre
-    up_ref[...] = up_pre
-    back_ref[...] = back_grad
     score_ref[...] = jnp.sum(gate_pre * sig_gate * up_pre * back_grad, axis=1, keepdims=True)
 
 
@@ -159,12 +156,7 @@
     return pl.pallas_call(
         dense_kernel,
         grid=(tokens_n // tile,),
-        out_shape=[
-            jax.ShapeDtypeStruct((tokens_n, hidden), f32),
-            jax.ShapeDtypeStruct((tokens_n, hidden), f32),
-            jax.ShapeDtypeStruct((tokens_n, hidden), f32),
-            jax.ShapeDtypeStruct((tokens_n, 1), f32),
-        ],
+        out_shape=jax.ShapeDtypeStruct((tokens_n, 1), f32),
         in_specs=[
             pl.BlockSpec((tile, width), rows),
             pl.BlockSpec((tile, width), lambda i: (i, 1)),
@@ -172,22 +164,19 @@
             pl.BlockSpec((width, hidden), fixed),
             pl.BlockSpec((hidden, width), fixed),
         ],
-        out_specs=[
-            pl.BlockSpec((tile, hidden), rows),
-            pl.BlockSpec((tile, hidden), rows),
-            pl.BlockSpec((tile, hidden), rows),
-            pl.BlockSpec((tile, 1), rows),
-        ],
+        out_specs=pl.BlockSpec((tile, 1), rows),
     )(gathered, gathered, gate_w, up_w, down_w)
 
 
-def sparse_terms(gate_pre, up_pre, back_grad, column, w_gate, w_up, group_rows):
+def sparse_terms(x_rows, g_rows, column, w_gate, w_up, w_down, group_rows):
     picked = slot_rows(column, group_rows)
     groups = picked.shape[1]
     starts = (jnp.arange(groups, dtype=jnp.int32) * group_rows)[None, :, None]
     rows = (picked + starts).reshape(picked.shape[0], -1)
-    take = lambda a: jnp.take_along_axis(a, rows[:, :, None], axis=1)
-    gate_s, up_s, back_s = take(gate_pre), take(up_pre), take(back_grad)
+    x_s, g_s = jnp.take(x_rows, rows, axis=0), jnp.take(g_rows, rows, axis=0)
+    gate_s = jnp.einsum("usd,udf->usf", x_s, w_gate, preferred_element_type=jnp.float32)
+    up_s = jnp.einsum("usd,udf->usf", x_s, w_up, preferred_element_type=jnp.float32)
+    back_s = jnp.einsum("usd,ufd->usf", g_s, w_down, preferred_element_type=jnp.float32)
     col_s = jnp.take_along_axis(column, rows, axis=1)
     sig_gate = jax.nn.sigmoid(gate_s)
     act_gate = gate_s * sig_gate
@@ -217,10 +206,12 @@
     gathered = lax.all_gather(hid_gather(packed), "exp", axis=0, tiled=True)
     combine_all = gathered[:, 2 * model_width :]
     dense = [dense_unit(gathered, w_gate[i], w_up[i], w_down[i]) for i in range(unit_count)]
-    gate_pre, up_pre, back_grad = (jnp.stack([d[j] for d in dense]) for j in range(3))
-    score_part = jnp.concatenate([d[3] for d in dense], axis=1)
+    score_part = jnp.concatenate(dense, axis=1)
     column = jnp.dot(combine_all, unit_pick, preferred_element_type=jnp.float32).T
-    part = sparse_terms(gate_pre, up_pre, back_grad, column, w_gate, w_up, group_rows)
+    part = sparse_terms(
+        gathered[:, :model_width], gathered[:, model_width : 2 * model_width], column, w_gate, w_up, w_down,
+        group_rows,
+    )
     lane = 128
     score_grp = jnp.swapaxes(score_part.T.reshape(unit_count, spread_exp, CAP, group_rows // CAP), 0, 1)
     score_grp = split3(score_grp)

time: 204 us -> 220 us (1.078)
  local copies, waits for them, and re-layouts: 13.1 us -> 25.2 us
  matrix products: 5.6 us -> 9.43 us
    slice x0 -> x1, local copies, waits for them, and re-layouts: none -> 6.03 us  [on_device(): gathered[:, :model_width]]
    gather x3 -> x2, local copies, waits for them, and re-layouts: 5.37 us -> 9.36 us  [sparse_terms(): x_s, g_s = (jnp.take(x_rows, rows, axis=0), jnp.take(g_rows, rows, axis=0))]
where the time goes in v10:
time: 220 us; the launch traced here: 219 us
  waiting for transfers between devices  91.9 us (42%)
  Pallas kernels  56.6 us (26%)
  local copies, waits for them, and re-layouts  25.2 us (11%)
  between operations  14.5 us (7%)
  other arithmetic  11.1 us (5%)
  starting transfers between devices  10.1 us (5%)
  matrix products  9.43 us (4%)
    all_gather x1, waiting for transfers between devices, on_device(): gathered = lax.all_gather(hid_gather(packed), 'exp', axis=0, tiled=True)  78.1 us
    pallas_call x2, Pallas kernels, exchange(): pl.pallas_call(functools.partial(exchange_kernel, axis, n), out_shape=jax...  33.9 us
    all_to_all x1, waiting for transfers between devices, on_device(): lax.all_to_all(jnp.broadcast_to(logit_grad[None], (devices,) + logit_grad...  13.9 us
    pallas_call x1, Pallas kernels, hid_gather(): pl.pallas_call(functools.partial(hid_gather_kernel, n), out_shape=jax.Sha...  11.4 us
    pallas_call x1, Pallas kernels, dense_unit(): pl.pallas_call(dense_kernel, grid=(tokens_n // tile,), out_shape=jax.Shap...  11.2 us
    all_to_all x1, starting transfers between devices, on_device(): lax.all_to_all(jnp.broadcast_to(logit_grad[None], (devices,) + logit_grad...  10 us
    gather x2, local copies, waits for them, and re-layouts, sparse_terms(): x_s, g_s = (jnp.take(x_rows, rows, axis=0), jnp.take(g_rows, rows, axis=0))  9.36 us
    slice x1, local copies, waits for them, and re-layouts, on_device(): gathered[:, :model_width]  6.03 us
  transfers between devices with their start and end apart: 2, of which 2 were waited for; matrix products, arithmetic and copies ran while one was open for 1% of the time, Pallas kernels for 0%

profile of v10, /device:TPU:1, one launch (start us, length us, event | category | flops | bytes accessed | tf_op | source)
XLA Modules:
  0.0 218.8 jit_solution(14214849286142056479)
XLA Ops:
  7.3 0.7 bitcast_or_fusion
  8.1 1.5 gather_fusion.1
  9.7 0.1 fusion.66
  9.8 0.2 fusion.43
  10.2 0.6 pad_maximum_fusion.2.x_ref
  10.8 11.4 %shard_map.95 = bf16[8,4,4224]{2,1,0:T(4,128)(2,1)} custom-call(bf16[4,4224]{1,0:T(4,128)(2,1)} %pad_maximum_fusion.2.x_ref), custom_call_target="tpu_custom_call" | custom-call | tf_op jit(solution)/shard_map/pallas_call | solution.py:88
  22.3 1.7 reshape.462
  24.0 0.1 reduce_max.19
  24.2 0.5 and_select_fusion.2
  24.7 0.2 fusion.45
  24.9 78.1 %all-gather.2.cloned.1.call-done.x_ref.g_ref = bf16[1024,4224]{1,0:T(8,128)(2,1)} async-done(((bf16[32,4224]{1,0:T(8,128)(2,1)}), bf16[1024,4224]{1,0:T(8,128)(2,1)}) %all-gather.2.cloned.1.call-update) | async-done | bytes 8650768 | tf_op jit(solution)/shard_map/all_gather | solution.py:206
  103.0 1.1 fusion.39
  104.4 0.8 top_k.24
  105.7 6.0 %fusion.67 = (bf16[1024,2048]{1,0:T(8,128)(2,1)}, bf16[1024,2048]{1,0:T(8,128)(2,1)}) fusion(bf16[1024,4224]{1,0:T(8,128)(2,1)} %all-gather.2.cloned.1.call-done.x_ref.g_ref), kind=kLoop, calls=%fused_computation.117 | loop fusion | bytes 16777216 | tf_op jit(solution)/shard_map/slice | solution.py:212
  111.7 4.2 %gather_fusion.3 = bf16[128,2048]{1,0:T(8,128)(2,1)S(1)} fusion(bf16[1024,2048]{1,0:T(8,128)(2,1)} %get-tuple-element.15, s32[1024]{0:T(1024)S(1)} %pad_clamp_fusion), kind=kCustom, calls=%fused_computation.1.clone | custom fusion | bytes 1049088 | tf_op jit(solution)/shard_map/jit(_take)/gather | solution.py:176
  115.9 5.2 %gather_fusion.2 = bf16[128,2048]{1,0:T(8,128)(2,1)} fusion(bf16[1024,2048]{1,0:T(8,128)(2,1)} %get-tuple-element.16, s32[1024]{0:T(1024)S(1)} %pad_clamp_fusion), kind=kCustom, calls=%fused_computation.clone | custom fusion | bytes 1049088 | tf_op jit(solution)/shard_map/jit(_take)/gather | solution.py:176
  121.1 1.0 gather_fusion
  122.1 0.5 fusion.8
  122.6 0.8 copy-done.5
  123.6 0.6 convolution_multiply_fusion.1
  124.2 0.8 copy-done.2
  125.0 2.6 %fusion.5 = f32[128,2048]{1,0:T(8,128)S(1)} fusion(f32[128,384]{1,0:T(8,128)S(1)} %convolution_multiply_fusion.1, bf16[128,2048]{1,0:T(8,128)(2,1)} %copy-done.4, pred[128]{0:T(512)(128)(4,1)} %copy-done.14, f32[128,384]{1,0:T(8,128)S(1)} %fusion.8, bf16[1,2048,384]{2,1,0:T(8,128)(2,1)} %param.15, bf16[1,2048,384]{2,1,0:T(8,128)(2,1)S(1)} %copy-done.2), kind=kOutput, calls=%fused_computation.14 | convolution fusion | flops 403406848 | bytes 5111936 | tf_op jit(solution)/shard_map/usf,udf->usd/dot_general | solution.py:186
  127.6 1.5 fusion
  129.1 1.2 convert_element_type.153
  130.3 11.2 %shard_map.96 = f32[1024,1]{1,0:T(8,128)} custom-call(bf16[1024,4224]{1,0:T(8,128)(2,1)} %all-gather.2.cloned.1.call-done.x_ref.g_ref, bf16[1024,4224]{1,0:T(8,128)(2,1)} %all-gather.2.cloned.1.call-done.x_ref.g_ref, bf16[2048,384]{1,0:T(8,128)(2,1)} %bitcast.85, bf16[2048,384]{1,0:T(8,128)(2,1)} %bitcast.84, bf16[384,2048]{1,0:T(8,128)(2,1)} %bitcast.86), custom_call_target="tpu_custom_call" | custom-call | tf_op jit(solution)/shard_map/pallas_call | solution.py:156
  141.6 1.2 reduce
  142.8 0.1 transpose_reshape_transpose.3
  143.0 0.1 copy.76
  143.2 0.1 fusion.29
  143.3 1.1 pad_maximum_fusion.x_ref
  144.4 26.3 %shard_map.97 = bf16[32,1,4,2176]{3,2,1,0:T(4,128)(2,1)} custom-call(bf16[32,1,4,2176]{3,2,1,0:T(4,128)(2,1)} %pad_maximum_fusion.x_ref), custom_call_target="tpu_custom_call" | custom-call | tf_op jit(solution)/shard_map/pallas_call | solution.py:72
  170.8 1.0 convert_add_fusion
  171.9 0.1 reshape.527
  172.0 0.2 fusion.7
  172.3 0.8 top_k.17
  173.4 0.2 convolution_convert_fusion
  173.7 0.7 pad_maximum_fusion.1.x_ref
  174.4 7.6 %shard_map.98 = bf16[8,4,2176]{2,1,0:T(4,128)(2,1)} custom-call(bf16[8,4,2176]{2,1,0:T(4,128)(2,1)} %pad_maximum_fusion.1.x_ref), custom_call_target="tpu_custom_call" | custom-call | tf_op jit(solution)/shard_map/pallas_call | solution.py:72
  182.0 0.9 add_bitcast_fusion
  182.9 0.1 copy.79
  183.1 0.2 reduce_sum.58
  183.3 0.2 multiply_reduce_fusion
  183.6 0.8 broadcast_in_dim.62
  184.4 10.0 %all-to-all-start = ((bf16[256,4,128]{2,1,0:T(4,128)(2,1)}), bf16[256,4,128]{2,1,0:T(4,128)(2,1)S(1)}, u32[]{:S(2)}, u32[]{:S(2)}) async-start(bf16[256,4,128]{2,1,0:T(4,128)(2,1)} %broadcast_in_dim.62), calls=%async_computation | async-start | bytes 524288 | tf_op jit(solution)/shard_map/all_to_all | solution.py:252
  194.4 1.0 convert_reduce_fusion
  195.4 0.9 fusion.1
  196.2 13.9 %all-to-all-done = bf16[256,4,128]{2,1,0:T(4,128)(2,1)S(1)} async-done(((bf16[256,4,128]{2,1,0:T(4,128)(2,1)}), bf16[256,4,128]{2,1,0:T(4,128)(2,1)S(1)}, u32[]{:S(2)}, u32[]{:S(2)}) %all-to-all-start) | async-done | bytes 262176 | tf_op jit(solution)/shard_map/all_to_all | solution.py:252
  210.1 1.9 fusion.15
  (73 shorter events, 2.1 us)
Async XLA Ops:
  7.2 188.2 %copy-start = (bf16[2048,128]{1,0:T(8,128)(2,1)S(1)}, bf16[2048,128]{1,0:T(8,128)(2,1)}, u32[]{:S(2)}) copy-start(bf16[2048,128]{1,0:T(8,128)(2,1)} %param.14) | copy-start | bytes 1572868
  7.2 2.5 %copy-start.7 = (s32[4,8]{1,0:T(4,128)S(1)}, s32[4,8]{1,0:T(4,128)}, u32[]{:S(2)}) copy-start(s32[4,8]{1,0:T(4,128)} %param.13) | copy-start | bytes 388
  7.2 3.0 %copy-start.9 = (bf16[4,2048]{1,0:T(4,128)(2,1)S(1)}, bf16[4,2048]{1,0:T(4,128)(2,1)}, u32[]{:S(2)}) copy-start(bf16[4,2048]{1,0:T(4,128)(2,1)} %param.10) | copy-start | bytes 49156
  7.2 3.0 %copy-start.8 = (bf16[4,2048]{1,0:T(4,128)(2,1)S(1)}, bf16[4,2048]{1,0:T(4,128)(2,1)}, u32[]{:S(2)}) copy-start(bf16[4,2048]{1,0:T(4,128)(2,1)} %param.11) | copy-start | bytes 49156
  7.2 95.8 %all-gather.2.cloned.1.call-start = ((), (), s32[]{:S(2)}) async-start(), calls=%async_computation.1 | async-start | bytes 8921088 | tf_op jit(solution)/shard_map/all_gather | solution.py:206
  8.1 16.0 %copy-start.1 = (f32[4,128]{1,0:T(4,128)S(1)}, f32[4,128]{1,0:T(4,128)}, u32[]{:S(2)}) copy-start(f32[4,128]{1,0:T(4,128)} %param.12) | copy-start | bytes 6148
  24.7 79.6 %copy-start.10 = (s32[32]{0:T(128)}, s32[32]{0:T(128)S(1)}, u32[]{:S(2)}) copy-start(s32[32]{0:T(128)S(1)} %get-tuple-element.21) | copy-start | bytes 388
  24.7 79.6 %copy-start.12 = (s32[32]{0:T(128)}, s32[32]{0:T(128)S(1)}, u32[]{:S(2)}) copy-start(s32[32]{0:T(128)S(1)} %get-tuple-element.22) | copy-start | bytes 388
  105.4 17.2 %copy-start.14 = (pred[128]{0:T(512)(128)(4,1)}, pred[128]{0:T(512)(128)(4,1)S(1)}, u32[]{:S(2)}) copy-start(pred[128]{0:T(512)(128)(4,1)S(1)} %and_bitcast_fusion) | copy-start | bytes 388
  115.9 6.2 %copy-start.4 = (bf16[128,2048]{1,0:T(8,128)(2,1)}, bf16[128,2048]{1,0:T(8,128)(2,1)S(1)}, u32[]{:S(2)}) copy-start(bf16[128,2048]{1,0:T(8,128)(2,1)S(1)} %gather_fusion.3) | copy-start | bytes 1572868
  115.9 6.2 %copy-start.3 = (bf16[1,2048,384]{2,1,0:T(8,128)(2,1)S(1)}, bf16[1,2048,384]{2,1,0:T(8,128)(2,1)}, u32[]{:S(2)}) copy-start(bf16[1,2048,384]{2,1,0:T(8,128)(2,1)} %param.15) | copy-start | bytes 4718596
  122.1 1.4 copy-start.5
  122.1 1.5 copy-start.6
  123.6 1.4 copy-start.2
  170.7 1.1 slice-start.1
  170.7 1.3 slice-start
  170.8 1.3 copy-start.11
  170.8 1.3 copy-start.13
  170.8 1.3 copy-start.15
  184.4 25.7 %all-to-all-start = ((bf16[256,4,128]{2,1,0:T(4,128)(2,1)}), bf16[256,4,128]{2,1,0:T(4,128)(2,1)S(1)}, u32[]{:S(2)}, u32[]{:S(2)}) async-start(bf16[256,4,128]{2,1,0:T(4,128)(2,1)} %broadcast_in_dim.62), calls=%async_computation | async-start | bytes 524288 | tf_op jit(solution)/shard_map/all_to_all | solution.py:252
Sparse Core Ops, SparseCore 0:
  24.1 78.8 all-gather.1

commit v11 on v9

--- a/solution.py
+++ b/solution.py
@@ -36,12 +36,9 @@
         copy.wait()
 
 
-def exchange_kernel(axis, n, x_ref, out_ref, local_sem, send_sem, recv_sem):
-    me = lax.axis_index(axis)
-    own_exp = lax.axis_index("exp")
-    own_hid = lax.axis_index("hid")
+def exchange_kernel(n, spot, where, x_ref, out_ref, local_sem, send_sem, recv_sem):
+    me = spot()
     mesh_ids = pl.DeviceIdType.MESH
-    where = lambda peer: (peer, own_hid) if axis == "exp" else (own_exp, peer)
     barrier = pltpu.get_barrier_semaphore()
     for k in range(1, n):
         peer = lax.rem(me + k, n)
@@ -67,10 +64,10 @@
         copy.wait()
 
 
-def exchange(chunks, axis, kernel_id):
+def exchange(chunks, spot, where, kernel_id):
     n = chunks.shape[0]
     return pl.pallas_call(
-        functools.partial(exchange_kernel, axis, n),
+        functools.partial(exchange_kernel, n, spot, where),
         out_shape=jax.ShapeDtypeStruct(chunks.shape, chunks.dtype),
         in_specs=[pl.BlockSpec(memory_space=pltpu.VMEM)],
         out_specs=pl.BlockSpec(memory_space=pltpu.VMEM),
@@ -81,6 +78,31 @@
         ],
         compiler_params=pltpu.CompilerParams(collective_id=kernel_id, has_side_effects=True),
     )(chunks)
+
+
+def exp_exchange(sent):
+    exp_at = lambda: lax.axis_index("exp")
+    hid_at = lambda: lax.axis_index("hid")
+    chips = sent.shape[0] // 2
+    across = exchange(
+        sent.reshape((chips, 2) + sent.shape[1:]),
+        lambda: exp_at() // 2,
+        lambda p: (p * 2 + exp_at() % 2, hid_at()),
+        1,
+    )
+    within = exchange(
+        jnp.swapaxes(across, 0, 1),
+        lambda: exp_at() % 2,
+        lambda p: ((exp_at() // 2) * 2 + p, hid_at()),
+        3,
+    )
+    return jnp.swapaxes(within, 0, 1).reshape(sent.shape)
+
+
+def hid_exchange(sent):
+    return exchange(
+        sent, lambda: lax.axis_index("hid"), lambda p: (lax.axis_index("exp"), p), 2
+    )
 
 
 def hid_gather(block):
@@ -226,7 +248,7 @@
     score_grp = split3(score_grp)
     score_grp = jnp.pad(score_grp, ((0, 0), (0, 0), (0, 0), (0, lane - score_grp.shape[3])))
     sent = jnp.concatenate([jnp.swapaxes(part, 0, 1).astype(jnp.bfloat16), score_grp], axis=3)
-    arrived_part = exchange(sent, "exp", 1)
+    arrived_part = exp_exchange(sent)
     sender_block = (jnp.arange(spread_exp, dtype=jnp.int32) * spread_hid + own_hid)[:, None]
     sender_expert = (sender_block * unit_count + jnp.arange(unit_count, dtype=jnp.int32)[None, :]) // 2
     own_combine = lax.dynamic_slice_in_dim(combine_all, own_exp * group_rows, group_rows, 0)
@@ -248,7 +270,7 @@
     hid_sent = jnp.concatenate(
         [group_sum.reshape(spread_hid, tok_local, model_width).astype(jnp.bfloat16), hid_scores], axis=2
     )
-    spread_rows = exchange(hid_sent, "hid", 2)
+    spread_rows = hid_exchange(hid_sent)
     input_sum = jnp.sum(spread_rows[..., :model_width].astype(jnp.float32), axis=0)
     own_scores = join3(spread_rows[..., model_width:], score_cols)
     own_scores = own_scores.reshape(spread_hid, tok_local, spread_exp, unit_count)

time: 204 us -> 210 us (1.029)
  local copies, waits for them, and re-layouts: 13.1 us -> 17.1 us
  Pallas kernels: 56.8 us -> 60.3 us
    pallas_call x2 -> x3, Pallas kernels: 33.9 us -> 37.4 us  [exchange(): pl.pallas_call(functools.partial(exchange_kernel, n, spot, where), out_sh...]
where the time goes in v11:
time: 210 us; the launch traced here: 209 us
  waiting for transfers between devices  92.5 us (44%)
  Pallas kernels  60.3 us (29%)
  local copies, waits for them, and re-layouts  17.1 us (8%)
  between operations  14.4 us (7%)
  starting transfers between devices  9.94 us (5%)
  other arithmetic  9.58 us (5%)
  matrix products  5.58 us (3%)
    all_gather x1, waiting for transfers between devices, on_device(): gathered = lax.all_gather(hid_gather(packed), 'exp', axis=0, tiled=True)  78.6 us
    pallas_call x3, Pallas kernels, exchange(): pl.pallas_call(functools.partial(exchange_kernel, n, spot, where), out_sh...  37.4 us
    all_to_all x1, waiting for transfers between devices, on_device(): lax.all_to_all(jnp.broadcast_to(logit_grad[None], (devices,) + logit_grad...  13.9 us
    pallas_call x1, Pallas kernels, dense_unit(): pl.pallas_call(dense_kernel, grid=(tokens_n // tile,), out_shape=[jax.Sha...  11.5 us
    pallas_call x1, Pallas kernels, hid_gather(): pl.pallas_call(functools.partial(hid_gather_kernel, n), out_shape=jax.Sha...  11.4 us
    all_to_all x1, starting transfers between devices, on_device(): lax.all_to_all(jnp.broadcast_to(logit_grad[None], (devices,) + logit_grad...  9.9 us
    gather x3, local copies, waits for them, and re-layouts, sparse_terms(): take = lambda a: jnp.take_along_axis(a, rows[:, :, None], axis=1)  5.37 us
  transfers between devices with their start and end apart: 2, of which 2 were waited for; matrix products, arithmetic and copies ran while one was open for 1% of the time, Pallas kernels for 0%

profile of v11, /device:TPU:1, one launch (start us, length us, event | category | flops | bytes accessed | tf_op | source)
XLA Modules:
  0.0 209.4 jit_solution(8495930024929133885)
XLA Ops:
  7.3 0.7 bitcast_or_fusion
  8.1 1.5 gather_fusion.1
  9.7 0.1 fusion.54
  9.8 0.2 fusion.37
  10.2 0.6 pad_maximum_fusion.2.x_ref
  10.8 11.4 %shard_map.95 = bf16[8,4,4224]{2,1,0:T(4,128)(2,1)} custom-call(bf16[4,4224]{1,0:T(4,128)(2,1)} %pad_maximum_fusion.2.x_ref), custom_call_target="tpu_custom_call" | custom-call | tf_op jit(solution)/shard_map/pallas_call | solution.py:110
  22.3 1.7 reshape.438
  24.0 0.1 reduce_max.19
  24.2 0.2 fusion.39
  24.4 78.6 %all-gather.2.cloned.1.call-done.x_ref.g_ref = bf16[1024,4224]{1,0:T(8,128)(2,1)} async-done(((bf16[32,4224]{1,0:T(8,128)(2,1)}), bf16[1024,4224]{1,0:T(8,128)(2,1)}) %all-gather.2.cloned.1.call-update) | async-done | bytes 8650768 | tf_op jit(solution)/shard_map/all_gather | solution.py:239
  103.0 1.1 fusion.33
  104.4 0.8 top_k.24
  105.4 0.1 reshape.440
  105.5 0.1 reshape.439
  105.6 11.5 %shard_map.96 = (f32[1024,384]{1,0:T(8,128)}, f32[1024,384]{1,0:T(8,128)}, f32[1024,384]{1,0:T(8,128)}, f32[1024,1]{1,0:T(8,128)}) custom-call(bf16[1024,4224]{1,0:T(8,128)(2,1)} %all-gather.2.cloned.1.call-done.x_ref.g_ref, bf16[1024,4224]{1,0:T(8,128)(2,1)} %all-gather.2.cloned.1.call-done.x_ref.g_ref, bf16[2048,384]{1,0:T(8,128)(2,1)} %bitcast.104, ...), custom_call_target="tpu_custom_call" | custom-call | tf_op jit(solution)/shard_map/pallas_call | solution.py:181
  117.1 1.4 reduce
  118.5 0.1 transpose_reshape_transpose.3
  118.8 2.2 %gather_fusion.3 = f32[128,384]{1,0:T(8,128)S(1)} fusion(f32[1024,384]{1,0:T(8,128)} %get-tuple-element.16, s32[1024]{0:T(1024)S(1)} %pad_clamp_fusion), kind=kCustom, calls=%fused_computation.1.clone | custom fusion | bytes 393728 | tf_op jit(solution)/shard_map/jit(take_along_axis)/gather | solution.py:211
  121.1 0.8 gather_fusion.4
  121.9 2.4 %gather_fusion.2 = f32[128,384]{1,0:T(8,128)S(1)} fusion(f32[1024,384]{1,0:T(8,128)} %get-tuple-element.15, s32[1024]{0:T(1024)S(1)} %pad_clamp_fusion), kind=kCustom, calls=%fused_computation.clone | custom fusion | bytes 393728 | tf_op jit(solution)/shard_map/jit(take_along_axis)/gather | solution.py:211
  124.3 1.0 gather_fusion
  125.3 0.7 fusion.12
  126.0 0.7 copy-done.3
  126.7 0.7 fusion
  127.4 0.2 convert_element_type.152
  127.6 1.1 pad_maximum_fusion.x_ref
  128.7 25.2 %shard_map.97 = bf16[16,2,1,4,2176]{4,3,2,1,0:T(4,128)(2,1)} custom-call(bf16[16,2,1,4,2176]{4,3,2,1,0:T(4,128)(2,1)} %pad_maximum_fusion.x_ref), custom_call_target="tpu_custom_call" | custom-call | tf_op jit(solution)/shard_map/pallas_call | solution.py:69
  153.9 2.1 copy.95
  156.0 4.5 %shard_map.98 = bf16[2,16,1,4,2176]{4,3,2,1,0:T(4,128)(2,1)} custom-call(bf16[2,16,1,4,2176]{4,3,2,1,0:T(4,128)(2,1)} %bitcast.108), custom_call_target="tpu_custom_call" | custom-call | tf_op jit(solution)/shard_map/pallas_call | solution.py:69
  160.5 1.2 copy.78
  162.2 0.3 slice.59
  162.5 0.1 reshape.525
  162.6 0.1 slice-done
  162.7 0.2 fusion.3
  163.0 0.8 top_k.17
  164.1 0.2 convolution_convert_fusion
  164.4 0.7 pad_maximum_fusion.1.x_ref
  165.1 7.6 %shard_map.99 = bf16[8,4,2176]{2,1,0:T(4,128)(2,1)} custom-call(bf16[8,4,2176]{2,1,0:T(4,128)(2,1)} %pad_maximum_fusion.1.x_ref), custom_call_target="tpu_custom_call" | custom-call | tf_op jit(solution)/shard_map/pallas_call | solution.py:69
  172.7 0.9 add_bitcast_fusion
  173.6 0.1 copy.83
  173.7 0.2 reduce_sum.58
  174.0 0.2 multiply_reduce_fusion
  174.2 0.8 broadcast_in_dim.59
  175.0 9.9 %all-to-all-start = ((bf16[256,4,128]{2,1,0:T(4,128)(2,1)}), bf16[256,4,128]{2,1,0:T(4,128)(2,1)S(1)}, u32[]{:S(2)}, u32[]{:S(2)}) async-start(bf16[256,4,128]{2,1,0:T(4,128)(2,1)} %broadcast_in_dim.59), calls=%async_computation | async-start | bytes 524288 | tf_op jit(solution)/shard_map/all_to_all | solution.py:283
  184.9 1.0 convert_reduce_fusion
  185.9 0.9 fusion.1
  186.8 13.9 %all-to-all-done = bf16[256,4,128]{2,1,0:T(4,128)(2,1)S(1)} async-done(((bf16[256,4,128]{2,1,0:T(4,128)(2,1)}), bf16[256,4,128]{2,1,0:T(4,128)(2,1)S(1)}, u32[]{:S(2)}, u32[]{:S(2)}) %all-to-all-start) | async-done | bytes 262176 | tf_op jit(solution)/shard_map/all_to_all | solution.py:283
  200.6 1.9 fusion.4
  (61 shorter events, 2.1 us)
Async XLA Ops:
  7.2 178.7 %copy-start = (bf16[2048,128]{1,0:T(8,128)(2,1)S(1)}, bf16[2048,128]{1,0:T(8,128)(2,1)}, u32[]{:S(2)}) copy-start(bf16[2048,128]{1,0:T(8,128)(2,1)} %param.14) | copy-start | bytes 1572868
  7.2 2.5 %copy-start.5 = (s32[4,8]{1,0:T(4,128)S(1)}, s32[4,8]{1,0:T(4,128)}, u32[]{:S(2)}) copy-start(s32[4,8]{1,0:T(4,128)} %param.13) | copy-start | bytes 388
  7.2 3.0 %copy-start.6 = (bf16[4,2048]{1,0:T(4,128)(2,1)S(1)}, bf16[4,2048]{1,0:T(4,128)(2,1)}, u32[]{:S(2)}) copy-start(bf16[4,2048]{1,0:T(4,128)(2,1)} %param.11) | copy-start | bytes 49156
  7.2 3.0 %copy-start.7 = (bf16[4,2048]{1,0:T(4,128)(2,1)S(1)}, bf16[4,2048]{1,0:T(4,128)(2,1)}, u32[]{:S(2)}) copy-start(bf16[4,2048]{1,0:T(4,128)(2,1)} %param.10) | copy-start | bytes 49156
  7.2 95.8 %all-gather.2.cloned.1.call-start = ((), (), s32[]{:S(2)}) async-start(), calls=%async_computation.1 | async-start | bytes 8921088 | tf_op jit(solution)/shard_map/all_gather | solution.py:239
  8.1 16.0 %copy-start.1 = (f32[4,128]{1,0:T(4,128)S(1)}, f32[4,128]{1,0:T(4,128)}, u32[]{:S(2)}) copy-start(f32[4,128]{1,0:T(4,128)} %param.12) | copy-start | bytes 6148
  117.1 4.0 %copy-start.4 = (f32[1024,384]{1,0:T(8,128)S(1)}, f32[1024,384]{1,0:T(8,128)}, u32[]{:S(2)}) copy-start(f32[1024,384]{1,0:T(8,128)} %get-tuple-element.17) | copy-start | bytes 4718596
  121.9 3.4 %copy-start.2 = (bf16[1,2048,384]{2,1,0:T(8,128)(2,1)S(1)}, bf16[1,2048,384]{2,1,0:T(8,128)(2,1)}, u32[]{:S(2)}) copy-start(bf16[1,2048,384]{2,1,0:T(8,128)(2,1)} %param.15) | copy-start | bytes 4718596
  125.3 1.4 copy-start.3
  161.8 1.0 slice-start
  175.0 25.6 %all-to-all-start = ((bf16[256,4,128]{2,1,0:T(4,128)(2,1)}), bf16[256,4,128]{2,1,0:T(4,128)(2,1)S(1)}, u32[]{:S(2)}, u32[]{:S(2)}) async-start(bf16[256,4,128]{2,1,0:T(4,128)(2,1)} %broadcast_in_dim.59), calls=%async_computation | async-start | bytes 524288 | tf_op jit(solution)/shard_map/all_to_all | solution.py:283
Sparse Core Ops, SparseCore 0:
  24.1 78.8 all-gather.1

commit v12 on v9

--- a/solution.py
+++ b/solution.py
@@ -136,7 +136,17 @@
     return (part(0) + part(1)) + part(2)
 
 
-def dense_kernel(x_ref, g_ref, wg_ref, wu_ref, wd_ref, gate_ref, up_ref, back_ref, score_ref):
+def pick_rows(choice, value):
+    hi = value.astype(jnp.bfloat16)
+    rest = value - hi.astype(jnp.float32)
+    mid = rest.astype(jnp.bfloat16)
+    lo = (rest - mid.astype(jnp.float32)).astype(jnp.bfloat16)
+    dot = lambda piece: jnp.dot(choice, piece, preferred_element_type=jnp.float32)
+    return (dot(hi) + dot(mid)) + dot(lo)
+
+
+def dense_kernel(rows_ref, x_ref, g_ref, wg_ref, wu_ref, wd_ref, score_ref, gate_ref, up_ref, back_ref):
+    step = pl.program_id(0)
     x = x_ref[...]
     gate_pre = jnp.dot(x, wg_ref[...], preferred_element_type=jnp.float32)
     up_pre = jnp.dot(x, wu_ref[...], preferred_element_type=jnp.float32)
@@ -144,50 +154,62 @@
         g_ref[...], wd_ref[...], (((1,), (1,)), ((), ())), preferred_element_type=jnp.float32
     )
     sig_gate = 1.0 / (1.0 + jnp.exp(-gate_pre))
-    gate_ref[...] = gate_pre
-    up_ref[...] = up_pre
-    back_ref[...] = back_grad
     score_ref[...] = jnp.sum(gate_pre * sig_gate * up_pre * back_grad, axis=1, keepdims=True)
-
-
-def dense_unit(gathered, gate_w, up_w, down_w, tile=256):
+    tile = x.shape[0]
+    place = step * tile + lax.broadcasted_iota(jnp.int32, (1, tile), 1)
+    choice = (rows_ref[...] == place).astype(jnp.bfloat16)
+
+    @pl.when(step == 0)
+    def _():
+        gate_ref[...] = jnp.zeros_like(gate_ref)
+        up_ref[...] = jnp.zeros_like(up_ref)
+        back_ref[...] = jnp.zeros_like(back_ref)
+
+    gate_ref[...] += pick_rows(choice, gate_pre)
+    up_ref[...] += pick_rows(choice, up_pre)
+    back_ref[...] += pick_rows(choice, back_grad)
+
+
+def dense_unit(gathered, rows, gate_w, up_w, down_w, tile=256):
     tokens_n = gathered.shape[0]
     width, hidden = gate_w.shape
-    rows = lambda i: (i, 0)
+    slots = rows.shape[0]
+    tiles = lambda i: (i, 0)
     fixed = lambda i: (0, 0)
     f32 = jnp.float32
     return pl.pallas_call(
         dense_kernel,
         grid=(tokens_n // tile,),
         out_shape=[
-            jax.ShapeDtypeStruct((tokens_n, hidden), f32),
-            jax.ShapeDtypeStruct((tokens_n, hidden), f32),
-            jax.ShapeDtypeStruct((tokens_n, hidden), f32),
             jax.ShapeDtypeStruct((tokens_n, 1), f32),
+            jax.ShapeDtypeStruct((slots, hidden), f32),
+            jax.ShapeDtypeStruct((slots, hidden), f32),
+            jax.ShapeDtypeStruct((slots, hidden), f32),
         ],
         in_specs=[
-            pl.BlockSpec((tile, width), rows),
+            pl.BlockSpec((slots, 1), fixed),
+            pl.BlockSpec((tile, width), tiles),
             pl.BlockSpec((tile, width), lambda i: (i, 1)),
             pl.BlockSpec((width, hidden), fixed),
             pl.BlockSpec((width, hidden), fixed),
             pl.BlockSpec((hidden, width), fixed),
         ],
         out_specs=[
-            pl.BlockSpec((tile, hidden), rows),
-            pl.BlockSpec((tile, hidden), rows),
-            pl.BlockSpec((tile, hidden), rows),
-            pl.BlockSpec((tile, 1), rows),
-        ],
-    )(gathered, gathered, gate_w, up_w, down_w)
-
-
-def sparse_terms(gate_pre, up_pre, back_grad, column, w_gate, w_up, group_rows):
+            pl.BlockSpec((tile, 1), tiles),
+            pl.BlockSpec((slots, hidden), fixed),
+            pl.BlockSpec((slots, hidden), fixed),
+            pl.BlockSpec((slots, hidden), fixed),
+        ],
+    )(rows.reshape(slots, 1), gathered, gathered, gate_w, up_w, down_w)
+
+
+def chosen_rows(column, group_rows):
     picked = slot_rows(column, group_rows)
-    groups = picked.shape[1]
-    starts = (jnp.arange(groups, dtype=jnp.int32) * group_rows)[None, :, None]
-    rows = (picked + starts).reshape(picked.shape[0], -1)
-    take = lambda a: jnp.take_along_axis(a, rows[:, :, None], axis=1)
-    gate_s, up_s, back_s = take(gate_pre), take(up_pre), take(back_grad)
+    starts = (jnp.arange(picked.shape[1], dtype=jnp.int32) * group_rows)[None, :, None]
+    return (picked + starts).reshape(picked.shape[0], -1)
+
+
+def sparse_terms(gate_s, up_s, back_s, rows, column, w_gate, w_up):
     col_s = jnp.take_along_axis(column, rows, axis=1)
     sig_gate = jax.nn.sigmoid(gate_s)
     act_gate = gate_s * sig_gate
@@ -196,7 +218,7 @@
     grad_up = (weighted * act_gate).astype(jnp.bfloat16)
     part = jnp.einsum("usf,udf->usd", grad_gate, w_gate, preferred_element_type=jnp.float32)
     part = part + jnp.einsum("usf,udf->usd", grad_up, w_up, preferred_element_type=jnp.float32)
-    return part.reshape(part.shape[0], groups, CAP, part.shape[-1])
+    return part.reshape(part.shape[0], -1, CAP, part.shape[-1])
 
 
 def on_device(tokens, grad_out, router_logits, selected, router_w, w_gate, w_up, w_down):
@@ -216,11 +238,12 @@
     packed = jnp.concatenate([tokens, grad_out, combine], axis=1)
     gathered = lax.all_gather(hid_gather(packed), "exp", axis=0, tiled=True)
     combine_all = gathered[:, 2 * model_width :]
-    dense = [dense_unit(gathered, w_gate[i], w_up[i], w_down[i]) for i in range(unit_count)]
-    gate_pre, up_pre, back_grad = (jnp.stack([d[j] for d in dense]) for j in range(3))
-    score_part = jnp.concatenate([d[3] for d in dense], axis=1)
     column = jnp.dot(combine_all, unit_pick, preferred_element_type=jnp.float32).T
-    part = sparse_terms(gate_pre, up_pre, back_grad, column, w_gate, w_up, group_rows)
+    rows = chosen_rows(column, group_rows)
+    dense = [dense_unit(gathered, rows[i], w_gate[i], w_up[i], w_down[i]) for i in range(unit_count)]
+    score_part = jnp.concatenate([d[0] for d in dense], axis=1)
+    gate_s, up_s, back_s = (jnp.stack([d[j] for d in dense]) for j in (1, 2, 3))
+    part = sparse_terms(gate_s, up_s, back_s, rows, column, w_gate, w_up)
     lane = 128
     score_grp = jnp.swapaxes(score_part.T.reshape(unit_count, spread_exp, CAP, group_rows // CAP), 0, 1)
     score_grp = split3(score_grp)

time: 204 us -> 201 us (0.985)
  local copies, waits for them, and re-layouts: 13.1 us -> 7.62 us
    gather x3 -> x0, local copies, waits for them, and re-layouts: 5.37 us -> none  [sparse_terms(): take = lambda a: jnp.take_along_axis(a, rows[:, :, None], axis=1)]
where the time goes in v12:
time: 201 us
  waiting for transfers between devices  92.5 us (46%)
  Pallas kernels  58.8 us (29%)
  between operations  14.4 us (7%)
  other arithmetic  10.6 us (5%)
  starting transfers between devices  10.1 us (5%)
  local copies, waits for them, and re-layouts  7.62 us (4%)
  matrix products  6.77 us (3%)
    all_gather x1, waiting for transfers between devices, on_device(): gathered = lax.all_gather(hid_gather(packed), 'exp', axis=0, tiled=True)  78.6 us
    pallas_call x2, Pallas kernels, exchange(): pl.pallas_call(functools.partial(exchange_kernel, axis, n), out_shape=jax...  33.9 us
    all_to_all x1, waiting for transfers between devices, on_device(): lax.all_to_all(jnp.broadcast_to(logit_grad[None], (devices,) + logit_grad...  13.9 us
    pallas_call x1, Pallas kernels, dense_unit(): pl.pallas_call(dense_kernel, grid=(tokens_n // tile,), out_shape=[jax.Sha...  13.5 us
    pallas_call x1, Pallas kernels, hid_gather(): pl.pallas_call(functools.partial(hid_gather_kernel, n), out_shape=jax.Sha...  11.4 us
    all_to_all x1, starting transfers between devices, on_device(): lax.all_to_all(jnp.broadcast_to(logit_grad[None], (devices,) + logit_grad...  10 us
  transfers between devices with their start and end apart: 2, of which 2 were waited for; matrix products, arithmetic and copies ran while one was open for 1% of the time, Pallas kernels for 0%

profile of v12, /device:TPU:1, one launch (start us, length us, event | category | flops | bytes accessed | tf_op | source)
XLA Modules:
  0.0 200.7 jit_solution(4837424545140981722)
XLA Ops:
  7.3 0.7 bitcast_or_fusion
  8.1 1.5 gather_fusion.1
  9.7 0.1 fusion.46
  9.8 0.2 fusion.32
  10.1 0.1 select_reduce_fusion
  10.2 0.6 pad_maximum_fusion.2.x_ref
  10.8 11.4 %shard_map.95 = bf16[8,4,4224]{2,1,0:T(4,128)(2,1)} custom-call(bf16[4,4224]{1,0:T(4,128)(2,1)} %pad_maximum_fusion.2.x_ref), custom_call_target="tpu_custom_call" | custom-call | tf_op jit(solution)/shard_map/pallas_call | solution.py:88
  22.3 1.7 reshape.400
  24.0 0.1 reduce_max.19
  24.2 0.2 fusion.34
  24.4 78.6 %all-gather.2.cloned.1.call-done.x_ref.g_ref = bf16[1024,4224]{1,0:T(8,128)(2,1)} async-done(((bf16[32,4224]{1,0:T(8,128)(2,1)}), bf16[1024,4224]{1,0:T(8,128)(2,1)}) %all-gather.2.cloned.1.call-update) | async-done | bytes 8650768 | tf_op jit(solution)/shard_map/all_gather | solution.py:239
  103.0 1.1 fusion.28
  104.1 0.1 ne.69
  104.2 0.1 copy.70
  104.4 0.8 top_k.24
  105.2 0.1 copy.71
  105.3 0.1 reshape.402
  105.4 0.7 copy.73.rows_ref
  106.1 0.1 reshape.401
  106.2 13.5 %shard_map.96 = (f32[1024,1]{1,0:T(8,128)}, f32[128,384]{1,0:T(8,128)}, f32[128,384]{1,0:T(8,128)}, f32[128,384]{1,0:T(8,128)}) custom-call(s32[128,1]{1,0:T(8,128)} %copy.73.rows_ref, bf16[1024,4224]{1,0:T(8,128)(2,1)} %all-gather.2.cloned.1.call-done.x_ref.g_ref, bf16[1024,4224]{1,0:T(8,128)(2,1)} %all-gather.2.cloned.1.call-done.x_ref.g_ref, ...), custom_call_target="tpu_custom_call" | custom-call | tf_op jit(solution)/shard_map/pallas_call | solution.py:180
  119.7 1.2 reduce
  121.0 0.1 transpose_reshape_transpose.3
  121.2 0.1 copy.77
  121.4 1.0 gather_fusion
  122.4 1.9 fusion.6
  124.3 0.6 fusion
  125.0 0.2 convert_element_type.153
  125.2 0.1 fusion.18
  125.3 1.1 pad_maximum_fusion.x_ref
  126.4 26.3 %shard_map.97 = bf16[32,1,4,2176]{3,2,1,0:T(4,128)(2,1)} custom-call(bf16[32,1,4,2176]{3,2,1,0:T(4,128)(2,1)} %pad_maximum_fusion.x_ref), custom_call_target="tpu_custom_call" | custom-call | tf_op jit(solution)/shard_map/pallas_call | solution.py:72
  152.7 1.0 convert_add_fusion
  153.8 0.1 reshape.433
  154.0 0.2 fusion.3
  154.2 0.8 top_k.17
  155.1 0.1 eq.76
  155.3 0.2 convolution_convert_fusion
  155.6 0.7 pad_maximum_fusion.1.x_ref
  156.3 7.6 %shard_map.98 = bf16[8,4,2176]{2,1,0:T(4,128)(2,1)} custom-call(bf16[8,4,2176]{2,1,0:T(4,128)(2,1)} %pad_maximum_fusion.1.x_ref), custom_call_target="tpu_custom_call" | custom-call | tf_op jit(solution)/shard_map/pallas_call | solution.py:72
  163.9 0.9 add_bitcast_fusion
  164.8 0.1 copy.80
  165.0 0.2 reduce_sum.58
  165.2 0.2 multiply_reduce_fusion
  165.5 0.8 broadcast_in_dim.53
  166.3 10.0 %all-to-all-start = ((bf16[256,4,128]{2,1,0:T(4,128)(2,1)}), bf16[256,4,128]{2,1,0:T(4,128)(2,1)S(1)}, u32[]{:S(2)}, u32[]{:S(2)}) async-start(bf16[256,4,128]{2,1,0:T(4,128)(2,1)} %broadcast_in_dim.53), calls=%async_computation | async-start | bytes 524288 | tf_op jit(solution)/shard_map/all_to_all | solution.py:284
  176.3 1.0 convert_reduce_fusion
  177.3 0.9 fusion.1
  178.2 13.9 %all-to-all-done = bf16[256,4,128]{2,1,0:T(4,128)(2,1)S(1)} async-done(((bf16[256,4,128]{2,1,0:T(4,128)(2,1)}), bf16[256,4,128]{2,1,0:T(4,128)(2,1)S(1)}, u32[]{:S(2)}, u32[]{:S(2)}) %all-to-all-start) | async-done | bytes 262176 | tf_op jit(solution)/shard_map/all_to_all | solution.py:284
  192.0 1.9 fusion.4
  (51 shorter events, 1.2 us)
Async XLA Ops:
  7.2 170.1 %copy-start = (bf16[2048,128]{1,0:T(8,128)(2,1)S(1)}, bf16[2048,128]{1,0:T(8,128)(2,1)}, u32[]{:S(2)}) copy-start(bf16[2048,128]{1,0:T(8,128)(2,1)} %param.12) | copy-start | bytes 1572868
  7.2 2.5 %copy-start.6 = (s32[4,8]{1,0:T(4,128)S(1)}, s32[4,8]{1,0:T(4,128)}, u32[]{:S(2)}) copy-start(s32[4,8]{1,0:T(4,128)} %param.11) | copy-start | bytes 388
  7.2 3.0 %copy-start.7 = (bf16[4,2048]{1,0:T(4,128)(2,1)S(1)}, bf16[4,2048]{1,0:T(4,128)(2,1)}, u32[]{:S(2)}) copy-start(bf16[4,2048]{1,0:T(4,128)(2,1)} %param.9) | copy-start | bytes 49156
  7.2 3.0 %copy-start.8 = (bf16[4,2048]{1,0:T(4,128)(2,1)S(1)}, bf16[4,2048]{1,0:T(4,128)(2,1)}, u32[]{:S(2)}) copy-start(bf16[4,2048]{1,0:T(4,128)(2,1)} %param.8) | copy-start | bytes 49156
  7.2 95.8 %all-gather.2.cloned.1.call-start = ((), (), s32[]{:S(2)}) async-start(), calls=%async_computation.1 | async-start | bytes 8921088 | tf_op jit(solution)/shard_map/all_gather | solution.py:239
  8.1 16.0 %copy-start.1 = (f32[4,128]{1,0:T(4,128)S(1)}, f32[4,128]{1,0:T(4,128)}, u32[]{:S(2)}) copy-start(f32[4,128]{1,0:T(4,128)} %param.10) | copy-start | bytes 6148
  106.2 16.1 %copy-start.2 = (bf16[1,2048,384]{2,1,0:T(8,128)(2,1)S(1)}, bf16[1,2048,384]{2,1,0:T(8,128)(2,1)}, u32[]{:S(2)}) copy-start(bf16[1,2048,384]{2,1,0:T(8,128)(2,1)} %param.13) | copy-start | bytes 4718596
  122.4 1.9 copy-start.3
  122.4 1.9 copy-start.4
  122.4 1.9 copy-start.5
  152.7 1.1 slice-start.1
  152.7 1.2 slice-start
  166.3 25.7 %all-to-all-start = ((bf16[256,4,128]{2,1,0:T(4,128)(2,1)}), bf16[256,4,128]{2,1,0:T(4,128)(2,1)S(1)}, u32[]{:S(2)}, u32[]{:S(2)}) async-start(bf16[256,4,128]{2,1,0:T(4,128)(2,1)} %broadcast_in_dim.53), calls=%async_computation | async-start | bytes 524288 | tf_op jit(solution)/shard_map/all_to_all | solution.py:284
Sparse Core Ops, SparseCore 0:
  24.1 78.8 all-gather.1

commit v13 on v12

--- a/solution.py
+++ b/solution.py
@@ -9,6 +9,8 @@
 
 def hid_gather_kernel(n, x_ref, out_ref, local_sem, send_sem, recv_sem):
     me = lax.axis_index("hid")
+    rows = x_ref.shape[0]
+    slot = out_ref.at[pl.ds(pl.multiple_of(me * rows, rows), rows)]
     row = lax.axis_index("exp")
     mesh_ids = pl.DeviceIdType.MESH
     barrier = pltpu.get_barrier_semaphore()
@@ -16,14 +18,14 @@
         peer = lax.rem(me + k, n)
         pl.semaphore_signal(barrier, inc=1, device_id=(row, peer), device_id_type=mesh_ids)
     pl.semaphore_wait(barrier, n - 1)
-    local = pltpu.make_async_copy(x_ref, out_ref.at[me], local_sem)
+    local = pltpu.make_async_copy(x_ref, slot, local_sem)
     local.start()
     copies = []
     for k in range(1, n):
         peer = lax.rem(me + k, n)
         copy = pltpu.make_async_remote_copy(
             src_ref=x_ref,
-            dst_ref=out_ref.at[me],
+            dst_ref=slot,
             send_sem=send_sem.at[k],
             recv_sem=recv_sem.at[k],
             device_id=(row, peer),
@@ -87,7 +89,7 @@
     n = lax.axis_size("hid")
     return pl.pallas_call(
         functools.partial(hid_gather_kernel, n),
-        out_shape=jax.ShapeDtypeStruct((n,) + block.shape, block.dtype),
+        out_shape=jax.ShapeDtypeStruct((n * block.shape[0],) + block.shape[1:], block.dtype),
         in_specs=[pl.BlockSpec(memory_space=pltpu.VMEM)],
         out_specs=pl.BlockSpec(memory_space=pltpu.VMEM),
         scratch_shapes=[
@@ -96,7 +98,7 @@
             pltpu.SemaphoreType.DMA((n,)),
         ],
         compiler_params=pltpu.CompilerParams(collective_id=0, has_side_effects=True),
-    )(block).reshape((n * block.shape[0],) + block.shape[1:])
+    )(block)
 
 
 def softmax_rows(values):

time: 201 us -> 199 us (0.990)
  no operation moved by 1% of the time
where the time goes in v13:
time: 199 us
  waiting for transfers between devices  92.5 us (46%)
  Pallas kernels  58.9 us (30%)
  between operations  14.4 us (7%)
  other arithmetic  10.6 us (5%)
  starting transfers between devices  10.1 us (5%)
  matrix products  6.77 us (3%)
  local copies, waits for them, and re-layouts  5.82 us (3%)
    all_gather x1, waiting for transfers between devices, on_device(): gathered = lax.all_gather(hid_gather(packed), 'exp', axis=0, tiled=True)  78.6 us
    pallas_call x2, Pallas kernels, exchange(): pl.pallas_call(functools.partial(exchange_kernel, axis, n), out_shape=jax...  33.9 us
    all_to_all x1, waiting for transfers between devices, on_device(): lax.all_to_all(jnp.broadcast_to(logit_grad[None], (devices,) + logit_grad...  13.9 us
    pallas_call x1, Pallas kernels, dense_unit(): pl.pallas_call(dense_kernel, grid=(tokens_n // tile,), out_shape=[jax.Sha...  13.5 us
    pallas_call x1, Pallas kernels, hid_gather(): pl.pallas_call(functools.partial(hid_gather_kernel, n), out_shape=jax.Sha...  11.5 us
    all_to_all x1, starting transfers between devices, on_device(): lax.all_to_all(jnp.broadcast_to(logit_grad[None], (devices,) + logit_grad...  10 us
  transfers between devices with their start and end apart: 2, of which 2 were waited for; matrix products, arithmetic and copies ran while one was open for 1% of the time, Pallas kernels for 0%

profile of v13, /device:TPU:1, one launch (start us, length us, event | category | flops | bytes accessed | tf_op | source)
XLA Modules:
  0.0 199.0 jit_solution(3176500602205491199)
XLA Ops:
  7.3 0.7 bitcast_or_fusion
  8.1 1.4 gather_fusion.1
  9.6 0.1 fusion.46
  9.7 0.2 fusion.32
  10.0 0.1 select_reduce_fusion
  10.1 0.6 pad_maximum_fusion.2.x_ref
  10.7 11.5 %shard_map.95 = bf16[32,4224]{1,0:T(8,128)(2,1)} custom-call(bf16[4,4224]{1,0:T(4,128)(2,1)} %pad_maximum_fusion.2.x_ref), custom_call_target="tpu_custom_call" | custom-call | tf_op jit(solution)/shard_map/pallas_call | solution.py:90
  22.3 0.1 reduce_max.19
  22.4 0.2 fusion.34
  22.6 78.6 %all-gather.2.cloned.1.call-done.x_ref.g_ref = bf16[1024,4224]{1,0:T(8,128)(2,1)} async-done(((bf16[32,4224]{1,0:T(8,128)(2,1)}), bf16[1024,4224]{1,0:T(8,128)(2,1)}) %all-gather.2.cloned.1.call-update) | async-done | bytes 8650768 | tf_op jit(solution)/shard_map/all_gather | solution.py:241
  101.2 1.1 fusion.28
  102.3 0.1 ne.69
  102.4 0.1 copy.70
  102.6 0.8 top_k.24
  103.4 0.1 copy.71
  103.5 0.1 reshape.398
  103.6 0.7 copy.73.rows_ref
  104.3 0.1 reshape.397
  104.5 13.5 %shard_map.96 = (f32[1024,1]{1,0:T(8,128)}, f32[128,384]{1,0:T(8,128)}, f32[128,384]{1,0:T(8,128)}, f32[128,384]{1,0:T(8,128)}) custom-call(s32[128,1]{1,0:T(8,128)} %copy.73.rows_ref, bf16[1024,4224]{1,0:T(8,128)(2,1)} %all-gather.2.cloned.1.call-done.x_ref.g_ref, bf16[1024,4224]{1,0:T(8,128)(2,1)} %all-gather.2.cloned.1.call-done.x_ref.g_ref, ...), custom_call_target="tpu_custom_call" | custom-call | tf_op jit(solution)/shard_map/pallas_call | solution.py:182
  117.9 1.2 reduce
  119.2 0.1 transpose_reshape_transpose.3
  119.4 0.1 copy.77
  119.6 1.0 gather_fusion
  120.6 1.9 fusion.6
  122.5 0.6 fusion
  123.2 0.2 convert_element_type.153
  123.4 0.1 fusion.18
  123.5 1.1 pad_maximum_fusion.x_ref
  124.6 26.3 %shard_map.97 = bf16[32,1,4,2176]{3,2,1,0:T(4,128)(2,1)} custom-call(bf16[32,1,4,2176]{3,2,1,0:T(4,128)(2,1)} %pad_maximum_fusion.x_ref), custom_call_target="tpu_custom_call" | custom-call | tf_op jit(solution)/shard_map/pallas_call | solution.py:74
  151.0 1.0 convert_add_fusion
  152.1 0.1 reshape.429
  152.2 0.2 fusion.3
  152.4 0.8 top_k.17
  153.3 0.1 copy.69
  153.4 0.1 eq.76
  153.5 0.2 convolution_convert_fusion
  153.8 0.7 pad_maximum_fusion.1.x_ref
  154.5 7.6 %shard_map.98 = bf16[8,4,2176]{2,1,0:T(4,128)(2,1)} custom-call(bf16[8,4,2176]{2,1,0:T(4,128)(2,1)} %pad_maximum_fusion.1.x_ref), custom_call_target="tpu_custom_call" | custom-call | tf_op jit(solution)/shard_map/pallas_call | solution.py:74
  162.2 0.9 add_bitcast_fusion
  163.1 0.1 copy.80
  163.2 0.2 reduce_sum.58
  163.4 0.2 multiply_reduce_fusion
  163.7 0.8 broadcast_in_dim.53
  164.5 10.0 %all-to-all-start = ((bf16[256,4,128]{2,1,0:T(4,128)(2,1)}), bf16[256,4,128]{2,1,0:T(4,128)(2,1)S(1)}, u32[]{:S(2)}, u32[]{:S(2)}) async-start(bf16[256,4,128]{2,1,0:T(4,128)(2,1)} %broadcast_in_dim.53), calls=%async_computation | async-start | bytes 524288 | tf_op jit(solution)/shard_map/all_to_all | solution.py:286
  174.5 1.0 convert_reduce_fusion
  175.5 0.9 fusion.1
  176.4 13.9 %all-to-all-done = bf16[256,4,128]{2,1,0:T(4,128)(2,1)S(1)} async-done(((bf16[256,4,128]{2,1,0:T(4,128)(2,1)}), bf16[256,4,128]{2,1,0:T(4,128)(2,1)S(1)}, u32[]{:S(2)}, u32[]{:S(2)}) %all-to-all-start) | async-done | bytes 262176 | tf_op jit(solution)/shard_map/all_to_all | solution.py:286
  190.2 1.9 fusion.4
  (50 shorter events, 1.1 us)
Async XLA Ops:
  7.2 168.3 %copy-start = (bf16[2048,128]{1,0:T(8,128)(2,1)S(1)}, bf16[2048,128]{1,0:T(8,128)(2,1)}, u32[]{:S(2)}) copy-start(bf16[2048,128]{1,0:T(8,128)(2,1)} %param.12) | copy-start | bytes 1572868
  7.2 2.4 %copy-start.6 = (s32[4,8]{1,0:T(4,128)S(1)}, s32[4,8]{1,0:T(4,128)}, u32[]{:S(2)}) copy-start(s32[4,8]{1,0:T(4,128)} %param.11) | copy-start | bytes 388
  7.2 15.1 %copy-start.1 = (f32[4,128]{1,0:T(4,128)S(1)}, f32[4,128]{1,0:T(4,128)}, u32[]{:S(2)}) copy-start(f32[4,128]{1,0:T(4,128)} %param.10) | copy-start | bytes 6148
  7.2 2.9 %copy-start.7 = (bf16[4,2048]{1,0:T(4,128)(2,1)S(1)}, bf16[4,2048]{1,0:T(4,128)(2,1)}, u32[]{:S(2)}) copy-start(bf16[4,2048]{1,0:T(4,128)(2,1)} %param.9) | copy-start | bytes 49156
  7.2 2.9 %copy-start.8 = (bf16[4,2048]{1,0:T(4,128)(2,1)S(1)}, bf16[4,2048]{1,0:T(4,128)(2,1)}, u32[]{:S(2)}) copy-start(bf16[4,2048]{1,0:T(4,128)(2,1)} %param.8) | copy-start | bytes 49156
  7.2 94.0 %all-gather.2.cloned.1.call-start = ((), (), s32[]{:S(2)}) async-start(), calls=%async_computation.1 | async-start | bytes 8921088 | tf_op jit(solution)/shard_map/all_gather | solution.py:241
  104.5 16.1 %copy-start.2 = (bf16[1,2048,384]{2,1,0:T(8,128)(2,1)S(1)}, bf16[1,2048,384]{2,1,0:T(8,128)(2,1)}, u32[]{:S(2)}) copy-start(bf16[1,2048,384]{2,1,0:T(8,128)(2,1)} %param.13) | copy-start | bytes 4718596
  120.6 1.9 copy-start.3
  120.6 1.9 copy-start.4
  120.6 1.9 copy-start.5
  150.9 1.1 slice-start.1
  150.9 1.2 slice-start
  164.5 25.7 %all-to-all-start = ((bf16[256,4,128]{2,1,0:T(4,128)(2,1)}), bf16[256,4,128]{2,1,0:T(4,128)(2,1)S(1)}, u32[]{:S(2)}, u32[]{:S(2)}) async-start(bf16[256,4,128]{2,1,0:T(4,128)(2,1)} %broadcast_in_dim.53), calls=%async_computation | async-start | bytes 524288 | tf_op jit(solution)/shard_map/all_to_all | solution.py:286
Sparse Core Ops, SparseCore 0:
  22.4 78.8 all-gather.1

commit v14 on v13

--- a/solution.py
+++ b/solution.py
@@ -172,7 +172,7 @@
     back_ref[...] += pick_rows(choice, back_grad)
 
 
-def dense_unit(gathered, rows, gate_w, up_w, down_w, tile=256):
+def dense_unit(gathered, rows, gate_w, up_w, down_w, tile=512):
     tokens_n = gathered.shape[0]
     width, hidden = gate_w.shape
     slots = rows.shape[0]

time: 199 us -> 199 us (level)
  no operation moved by 1% of the time
where the time goes in v14:
time: 199 us
  waiting for transfers between devices  92.5 us (46%)
  Pallas kernels  58.6 us (29%)
  between operations  14.4 us (7%)
  other arithmetic  10.6 us (5%)
  starting transfers between devices  10.1 us (5%)
  matrix products  6.78 us (3%)
  local copies, waits for them, and re-layouts  5.82 us (3%)
    all_gather x1, waiting for transfers between devices, on_device(): gathered = lax.all_gather(hid_gather(packed), 'exp', axis=0, tiled=True)  78.6 us
    pallas_call x2, Pallas kernels, exchange(): pl.pallas_call(functools.partial(exchange_kernel, axis, n), out_shape=jax...  33.9 us
    all_to_all x1, waiting for transfers between devices, on_device(): lax.all_to_all(jnp.broadcast_to(logit_grad[None], (devices,) + logit_grad...  13.9 us
    pallas_call x1, Pallas kernels, dense_unit(): pl.pallas_call(dense_kernel, grid=(tokens_n // tile,), out_shape=[jax.Sha...  13.2 us
    pallas_call x1, Pallas kernels, hid_gather(): pl.pallas_call(functools.partial(hid_gather_kernel, n), out_shape=jax.Sha...  11.5 us
    all_to_all x1, starting transfers between devices, on_device(): lax.all_to_all(jnp.broadcast_to(logit_grad[None], (devices,) + logit_grad...  10 us
  transfers between devices with their start and end apart: 2, of which 2 were waited for; matrix products, arithmetic and copies ran while one was open for 1% of the time, Pallas kernels for 0%

profile of v14, /device:TPU:1, one launch (start us, length us, event | category | flops | bytes accessed | tf_op | source)
XLA Modules:
  0.0 198.8 jit_solution(16720167445308625376)
XLA Ops:
  7.3 0.7 bitcast_or_fusion
  8.1 1.4 gather_fusion.1
  9.6 0.1 fusion.46
  9.7 0.2 fusion.32
  10.0 0.1 select_reduce_fusion
  10.1 0.6 pad_maximum_fusion.2.x_ref
  10.7 11.5 %shard_map.95 = bf16[32,4224]{1,0:T(8,128)(2,1)} custom-call(bf16[4,4224]{1,0:T(4,128)(2,1)} %pad_maximum_fusion.2.x_ref), custom_call_target="tpu_custom_call" | custom-call | tf_op jit(solution)/shard_map/pallas_call | solution.py:90
  22.3 0.1 reduce_max.19
  22.4 0.2 fusion.34
  22.6 78.6 %all-gather.2.cloned.1.call-done.x_ref.g_ref = bf16[1024,4224]{1,0:T(8,128)(2,1)} async-done(((bf16[32,4224]{1,0:T(8,128)(2,1)}), bf16[1024,4224]{1,0:T(8,128)(2,1)}) %all-gather.2.cloned.1.call-update) | async-done | bytes 8650768 | tf_op jit(solution)/shard_map/all_gather | solution.py:241
  101.2 1.1 fusion.28
  102.3 0.1 ne.69
  102.4 0.1 copy.70
  102.6 0.8 top_k.24
  103.4 0.1 copy.71
  103.5 0.1 reshape.398
  103.6 0.7 copy.73.rows_ref
  104.3 0.1 reshape.397
  104.5 13.2 %shard_map.96 = (f32[1024,1]{1,0:T(8,128)}, f32[128,384]{1,0:T(8,128)}, f32[128,384]{1,0:T(8,128)}, f32[128,384]{1,0:T(8,128)}) custom-call(s32[128,1]{1,0:T(8,128)} %copy.73.rows_ref, bf16[1024,4224]{1,0:T(8,128)(2,1)} %all-gather.2.cloned.1.call-done.x_ref.g_ref, bf16[1024,4224]{1,0:T(8,128)(2,1)} %all-gather.2.cloned.1.call-done.x_ref.g_ref, ...), custom_call_target="tpu_custom_call" | custom-call | tf_op jit(solution)/shard_map/pallas_call | solution.py:182
  117.7 1.2 reduce
  119.0 0.1 transpose_reshape_transpose.3
  119.2 0.1 copy.77
  119.3 1.0 gather_fusion
  120.4 1.9 fusion.6
  122.3 0.6 fusion
  123.0 0.2 convert_element_type.153
  123.2 0.1 fusion.18
  123.3 1.1 pad_maximum_fusion.x_ref
  124.4 26.3 %shard_map.97 = bf16[32,1,4,2176]{3,2,1,0:T(4,128)(2,1)} custom-call(bf16[32,1,4,2176]{3,2,1,0:T(4,128)(2,1)} %pad_maximum_fusion.x_ref), custom_call_target="tpu_custom_call" | custom-call | tf_op jit(solution)/shard_map/pallas_call | solution.py:74
  150.7 1.0 convert_add_fusion
  151.8 0.1 reshape.429
  152.0 0.2 fusion.3
  152.2 0.8 top_k.17
  153.0 0.1 copy.69
  153.1 0.1 eq.76
  153.3 0.2 convolution_convert_fusion
  153.6 0.7 pad_maximum_fusion.1.x_ref
  154.3 7.6 %shard_map.98 = bf16[8,4,2176]{2,1,0:T(4,128)(2,1)} custom-call(bf16[8,4,2176]{2,1,0:T(4,128)(2,1)} %pad_maximum_fusion.1.x_ref), custom_call_target="tpu_custom_call" | custom-call | tf_op jit(solution)/shard_map/pallas_call | solution.py:74
  161.9 0.9 add_bitcast_fusion
  162.8 0.1 copy.80
  163.0 0.2 reduce_sum.58
  163.2 0.2 multiply_reduce_fusion
  163.5 0.8 broadcast_in_dim.53
  164.3 10.0 %all-to-all-start = ((bf16[256,4,128]{2,1,0:T(4,128)(2,1)}), bf16[256,4,128]{2,1,0:T(4,128)(2,1)S(1)}, u32[]{:S(2)}, u32[]{:S(2)}) async-start(bf16[256,4,128]{2,1,0:T(4,128)(2,1)} %broadcast_in_dim.53), calls=%async_computation | async-start | bytes 524288 | tf_op jit(solution)/shard_map/all_to_all | solution.py:286
  174.3 1.0 convert_reduce_fusion
  175.3 0.9 fusion.1
  176.2 13.9 %all-to-all-done = bf16[256,4,128]{2,1,0:T(4,128)(2,1)S(1)} async-done(((bf16[256,4,128]{2,1,0:T(4,128)(2,1)}), bf16[256,4,128]{2,1,0:T(4,128)(2,1)S(1)}, u32[]{:S(2)}, u32[]{:S(2)}) %all-to-all-start) | async-done | bytes 262176 | tf_op jit(solution)/shard_map/all_to_all | solution.py:286
  190.0 1.9 fusion.4
  (50 shorter events, 1.1 us)
Async XLA Ops:
  7.2 168.1 %copy-start = (bf16[2048,128]{1,0:T(8,128)(2,1)S(1)}, bf16[2048,128]{1,0:T(8,128)(2,1)}, u32[]{:S(2)}) copy-start(bf16[2048,128]{1,0:T(8,128)(2,1)} %param.12) | copy-start | bytes 1572868
  7.2 2.4 %copy-start.6 = (s32[4,8]{1,0:T(4,128)S(1)}, s32[4,8]{1,0:T(4,128)}, u32[]{:S(2)}) copy-start(s32[4,8]{1,0:T(4,128)} %param.11) | copy-start | bytes 388
  7.2 15.1 %copy-start.1 = (f32[4,128]{1,0:T(4,128)S(1)}, f32[4,128]{1,0:T(4,128)}, u32[]{:S(2)}) copy-start(f32[4,128]{1,0:T(4,128)} %param.10) | copy-start | bytes 6148
  7.2 2.9 %copy-start.7 = (bf16[4,2048]{1,0:T(4,128)(2,1)S(1)}, bf16[4,2048]{1,0:T(4,128)(2,1)}, u32[]{:S(2)}) copy-start(bf16[4,2048]{1,0:T(4,128)(2,1)} %param.9) | copy-start | bytes 49156
  7.2 2.9 %copy-start.8 = (bf16[4,2048]{1,0:T(4,128)(2,1)S(1)}, bf16[4,2048]{1,0:T(4,128)(2,1)}, u32[]{:S(2)}) copy-start(bf16[4,2048]{1,0:T(4,128)(2,1)} %param.8) | copy-start | bytes 49156
  7.2 94.0 %all-gather.2.cloned.1.call-start = ((), (), s32[]{:S(2)}) async-start(), calls=%async_computation.1 | async-start | bytes 8921088 | tf_op jit(solution)/shard_map/all_gather | solution.py:241
  104.5 15.9 %copy-start.2 = (bf16[1,2048,384]{2,1,0:T(8,128)(2,1)S(1)}, bf16[1,2048,384]{2,1,0:T(8,128)(2,1)}, u32[]{:S(2)}) copy-start(bf16[1,2048,384]{2,1,0:T(8,128)(2,1)} %param.13) | copy-start | bytes 4718596
  120.3 2.0 copy-start.3
  120.4 2.0 copy-start.4
  120.4 2.0 copy-start.5
  150.7 1.1 slice-start.1
  150.7 1.2 slice-start
  164.3 25.8 %all-to-all-start = ((bf16[256,4,128]{2,1,0:T(4,128)(2,1)}), bf16[256,4,128]{2,1,0:T(4,128)(2,1)S(1)}, u32[]{:S(2)}, u32[]{:S(2)}) async-start(bf16[256,4,128]{2,1,0:T(4,128)(2,1)} %broadcast_in_dim.53), calls=%async_computation | async-start | bytes 524288 | tf_op jit(solution)/shard_map/all_to_all | solution.py:286
Sparse Core Ops, SparseCore 0:
  22.4 78.8 all-gather.1

commit v15 on v13

--- a/solution.py
+++ b/solution.py
@@ -85,7 +85,7 @@
     )(chunks)
 
 
-def hid_gather(block):
+def hid_gather(block, kernel_id=0):
     n = lax.axis_size("hid")
     return pl.pallas_call(
         functools.partial(hid_gather_kernel, n),
@@ -97,7 +97,7 @@
             pltpu.SemaphoreType.DMA((n,)),
             pltpu.SemaphoreType.DMA((n,)),
         ],
-        compiler_params=pltpu.CompilerParams(collective_id=0, has_side_effects=True),
+        compiler_params=pltpu.CompilerParams(collective_id=kernel_id, has_side_effects=True),
     )(block)
 
 
@@ -283,8 +283,9 @@
     mean_score = jnp.sum(probs_all * expert_scores, axis=1, keepdims=True)
     logit_grad = (probs_all * (expert_scores - mean_score)).astype(jnp.bfloat16)
     devices = spread_exp * spread_hid
-    logit_all = lax.all_to_all(
-        jnp.broadcast_to(logit_grad[None], (devices,) + logit_grad.shape), ("exp", "hid"), 0, 0, tiled=True
+    near_logit = hid_gather(logit_grad, 3)
+    logit_all = exchange(
+        jnp.broadcast_to(near_logit[None], (spread_exp,) + near_logit.shape), "exp", 4
     ).reshape(-1, expert_count)
     grad_rows = model_width // devices
     token_cols = lax.dynamic_slice_in_dim(gathered, own_block * grad_rows, grad_rows, 1)

time: 199 us -> 203 us (1.020)
  Pallas kernels: 58.9 us -> 84 us
  waiting for transfers between devices: 92.5 us -> 78.6 us
  starting transfers between devices: 10.1 us -> 0.04 us
    pallas_call x2 -> x3, Pallas kernels: 33.9 us -> 52.3 us  [exchange(): pl.pallas_call(functools.partial(exchange_kernel, axis, n), out_shape=jax...]
    all_to_all x1 -> x0, waiting for transfers between devices: 13.9 us -> none  [on_device(): lax.all_to_all(jnp.broadcast_to(logit_grad[None], (devices,) + logit_grad...]
    all_to_all x1 -> x0, starting transfers between devices: 10 us -> none  [on_device(): lax.all_to_all(jnp.broadcast_to(logit_grad[None], (devices,) + logit_grad...]
    pallas_call x1 -> x2, Pallas kernels: 11.5 us -> 18.2 us  [hid_gather(): pl.pallas_call(functools.partial(hid_gather_kernel, n), out_shape=jax.Sha...]
  transfers between devices with their start and end apart: 2 -> 1, of which waited for: 2 -> 1; matrix products, arithmetic and copies ran while one was open for 1% -> 0% of each run, Pallas kernels for 0% -> 0%
where the time goes in v15:
time: 203 us; the launch traced here: 202 us
  Pallas kernels  84 us (41%)
  waiting for transfers between devices  78.6 us (39%)
  between operations  14.4 us (7%)
  other arithmetic  11.1 us (5%)
  matrix products  7.54 us (4%)
  local copies, waits for them, and re-layouts  6.47 us (3%)
    all_gather x1, waiting for transfers between devices, on_device(): gathered = lax.all_gather(hid_gather(packed), 'exp', axis=0, tiled=True)  78.6 us
    pallas_call x3, Pallas kernels, exchange(): pl.pallas_call(functools.partial(exchange_kernel, axis, n), out_shape=jax...  52.3 us
    pallas_call x2, Pallas kernels, hid_gather(): pl.pallas_call(functools.partial(hid_gather_kernel, n), out_shape=jax.Sha...  18.2 us
    pallas_call x1, Pallas kernels, dense_unit(): pl.pallas_call(dense_kernel, grid=(tokens_n // tile,), out_shape=[jax.Sha...  13.5 us
  transfers between devices with their start and end apart: 1, of which 1 were waited for; matrix products, arithmetic and copies ran while one was open for 0% of the time, Pallas kernels for 0%

profile of v15, /device:TPU:1, one launch (start us, length us, event | category | flops | bytes accessed | tf_op | source)
XLA Modules:
  0.0 202.2 jit_solution(17340397947600887731)
XLA Ops:
  7.3 0.7 bitcast_or_fusion
  8.1 1.4 gather_fusion.1
  9.6 0.1 fusion.46
  9.7 0.2 fusion.32
  10.0 0.1 select_reduce_fusion
  10.1 0.6 pad_maximum_fusion.2.x_ref
  10.7 11.5 %shard_map.95 = bf16[32,4224]{1,0:T(8,128)(2,1)} custom-call(bf16[4,4224]{1,0:T(4,128)(2,1)} %pad_maximum_fusion.2.x_ref), custom_call_target="tpu_custom_call" | custom-call | tf_op jit(solution)/shard_map/pallas_call | solution.py:90
  22.3 0.1 reduce_max.19
  22.4 0.2 fusion.34
  22.6 78.6 %all-gather.2.cloned.1.call-done.x_ref.g_ref = bf16[1024,4224]{1,0:T(8,128)(2,1)} async-done(((bf16[32,4224]{1,0:T(8,128)(2,1)}), bf16[1024,4224]{1,0:T(8,128)(2,1)}) %all-gather.2.cloned.1.call-update) | async-done | bytes 8650768 | tf_op jit(solution)/shard_map/all_gather | solution.py:241
  101.2 1.1 fusion.28
  102.3 0.1 ne.69
  102.4 0.1 copy.62
  102.6 0.8 top_k.24
  103.5 0.1 reshape.398
  103.6 0.7 copy.65.rows_ref
  104.3 0.1 reshape.397
  104.5 13.5 %shard_map.96 = (f32[1024,1]{1,0:T(8,128)}, f32[128,384]{1,0:T(8,128)}, f32[128,384]{1,0:T(8,128)}, f32[128,384]{1,0:T(8,128)}) custom-call(s32[128,1]{1,0:T(8,128)} %copy.65.rows_ref, bf16[1024,4224]{1,0:T(8,128)(2,1)} %all-gather.2.cloned.1.call-done.x_ref.g_ref, bf16[1024,4224]{1,0:T(8,128)(2,1)} %all-gather.2.cloned.1.call-done.x_ref.g_ref, ...), custom_call_target="tpu_custom_call" | custom-call | tf_op jit(solution)/shard_map/pallas_call | solution.py:182
  117.9 1.2 reduce
  119.2 0.1 transpose_reshape_transpose.3
  119.4 0.1 copy.69
  119.6 1.0 gather_fusion
  120.6 1.9 fusion.6
  122.5 0.6 fusion
  123.2 0.2 convert_element_type.153
  123.4 0.1 fusion.18
  123.5 1.1 pad_maximum_fusion.x_ref
  124.6 26.3 %shard_map.97 = bf16[32,1,4,2176]{3,2,1,0:T(4,128)(2,1)} custom-call(bf16[32,1,4,2176]{3,2,1,0:T(4,128)(2,1)} %pad_maximum_fusion.x_ref), custom_call_target="tpu_custom_call" | custom-call | tf_op jit(solution)/shard_map/pallas_call | solution.py:74
  151.0 1.0 convert_add_fusion
  152.1 0.1 reshape.429
  152.2 0.2 fusion.3
  152.4 0.8 top_k.17
  153.3 0.1 copy.61
  153.4 0.1 eq.76
  153.5 0.2 convolution_convert_fusion
  153.8 0.7 pad_maximum_fusion.1.x_ref
  154.5 7.6 %shard_map.98 = bf16[8,4,2176]{2,1,0:T(4,128)(2,1)} custom-call(bf16[8,4,2176]{2,1,0:T(4,128)(2,1)} %pad_maximum_fusion.1.x_ref), custom_call_target="tpu_custom_call" | custom-call | tf_op jit(solution)/shard_map/pallas_call | solution.py:74
  162.2 1.0 convert_reduce_fusion
  163.1 0.9 add_bitcast_fusion
  164.0 0.1 copy.72
  164.2 0.2 reduce_sum.58
  164.4 0.2 multiply_reduce_fusion
  164.6 0.6 multiply_convert_fusion.4.x_ref
  165.3 6.7 %shard_map.99 = bf16[32,128]{1,0:T(8,128)(2,1)} custom-call(bf16[4,128]{1,0:T(4,128)(2,1)} %multiply_convert_fusion.4.x_ref), custom_call_target="tpu_custom_call" | custom-call | tf_op jit(solution)/shard_map/pallas_call | solution.py:90
  172.0 1.4 broadcast_in_dim.53.x_ref
  173.4 18.4 %shard_map.100 = bf16[32,32,128]{2,1,0:T(8,128)(2,1)} custom-call(bf16[32,32,128]{2,1,0:T(8,128)(2,1)} %broadcast_in_dim.53.x_ref), custom_call_target="tpu_custom_call" | custom-call | tf_op jit(solution)/shard_map/pallas_call | solution.py:74
  191.8 1.5 fusion.1
  193.4 2.0 fusion.4
  (50 shorter events, 1.1 us)
Async XLA Ops:
  7.2 184.6 %copy-start = (bf16[2048,128]{1,0:T(8,128)(2,1)S(1)}, bf16[2048,128]{1,0:T(8,128)(2,1)}, u32[]{:S(2)}) copy-start(bf16[2048,128]{1,0:T(8,128)(2,1)} %param.12) | copy-start | bytes 1572868
  7.2 2.4 %copy-start.6 = (s32[4,8]{1,0:T(4,128)S(1)}, s32[4,8]{1,0:T(4,128)}, u32[]{:S(2)}) copy-start(s32[4,8]{1,0:T(4,128)} %param.11) | copy-start | bytes 388
  7.2 15.1 %copy-start.1 = (f32[4,128]{1,0:T(4,128)S(1)}, f32[4,128]{1,0:T(4,128)}, u32[]{:S(2)}) copy-start(f32[4,128]{1,0:T(4,128)} %param.10) | copy-start | bytes 6148
  7.2 2.9 %copy-start.7 = (bf16[4,2048]{1,0:T(4,128)(2,1)S(1)}, bf16[4,2048]{1,0:T(4,128)(2,1)}, u32[]{:S(2)}) copy-start(bf16[4,2048]{1,0:T(4,128)(2,1)} %param.9) | copy-start | bytes 49156
  7.2 2.9 %copy-start.8 = (bf16[4,2048]{1,0:T(4,128)(2,1)S(1)}, bf16[4,2048]{1,0:T(4,128)(2,1)}, u32[]{:S(2)}) copy-start(bf16[4,2048]{1,0:T(4,128)(2,1)} %param.8) | copy-start | bytes 49156
  7.2 94.0 %all-gather.2.cloned.1.call-start = ((), (), s32[]{:S(2)}) async-start(), calls=%async_computation | async-start | bytes 8921088 | tf_op jit(solution)/shard_map/all_gather | solution.py:241
  104.5 16.1 %copy-start.2 = (bf16[1,2048,384]{2,1,0:T(8,128)(2,1)S(1)}, bf16[1,2048,384]{2,1,0:T(8,128)(2,1)}, u32[]{:S(2)}) copy-start(bf16[1,2048,384]{2,1,0:T(8,128)(2,1)} %param.13) | copy-start | bytes 4718596
  120.6 1.9 copy-start.3
  120.6 1.9 copy-start.4
  120.6 1.9 copy-start.5
  150.9 1.1 slice-start.1
  150.9 1.2 slice-start
Sparse Core Ops, SparseCore 0:
  22.4 78.8 all-gather.1

commit v16 on v13

--- a/solution.py
+++ b/solution.py
@@ -238,7 +238,8 @@
     unit_pick = (expert_ids[:, None] == unit_expert[None, :]).astype(jnp.bfloat16)
     combine = combine_table(router_logits, selected, expert_count)
     packed = jnp.concatenate([tokens, grad_out, combine], axis=1)
-    gathered = lax.all_gather(hid_gather(packed), "exp", axis=0, tiled=True)
+    near = hid_gather(packed)
+    gathered = lax.all_gather(near, "exp", axis=0, tiled=True)
     combine_all = gathered[:, 2 * model_width :]
     column = jnp.dot(combine_all, unit_pick, preferred_element_type=jnp.float32).T
     rows = chosen_rows(column, group_rows)
@@ -254,7 +255,7 @@
     arrived_part = exchange(sent, "exp", 1)
     sender_block = (jnp.arange(spread_exp, dtype=jnp.int32) * spread_hid + own_hid)[:, None]
     sender_expert = (sender_block * unit_count + jnp.arange(unit_count, dtype=jnp.int32)[None, :]) // 2
-    own_combine = lax.dynamic_slice_in_dim(combine_all, own_exp * group_rows, group_rows, 0)
+    own_combine = near[:, 2 * model_width :]
     sender_pick = (expert_ids[:, None] == sender_expert.reshape(1, -1)).astype(jnp.bfloat16)
     sender_column = jnp.dot(own_combine, sender_pick, preferred_element_type=jnp.float32).T
     sender_rows = slot_rows(sender_column, group_rows).reshape(-1)

time: 199 us -> 198 us (level)
  waiting for transfers between devices: 92.5 us -> 90.4 us
    all_gather x1, waiting for transfers between devices: 78.6 us -> 76.6 us  [on_device(): gathered = lax.all_gather(near, 'exp', axis=0, tiled=True)]
  transfers between devices with their start and end apart: 2 -> 2, of which waited for: 2 -> 2; matrix products, arithmetic and copies ran while one was open for 1% -> 2% of each run, Pallas kernels for 0% -> 0%
where the time goes in v16:
time: 198 us
  waiting for transfers between devices  90.4 us (46%)
  Pallas kernels  58.8 us (30%)
  between operations  14.4 us (7%)
  other arithmetic  10.6 us (5%)
  starting transfers between devices  10.1 us (5%)
  matrix products  7.49 us (4%)
  local copies, waits for them, and re-layouts  5.81 us (3%)
    all_gather x1, waiting for transfers between devices, on_device(): gathered = lax.all_gather(near, 'exp', axis=0, tiled=True)  76.6 us
    pallas_call x2, Pallas kernels, exchange(): pl.pallas_call(functools.partial(exchange_kernel, axis, n), out_shape=jax...  33.9 us
    all_to_all x1, waiting for transfers between devices, on_device(): lax.all_to_all(jnp.broadcast_to(logit_grad[None], (devices,) + logit_grad...  13.9 us
    pallas_call x1, Pallas kernels, dense_unit(): pl.pallas_call(dense_kernel, grid=(tokens_n // tile,), out_shape=[jax.Sha...  13.5 us
    pallas_call x1, Pallas kernels, hid_gather(): pl.pallas_call(functools.partial(hid_gather_kernel, n), out_shape=jax.Sha...  11.5 us
    all_to_all x1, starting transfers between devices, on_device(): lax.all_to_all(jnp.broadcast_to(logit_grad[None], (devices,) + logit_grad...  10 us
  transfers between devices with their start and end apart: 2, of which 2 were waited for; matrix products, arithmetic and copies ran while one was open for 2% of the time, Pallas kernels for 0%

profile of v16, /device:TPU:1, one launch (start us, length us, event | category | flops | bytes accessed | tf_op | source)
XLA Modules:
  0.0 197.6 jit_solution(16835581885491845294)
XLA Ops:
  7.3 0.7 bitcast_or_fusion
  8.1 1.4 gather_fusion.1
  9.6 0.1 fusion.45
  9.7 0.2 fusion.33
  10.0 0.1 select_reduce_fusion
  10.1 0.6 pad_maximum_fusion.2.x_ref
  10.7 11.5 %shard_map.95 = bf16[32,4224]{1,0:T(8,128)(2,1)} custom-call(bf16[4,4224]{1,0:T(4,128)(2,1)} %pad_maximum_fusion.2.x_ref), custom_call_target="tpu_custom_call" | custom-call | tf_op jit(solution)/shard_map/pallas_call | solution.py:90
  22.3 0.1 reduce_max.19
  22.4 0.9 fusion.3
  23.3 0.8 top_k.17
  24.2 0.1 copy.69
  24.3 0.1 eq.76
  24.4 0.2 fusion.35
  24.6 76.6 %all-gather.2.cloned.1.call-done.x_ref.g_ref = bf16[1024,4224]{1,0:T(8,128)(2,1)} async-done(((bf16[32,4224]{1,0:T(8,128)(2,1)}), bf16[1024,4224]{1,0:T(8,128)(2,1)}) %all-gather.2.cloned.1.call-update) | async-done | bytes 8650768 | tf_op jit(solution)/shard_map/all_gather | solution.py:242
  101.2 1.1 fusion.4
  102.3 0.1 ne.69
  102.4 0.1 copy.70
  102.6 0.8 top_k.24
  103.4 0.1 copy.71
  103.5 0.1 reshape.398
  103.6 0.1 reshape.397
  103.7 0.7 copy.73.rows_ref
  104.5 1.0 gather_fusion
  105.5 13.5 %shard_map.96 = (f32[1024,1]{1,0:T(8,128)}, f32[128,384]{1,0:T(8,128)}, f32[128,384]{1,0:T(8,128)}, f32[128,384]{1,0:T(8,128)}) custom-call(s32[128,1]{1,0:T(8,128)} %copy.73.rows_ref, bf16[1024,4224]{1,0:T(8,128)(2,1)} %all-gather.2.cloned.1.call-done.x_ref.g_ref, bf16[1024,4224]{1,0:T(8,128)(2,1)} %all-gather.2.cloned.1.call-done.x_ref.g_ref, ...), custom_call_target="tpu_custom_call" | custom-call | tf_op jit(solution)/shard_map/pallas_call | solution.py:182
  118.9 1.2 reduce
  120.2 0.1 transpose_reshape_transpose.3
  120.4 0.1 copy.77
  120.6 1.9 fusion.8
  122.6 0.6 fusion
  123.2 0.2 convert_element_type.153
  123.4 0.1 fusion.20
  123.5 1.1 pad_maximum_fusion.x_ref
  124.6 26.3 %shard_map.97 = bf16[32,1,4,2176]{3,2,1,0:T(4,128)(2,1)} custom-call(bf16[32,1,4,2176]{3,2,1,0:T(4,128)(2,1)} %pad_maximum_fusion.x_ref), custom_call_target="tpu_custom_call" | custom-call | tf_op jit(solution)/shard_map/pallas_call | solution.py:74
  150.9 1.0 convert_add_fusion
  152.0 0.1 reshape.429
  152.2 0.2 convolution_convert_fusion
  152.5 0.7 pad_maximum_fusion.1.x_ref
  153.2 7.6 %shard_map.98 = bf16[8,4,2176]{2,1,0:T(4,128)(2,1)} custom-call(bf16[8,4,2176]{2,1,0:T(4,128)(2,1)} %pad_maximum_fusion.1.x_ref), custom_call_target="tpu_custom_call" | custom-call | tf_op jit(solution)/shard_map/pallas_call | solution.py:74
  160.8 0.9 add_bitcast_fusion
  161.7 0.1 copy.80
  161.8 0.2 reduce_sum.58
  162.1 0.2 multiply_reduce_fusion
  162.3 0.8 broadcast_in_dim.53
  163.1 10.0 %all-to-all-start = ((bf16[256,4,128]{2,1,0:T(4,128)(2,1)}), bf16[256,4,128]{2,1,0:T(4,128)(2,1)S(1)}, u32[]{:S(2)}, u32[]{:S(2)}) async-start(bf16[256,4,128]{2,1,0:T(4,128)(2,1)} %broadcast_in_dim.53), calls=%async_computation | async-start | bytes 524288 | tf_op jit(solution)/shard_map/all_to_all | solution.py:287
  173.2 1.0 convert_reduce_fusion
  174.2 0.9 fusion.1
  175.0 13.9 %all-to-all-done = bf16[256,4,128]{2,1,0:T(4,128)(2,1)S(1)} async-done(((bf16[256,4,128]{2,1,0:T(4,128)(2,1)}), bf16[256,4,128]{2,1,0:T(4,128)(2,1)S(1)}, u32[]{:S(2)}, u32[]{:S(2)}) %all-to-all-start) | async-done | bytes 262176 | tf_op jit(solution)/shard_map/all_to_all | solution.py:287
  188.9 1.9 fusion.6
  (48 shorter events, 1.1 us)
Async XLA Ops:
  7.2 167.0 %copy-start = (bf16[2048,128]{1,0:T(8,128)(2,1)S(1)}, bf16[2048,128]{1,0:T(8,128)(2,1)}, u32[]{:S(2)}) copy-start(bf16[2048,128]{1,0:T(8,128)(2,1)} %param.12) | copy-start | bytes 1572868
  7.2 2.4 %copy-start.6 = (s32[4,8]{1,0:T(4,128)S(1)}, s32[4,8]{1,0:T(4,128)}, u32[]{:S(2)}) copy-start(s32[4,8]{1,0:T(4,128)} %param.11) | copy-start | bytes 388
  7.2 15.1 %copy-start.1 = (f32[4,128]{1,0:T(4,128)S(1)}, f32[4,128]{1,0:T(4,128)}, u32[]{:S(2)}) copy-start(f32[4,128]{1,0:T(4,128)} %param.10) | copy-start | bytes 6148
  7.2 2.9 %copy-start.7 = (bf16[4,2048]{1,0:T(4,128)(2,1)S(1)}, bf16[4,2048]{1,0:T(4,128)(2,1)}, u32[]{:S(2)}) copy-start(bf16[4,2048]{1,0:T(4,128)(2,1)} %param.9) | copy-start | bytes 49156
  7.2 2.9 %copy-start.8 = (bf16[4,2048]{1,0:T(4,128)(2,1)S(1)}, bf16[4,2048]{1,0:T(4,128)(2,1)}, u32[]{:S(2)}) copy-start(bf16[4,2048]{1,0:T(4,128)(2,1)} %param.8) | copy-start | bytes 49156
  7.2 94.0 %all-gather.2.cloned.1.call-start = ((), (), s32[]{:S(2)}) async-start(), calls=%async_computation.1 | async-start | bytes 8921088 | tf_op jit(solution)/shard_map/all_gather | solution.py:242
  105.4 15.1 %copy-start.2 = (bf16[1,2048,384]{2,1,0:T(8,128)(2,1)S(1)}, bf16[1,2048,384]{2,1,0:T(8,128)(2,1)}, u32[]{:S(2)}) copy-start(bf16[1,2048,384]{2,1,0:T(8,128)(2,1)} %param.13) | copy-start | bytes 4718596
  120.6 2.0 copy-start.3
  120.6 2.0 copy-start.4
  120.6 2.0 copy-start.5
  150.9 1.1 slice-start
  163.1 25.7 %all-to-all-start = ((bf16[256,4,128]{2,1,0:T(4,128)(2,1)}), bf16[256,4,128]{2,1,0:T(4,128)(2,1)S(1)}, u32[]{:S(2)}, u32[]{:S(2)}) async-start(bf16[256,4,128]{2,1,0:T(4,128)(2,1)} %broadcast_in_dim.53), calls=%async_computation | async-start | bytes 524288 | tf_op jit(solution)/shard_map/all_to_all | solution.py:287
Sparse Core Ops, SparseCore 0:
  22.4 78.8 all-gather.1

commit v17 on v16

--- a/solution.py
+++ b/solution.py
@@ -108,11 +108,11 @@
 
 
 def combine_table(logits, chosen, expert_count):
-    picked = jnp.take_along_axis(logits, chosen, axis=1)
+    expert_ids = jnp.arange(expert_count, dtype=jnp.int32)
+    matched = chosen[:, :, None] == expert_ids[None, None, :]
+    picked = jnp.sum(jnp.where(matched, logits[:, None, :], 0.0), axis=2)
     weights = softmax_rows(picked)
-    expert_ids = jnp.arange(expert_count, dtype=jnp.int32)
-    matched = (chosen[:, :, None] == expert_ids[None, None, :]).astype(jnp.float32)
-    return jnp.sum(weights[:, :, None] * matched, axis=1).astype(jnp.bfloat16)
+    return jnp.sum(weights[:, :, None] * matched.astype(jnp.float32), axis=1).astype(jnp.bfloat16)
 
 
 CAP = 4

time: 198 us -> 198 us (level)
  other arithmetic: 10.6 us -> 13.5 us
  transfers between devices with their start and end apart: 2 -> 2, of which waited for: 2 -> 2; matrix products, arithmetic and copies ran while one was open for 2% -> 3% of each run, Pallas kernels for 0% -> 0%
where the time goes in v17:
time: 198 us; the launch traced here: 197 us
  waiting for transfers between devices  89.1 us (45%)
  Pallas kernels  58.9 us (30%)
  between operations  14.4 us (7%)
  other arithmetic  13.5 us (7%)
  starting transfers between devices  10.1 us (5%)
  matrix products  7.44 us (4%)
  local copies, waits for them, and re-layouts  4.19 us (2%)
    all_gather x1, waiting for transfers between devices, on_device(): gathered = lax.all_gather(near, 'exp', axis=0, tiled=True)  75.2 us
    pallas_call x2, Pallas kernels, exchange(): pl.pallas_call(functools.partial(exchange_kernel, axis, n), out_shape=jax...  33.9 us
    all_to_all x1, waiting for transfers between devices, on_device(): lax.all_to_all(jnp.broadcast_to(logit_grad[None], (devices,) + logit_grad...  13.9 us
    pallas_call x1, Pallas kernels, dense_unit(): pl.pallas_call(dense_kernel, grid=(tokens_n // tile,), out_shape=[jax.Sha...  13.5 us
    pallas_call x1, Pallas kernels, hid_gather(): pl.pallas_call(functools.partial(hid_gather_kernel, n), out_shape=jax.Sha...  11.5 us
    all_to_all x1, starting transfers between devices, on_device(): lax.all_to_all(jnp.broadcast_to(logit_grad[None], (devices,) + logit_grad...  10 us
  transfers between devices with their start and end apart: 2, of which 2 were waited for; matrix products, arithmetic and copies ran while one was open for 3% of the time, Pallas kernels for 0%

profile of v17, /device:TPU:1, one launch (start us, length us, event | category | flops | bytes accessed | tf_op | source)
XLA Modules:
  0.0 197.5 jit_solution(15839737629604997731)
XLA Ops:
  7.2 0.9 select_reduce_fusion.1
  8.1 0.1 reduce_max.18
  8.2 0.2 fusion.33
  8.5 0.8 select_reduce_fusion
  9.3 1.4 pad_maximum_fusion.2.x_ref
  10.6 11.5 %shard_map.95 = bf16[32,4224]{1,0:T(8,128)(2,1)} custom-call(bf16[4,4224]{1,0:T(4,128)(2,1)} %pad_maximum_fusion.2.x_ref), custom_call_target="tpu_custom_call" | custom-call | tf_op jit(solution)/shard_map/pallas_call | solution.py:90
  22.2 0.8 reduce_max.19
  23.0 0.9 fusion.3
  23.9 0.8 top_k.17
  24.7 0.1 copy.69
  24.8 0.1 eq.76
  25.0 0.9 fusion.35
  25.9 75.2 %all-gather.2.cloned.1.call-done.x_ref.g_ref = bf16[1024,4224]{1,0:T(8,128)(2,1)} async-done(((bf16[32,4224]{1,0:T(8,128)(2,1)}), bf16[1024,4224]{1,0:T(8,128)(2,1)}) %all-gather.2.cloned.1.call-update) | async-done | bytes 8650768 | tf_op jit(solution)/shard_map/all_gather | solution.py:242
  101.1 1.1 fusion.4
  102.2 0.1 ne.69
  102.3 0.1 copy.70
  102.5 0.8 top_k.24
  103.3 0.1 copy.71
  103.4 0.1 reshape.404
  103.5 0.1 reshape.403
  103.6 0.7 copy.73.rows_ref
  104.4 1.0 gather_fusion
  105.4 13.5 %shard_map.96 = (f32[1024,1]{1,0:T(8,128)}, f32[128,384]{1,0:T(8,128)}, f32[128,384]{1,0:T(8,128)}, f32[128,384]{1,0:T(8,128)}) custom-call(s32[128,1]{1,0:T(8,128)} %copy.73.rows_ref, bf16[1024,4224]{1,0:T(8,128)(2,1)} %all-gather.2.cloned.1.call-done.x_ref.g_ref, bf16[1024,4224]{1,0:T(8,128)(2,1)} %all-gather.2.cloned.1.call-done.x_ref.g_ref, ...), custom_call_target="tpu_custom_call" | custom-call | tf_op jit(solution)/shard_map/pallas_call | solution.py:182
  118.8 1.2 reduce
  120.1 0.1 transpose_reshape_transpose.3
  120.3 0.1 copy.77
  120.5 1.9 fusion.8
  122.4 0.6 fusion
  123.1 0.2 convert_element_type.153
  123.3 0.1 fusion.20
  123.4 1.1 pad_maximum_fusion.x_ref
  124.5 26.3 %shard_map.97 = bf16[32,1,4,2176]{3,2,1,0:T(4,128)(2,1)} custom-call(bf16[32,1,4,2176]{3,2,1,0:T(4,128)(2,1)} %pad_maximum_fusion.x_ref), custom_call_target="tpu_custom_call" | custom-call | tf_op jit(solution)/shard_map/pallas_call | solution.py:74
  150.8 1.0 convert_add_fusion
  151.9 0.1 reshape.424
  152.1 0.2 convolution_convert_fusion
  152.3 0.1 fusion.28
  152.4 0.7 pad_maximum_fusion.1.x_ref
  153.1 7.6 %shard_map.98 = bf16[8,4,2176]{2,1,0:T(4,128)(2,1)} custom-call(bf16[8,4,2176]{2,1,0:T(4,128)(2,1)} %pad_maximum_fusion.1.x_ref), custom_call_target="tpu_custom_call" | custom-call | tf_op jit(solution)/shard_map/pallas_call | solution.py:74
  160.7 0.9 add_bitcast_fusion
  161.6 0.1 copy.80
  161.7 0.2 reduce_sum.68
  162.0 0.2 multiply_reduce_fusion
  162.2 0.8 broadcast_in_dim.63
  163.0 10.0 %all-to-all-start = ((bf16[256,4,128]{2,1,0:T(4,128)(2,1)}), bf16[256,4,128]{2,1,0:T(4,128)(2,1)S(1)}, u32[]{:S(2)}, u32[]{:S(2)}) async-start(bf16[256,4,128]{2,1,0:T(4,128)(2,1)} %broadcast_in_dim.63), calls=%async_computation | async-start | bytes 524288 | tf_op jit(solution)/shard_map/all_to_all | solution.py:287
  173.1 1.0 convert_reduce_fusion
  174.0 0.9 fusion.1
  174.9 13.9 %all-to-all-done = bf16[256,4,128]{2,1,0:T(4,128)(2,1)S(1)} async-done(((bf16[256,4,128]{2,1,0:T(4,128)(2,1)}), bf16[256,4,128]{2,1,0:T(4,128)(2,1)S(1)}, u32[]{:S(2)}, u32[]{:S(2)}) %all-to-all-start) | async-done | bytes 262176 | tf_op jit(solution)/shard_map/all_to_all | solution.py:287
  188.8 1.9 fusion.6
  (39 shorter events, 0.8 us)
Async XLA Ops:
  7.2 166.9 %copy-start = (bf16[2048,128]{1,0:T(8,128)(2,1)S(1)}, bf16[2048,128]{1,0:T(8,128)(2,1)}, u32[]{:S(2)}) copy-start(bf16[2048,128]{1,0:T(8,128)(2,1)} %param.12) | copy-start | bytes 1572868
  7.2 93.9 %all-gather.2.cloned.1.call-start = ((), (), s32[]{:S(2)}) async-start(), calls=%async_computation.1 | async-start | bytes 8921088 | tf_op jit(solution)/shard_map/all_gather | solution.py:242
  105.4 15.1 %copy-start.1 = (bf16[1,2048,384]{2,1,0:T(8,128)(2,1)S(1)}, bf16[1,2048,384]{2,1,0:T(8,128)(2,1)}, u32[]{:S(2)}) copy-start(bf16[1,2048,384]{2,1,0:T(8,128)(2,1)} %param.13) | copy-start | bytes 4718596
  120.5 1.9 copy-start.2
  120.5 1.9 copy-start.3
  120.5 1.9 copy-start.4
  150.8 1.1 slice-start
  151.8 10.1 %copy-start.5 = (f32[4,128]{1,0:T(4,128)S(1)}, f32[4,128]{1,0:T(4,128)}, u32[]{:S(2)}) copy-start(f32[4,128]{1,0:T(4,128)} %param.10) | copy-start | bytes 6148
  163.0 25.7 %all-to-all-start = ((bf16[256,4,128]{2,1,0:T(4,128)(2,1)}), bf16[256,4,128]{2,1,0:T(4,128)(2,1)S(1)}, u32[]{:S(2)}, u32[]{:S(2)}) async-start(bf16[256,4,128]{2,1,0:T(4,128)(2,1)} %broadcast_in_dim.63), calls=%async_computation | async-start | bytes 524288 | tf_op jit(solution)/shard_map/all_to_all | solution.py:287
Sparse Core Ops, SparseCore 0:
  22.3 78.8 all-gather.1

commit v18 on v17

--- a/solution.py
+++ b/solution.py
@@ -156,7 +156,7 @@
         g_ref[...], wd_ref[...], (((1,), (1,)), ((), ())), preferred_element_type=jnp.float32
     )
     sig_gate = 1.0 / (1.0 + jnp.exp(-gate_pre))
-    score_ref[...] = jnp.sum(gate_pre * sig_gate * up_pre * back_grad, axis=1, keepdims=True)
+    score_ref[...] = jnp.sum((gate_pre * sig_gate * up_pre * back_grad).T, axis=0, keepdims=True)
     tile = x.shape[0]
     place = step * tile + lax.broadcasted_iota(jnp.int32, (1, tile), 1)
     choice = (rows_ref[...] == place).astype(jnp.bfloat16)
@@ -183,7 +183,7 @@
         dense_kernel,
         grid=(tokens_n // tile,),
         out_shape=[
-            jax.ShapeDtypeStruct((tokens_n, 1), f32),
+            jax.ShapeDtypeStruct((1, tokens_n), f32),
             jax.ShapeDtypeStruct((slots, hidden), f32),
             jax.ShapeDtypeStruct((slots, hidden), f32),
             jax.ShapeDtypeStruct((slots, hidden), f32),
@@ -197,7 +197,7 @@
             pl.BlockSpec((hidden, width), fixed),
         ],
         out_specs=[
-            pl.BlockSpec((tile, 1), tiles),
+            pl.BlockSpec((1, tile), lambda i: (0, i)),
             pl.BlockSpec((slots, hidden), fixed),
             pl.BlockSpec((slots, hidden), fixed),
             pl.BlockSpec((slots, hidden), fixed),
@@ -244,7 +244,7 @@
     column = jnp.dot(combine_all, unit_pick, preferred_element_type=jnp.float32).T
     rows = chosen_rows(column, group_rows)
     dense = [dense_unit(gathered, rows[i], w_gate[i], w_up[i], w_down[i]) for i in range(unit_count)]
-    score_part = jnp.concatenate([d[0] for d in dense], axis=1)
+    score_part = jnp.concatenate([d[0] for d in dense], axis=0).T
     gate_s, up_s, back_s = (jnp.stack([d[j] for d in dense]) for j in (1, 2, 3))
     part = sparse_terms(gate_s, up_s, back_s, rows, column, w_gate, w_up)
     lane = 128

time: 198 us -> 199 us (level)
  no operation moved by 1% of the time
where the time goes in v18:
time: 199 us; the launch traced here: 198 us
  waiting for transfers between devices  89.1 us (45%)
  Pallas kernels  59 us (30%)
  between operations  14.4 us (7%)
  other arithmetic  13.6 us (7%)
  starting transfers between devices  10.1 us (5%)
  matrix products  7.44 us (4%)
  local copies, waits for them, and re-layouts  4.7 us (2%)
    all_gather x1, waiting for transfers between devices, on_device(): gathered = lax.all_gather(near, 'exp', axis=0, tiled=True)  75.2 us
    pallas_call x2, Pallas kernels, exchange(): pl.pallas_call(functools.partial(exchange_kernel, axis, n), out_shape=jax...  33.9 us
    all_to_all x1, waiting for transfers between devices, on_device(): lax.all_to_all(jnp.broadcast_to(logit_grad[None], (devices,) + logit_grad...  13.9 us
    pallas_call x1, Pallas kernels, dense_unit(): pl.pallas_call(dense_kernel, grid=(tokens_n // tile,), out_shape=[jax.Sha...  13.7 us
    pallas_call x1, Pallas kernels, hid_gather(): pl.pallas_call(functools.partial(hid_gather_kernel, n), out_shape=jax.Sha...  11.5 us
    all_to_all x1, starting transfers between devices, on_device(): lax.all_to_all(jnp.broadcast_to(logit_grad[None], (devices,) + logit_grad...  10 us
  transfers between devices with their start and end apart: 2, of which 2 were waited for; matrix products, arithmetic and copies ran while one was open for 3% of the time, Pallas kernels for 0%

profile of v18, /device:TPU:1, one launch (start us, length us, event | category | flops | bytes accessed | tf_op | source)
XLA Modules:
  0.0 198.3 jit_solution(74923678413759224)
XLA Ops:
  7.2 0.9 select_reduce_fusion.1
  8.1 0.1 reduce_max.18
  8.2 0.2 fusion.33
  8.5 0.8 select_reduce_fusion
  9.3 1.4 pad_maximum_fusion.2.x_ref
  10.6 11.5 %shard_map.95 = bf16[32,4224]{1,0:T(8,128)(2,1)} custom-call(bf16[4,4224]{1,0:T(4,128)(2,1)} %pad_maximum_fusion.2.x_ref), custom_call_target="tpu_custom_call" | custom-call | tf_op jit(solution)/shard_map/pallas_call | solution.py:90
  22.2 0.8 reduce_max.19
  23.0 0.9 fusion.3
  23.9 0.8 top_k.17
  24.7 0.1 copy.69
  24.8 0.1 eq.76
  25.0 0.9 fusion.35
  25.9 75.2 %all-gather.2.cloned.1.call-done.x_ref.g_ref = bf16[1024,4224]{1,0:T(8,128)(2,1)} async-done(((bf16[32,4224]{1,0:T(8,128)(2,1)}), bf16[1024,4224]{1,0:T(8,128)(2,1)}) %all-gather.2.cloned.1.call-update) | async-done | bytes 8650768 | tf_op jit(solution)/shard_map/all_gather | solution.py:242
  101.1 1.1 fusion.4
  102.2 0.1 ne.69
  102.3 0.1 copy.70
  102.5 0.8 top_k.24
  103.3 0.1 copy.71
  103.4 0.1 reshape.404
  103.5 0.1 reshape.403
  103.6 0.7 copy.73.rows_ref
  104.4 1.0 gather_fusion
  105.4 13.7 %shard_map.96 = (f32[1,1024]{1,0:T(1,128)}, f32[128,384]{1,0:T(8,128)}, f32[128,384]{1,0:T(8,128)}, f32[128,384]{1,0:T(8,128)}) custom-call(s32[128,1]{1,0:T(8,128)} %copy.73.rows_ref, bf16[1024,4224]{1,0:T(8,128)(2,1)} %all-gather.2.cloned.1.call-done.x_ref.g_ref, bf16[1024,4224]{1,0:T(8,128)(2,1)} %all-gather.2.cloned.1.call-done.x_ref.g_ref, ...), custom_call_target="tpu_custom_call" | custom-call | tf_op jit(solution)/shard_map/pallas_call | solution.py:182
  119.0 0.5 broadcast.299
  119.5 1.3 reduce.3
  120.9 0.1 transpose_reshape.4
  121.1 0.1 copy.77
  121.3 1.9 fusion.8
  123.2 0.6 fusion
  123.9 0.2 convert_element_type.153
  124.1 0.1 fusion.20
  124.2 1.1 pad_maximum_fusion.x_ref
  125.3 26.3 %shard_map.97 = bf16[32,1,4,2176]{3,2,1,0:T(4,128)(2,1)} custom-call(bf16[32,1,4,2176]{3,2,1,0:T(4,128)(2,1)} %pad_maximum_fusion.x_ref), custom_call_target="tpu_custom_call" | custom-call | tf_op jit(solution)/shard_map/pallas_call | solution.py:74
  151.6 1.0 convert_add_fusion
  152.8 0.1 reshape.424
  152.9 0.2 convolution_convert_fusion
  153.2 0.7 pad_maximum_fusion.1.x_ref
  153.9 7.6 %shard_map.98 = bf16[8,4,2176]{2,1,0:T(4,128)(2,1)} custom-call(bf16[8,4,2176]{2,1,0:T(4,128)(2,1)} %pad_maximum_fusion.1.x_ref), custom_call_target="tpu_custom_call" | custom-call | tf_op jit(solution)/shard_map/pallas_call | solution.py:74
  161.5 0.9 add_bitcast_fusion
  162.4 0.1 copy.80
  162.5 0.2 reduce_sum.68
  162.8 0.2 multiply_reduce_fusion
  163.0 0.8 broadcast_in_dim.63
  163.8 10.0 %all-to-all-start = ((bf16[256,4,128]{2,1,0:T(4,128)(2,1)}), bf16[256,4,128]{2,1,0:T(4,128)(2,1)S(1)}, u32[]{:S(2)}, u32[]{:S(2)}) async-start(bf16[256,4,128]{2,1,0:T(4,128)(2,1)} %broadcast_in_dim.63), calls=%async_computation | async-start | bytes 524288 | tf_op jit(solution)/shard_map/all_to_all | solution.py:287
  173.9 1.0 convert_reduce_fusion
  174.9 0.9 fusion.1
  175.7 13.9 %all-to-all-done = bf16[256,4,128]{2,1,0:T(4,128)(2,1)S(1)} async-done(((bf16[256,4,128]{2,1,0:T(4,128)(2,1)}), bf16[256,4,128]{2,1,0:T(4,128)(2,1)S(1)}, u32[]{:S(2)}, u32[]{:S(2)}) %all-to-all-start) | async-done | bytes 262176 | tf_op jit(solution)/shard_map/all_to_all | solution.py:287
  189.6 1.9 fusion.6
  (40 shorter events, 0.9 us)
Async XLA Ops:
  7.2 167.7 %copy-start = (bf16[2048,128]{1,0:T(8,128)(2,1)S(1)}, bf16[2048,128]{1,0:T(8,128)(2,1)}, u32[]{:S(2)}) copy-start(bf16[2048,128]{1,0:T(8,128)(2,1)} %param.12) | copy-start | bytes 1572868
  7.2 93.9 %all-gather.2.cloned.1.call-start = ((), (), s32[]{:S(2)}) async-start(), calls=%async_computation.1 | async-start | bytes 8921088 | tf_op jit(solution)/shard_map/all_gather | solution.py:242
  105.4 15.9 %copy-start.1 = (bf16[1,2048,384]{2,1,0:T(8,128)(2,1)S(1)}, bf16[1,2048,384]{2,1,0:T(8,128)(2,1)}, u32[]{:S(2)}) copy-start(bf16[1,2048,384]{2,1,0:T(8,128)(2,1)} %param.13) | copy-start | bytes 4718596
  121.3 1.9 copy-start.2
  121.3 1.9 copy-start.3
  121.3 1.9 copy-start.4
  151.6 1.1 slice-start
  152.6 10.1 %copy-start.5 = (f32[4,128]{1,0:T(4,128)S(1)}, f32[4,128]{1,0:T(4,128)}, u32[]{:S(2)}) copy-start(f32[4,128]{1,0:T(4,128)} %param.10) | copy-start | bytes 6148
  163.8 25.7 %all-to-all-start = ((bf16[256,4,128]{2,1,0:T(4,128)(2,1)}), bf16[256,4,128]{2,1,0:T(4,128)(2,1)S(1)}, u32[]{:S(2)}, u32[]{:S(2)}) async-start(bf16[256,4,128]{2,1,0:T(4,128)(2,1)} %broadcast_in_dim.63), calls=%async_computation | async-start | bytes 524288 | tf_op jit(solution)/shard_map/all_to_all | solution.py:287
Sparse Core Ops, SparseCore 0:
  22.3 78.8 all-gather.1

commit v19 on v17

--- a/solution.py
+++ b/solution.py
@@ -167,9 +167,11 @@
         up_ref[...] = jnp.zeros_like(up_ref)
         back_ref[...] = jnp.zeros_like(back_ref)
 
-    gate_ref[...] += pick_rows(choice, gate_pre)
-    up_ref[...] += pick_rows(choice, up_pre)
-    back_ref[...] += pick_rows(choice, back_grad)
+    hidden = gate_pre.shape[1]
+    picked = pick_rows(choice, jnp.concatenate([gate_pre, up_pre, back_grad], axis=1))
+    gate_ref[...] += picked[:, :hidden]
+    up_ref[...] += picked[:, hidden : 2 * hidden]
+    back_ref[...] += picked[:, 2 * hidden :]
 
 
 def dense_unit(gathered, rows, gate_w, up_w, down_w, tile=256):

time: 198 us -> 198 us (level)
  no operation moved by 1% of the time
where the time goes in v19:
time: 198 us
  waiting for transfers between devices  89.1 us (45%)
  Pallas kernels  59.1 us (30%)
  between operations  14.4 us (7%)
  other arithmetic  13.5 us (7%)
  starting transfers between devices  10.1 us (5%)
  matrix products  7.44 us (4%)
  local copies, waits for them, and re-layouts  4.19 us (2%)
    all_gather x1, waiting for transfers between devices, on_device(): gathered = lax.all_gather(near, 'exp', axis=0, tiled=True)  75.2 us
    pallas_call x2, Pallas kernels, exchange(): pl.pallas_call(functools.partial(exchange_kernel, axis, n), out_shape=jax...  33.9 us
    all_to_all x1, waiting for transfers between devices, on_device(): lax.all_to_all(jnp.broadcast_to(logit_grad[None], (devices,) + logit_grad...  13.9 us
    pallas_call x1, Pallas kernels, dense_unit(): pl.pallas_call(dense_kernel, grid=(tokens_n // tile,), out_shape=[jax.Sha...  13.7 us
    pallas_call x1, Pallas kernels, hid_gather(): pl.pallas_call(functools.partial(hid_gather_kernel, n), out_shape=jax.Sha...  11.5 us
    all_to_all x1, starting transfers between devices, on_device(): lax.all_to_all(jnp.broadcast_to(logit_grad[None], (devices,) + logit_grad...  10 us
  transfers between devices with their start and end apart: 2, of which 2 were waited for; matrix products, arithmetic and copies ran while one was open for 3% of the time, Pallas kernels for 0%

profile of v19, /device:TPU:1, one launch (start us, length us, event | category | flops | bytes accessed | tf_op | source)
XLA Modules:
  0.0 197.8 jit_solution(7013629803560654541)
XLA Ops:
  7.2 0.9 select_reduce_fusion.1
  8.1 0.1 reduce_max.18
  8.2 0.2 fusion.33
  8.5 0.8 select_reduce_fusion
  9.3 1.4 pad_maximum_fusion.2.x_ref
  10.6 11.5 %shard_map.95 = bf16[32,4224]{1,0:T(8,128)(2,1)} custom-call(bf16[4,4224]{1,0:T(4,128)(2,1)} %pad_maximum_fusion.2.x_ref), custom_call_target="tpu_custom_call" | custom-call | tf_op jit(solution)/shard_map/pallas_call | solution.py:90
  22.2 0.8 reduce_max.19
  23.0 0.9 fusion.3
  23.9 0.8 top_k.17
  24.7 0.1 copy.69
  24.8 0.1 eq.76
  25.0 0.9 fusion.35
  25.9 75.2 %all-gather.2.cloned.1.call-done.x_ref.g_ref = bf16[1024,4224]{1,0:T(8,128)(2,1)} async-done(((bf16[32,4224]{1,0:T(8,128)(2,1)}), bf16[1024,4224]{1,0:T(8,128)(2,1)}) %all-gather.2.cloned.1.call-update) | async-done | bytes 8650768 | tf_op jit(solution)/shard_map/all_gather | solution.py:244
  101.1 1.1 fusion.4
  102.2 0.1 ne.69
  102.3 0.1 copy.70
  102.5 0.8 top_k.24
  103.3 0.1 copy.71
  103.4 0.1 reshape.404
  103.5 0.1 reshape.403
  103.6 0.7 copy.73.rows_ref
  104.4 1.0 gather_fusion
  105.4 13.7 %shard_map.96 = (f32[1024,1]{1,0:T(8,128)}, f32[128,384]{1,0:T(8,128)}, f32[128,384]{1,0:T(8,128)}, f32[128,384]{1,0:T(8,128)}) custom-call(s32[128,1]{1,0:T(8,128)} %copy.73.rows_ref, bf16[1024,4224]{1,0:T(8,128)(2,1)} %all-gather.2.cloned.1.call-done.x_ref.g_ref, bf16[1024,4224]{1,0:T(8,128)(2,1)} %all-gather.2.cloned.1.call-done.x_ref.g_ref, ...), custom_call_target="tpu_custom_call" | custom-call | tf_op jit(solution)/shard_map/pallas_call | solution.py:184
  119.1 1.2 reduce
  120.4 0.1 transpose_reshape_transpose.3
  120.6 0.1 copy.77
  120.8 1.9 fusion.8
  122.7 0.6 fusion
  123.3 0.2 convert_element_type.153
  123.5 0.1 fusion.20
  123.7 1.1 pad_maximum_fusion.x_ref
  124.8 26.3 %shard_map.97 = bf16[32,1,4,2176]{3,2,1,0:T(4,128)(2,1)} custom-call(bf16[32,1,4,2176]{3,2,1,0:T(4,128)(2,1)} %pad_maximum_fusion.x_ref), custom_call_target="tpu_custom_call" | custom-call | tf_op jit(solution)/shard_map/pallas_call | solution.py:74
  151.1 1.0 convert_add_fusion
  152.2 0.1 reshape.424
  152.3 0.2 convolution_convert_fusion
  152.5 0.1 fusion.28
  152.6 0.7 pad_maximum_fusion.1.x_ref
  153.3 7.6 %shard_map.98 = bf16[8,4,2176]{2,1,0:T(4,128)(2,1)} custom-call(bf16[8,4,2176]{2,1,0:T(4,128)(2,1)} %pad_maximum_fusion.1.x_ref), custom_call_target="tpu_custom_call" | custom-call | tf_op jit(solution)/shard_map/pallas_call | solution.py:74
  160.9 0.9 add_bitcast_fusion
  161.8 0.1 copy.80
  162.0 0.2 reduce_sum.68
  162.2 0.2 multiply_reduce_fusion
  162.5 0.8 broadcast_in_dim.63
  163.3 10.0 %all-to-all-start = ((bf16[256,4,128]{2,1,0:T(4,128)(2,1)}), bf16[256,4,128]{2,1,0:T(4,128)(2,1)S(1)}, u32[]{:S(2)}, u32[]{:S(2)}) async-start(bf16[256,4,128]{2,1,0:T(4,128)(2,1)} %broadcast_in_dim.63), calls=%async_computation | async-start | bytes 524288 | tf_op jit(solution)/shard_map/all_to_all | solution.py:289
  173.3 1.0 convert_reduce_fusion
  174.3 0.9 fusion.1
  175.2 13.9 %all-to-all-done = bf16[256,4,128]{2,1,0:T(4,128)(2,1)S(1)} async-done(((bf16[256,4,128]{2,1,0:T(4,128)(2,1)}), bf16[256,4,128]{2,1,0:T(4,128)(2,1)S(1)}, u32[]{:S(2)}, u32[]{:S(2)}) %all-to-all-start) | async-done | bytes 262176 | tf_op jit(solution)/shard_map/all_to_all | solution.py:289
  189.0 1.9 fusion.6
  (39 shorter events, 0.8 us)
Async XLA Ops:
  7.2 167.1 %copy-start = (bf16[2048,128]{1,0:T(8,128)(2,1)S(1)}, bf16[2048,128]{1,0:T(8,128)(2,1)}, u32[]{:S(2)}) copy-start(bf16[2048,128]{1,0:T(8,128)(2,1)} %param.12) | copy-start | bytes 1572868
  7.2 93.9 %all-gather.2.cloned.1.call-start = ((), (), s32[]{:S(2)}) async-start(), calls=%async_computation.1 | async-start | bytes 8921088 | tf_op jit(solution)/shard_map/all_gather | solution.py:244
  105.4 15.4 %copy-start.1 = (bf16[1,2048,384]{2,1,0:T(8,128)(2,1)S(1)}, bf16[1,2048,384]{2,1,0:T(8,128)(2,1)}, u32[]{:S(2)}) copy-start(bf16[1,2048,384]{2,1,0:T(8,128)(2,1)} %param.13) | copy-start | bytes 4718596
  120.7 1.9 copy-start.2
  120.8 1.9 copy-start.3
  120.8 1.9 copy-start.4
  151.1 1.1 slice-start
  152.1 10.1 %copy-start.5 = (f32[4,128]{1,0:T(4,128)S(1)}, f32[4,128]{1,0:T(4,128)}, u32[]{:S(2)}) copy-start(f32[4,128]{1,0:T(4,128)} %param.10) | copy-start | bytes 6148
  163.3 25.7 %all-to-all-start = ((bf16[256,4,128]{2,1,0:T(4,128)(2,1)}), bf16[256,4,128]{2,1,0:T(4,128)(2,1)S(1)}, u32[]{:S(2)}, u32[]{:S(2)}) async-start(bf16[256,4,128]{2,1,0:T(4,128)(2,1)} %broadcast_in_dim.63), calls=%async_computation | async-start | bytes 524288 | tf_op jit(solution)/shard_map/all_to_all | solution.py:289
Sparse Core Ops, SparseCore 0:
  22.3 78.8 all-gather.1
